TPU v7x, 512 devices: a whole 4x8x8 slice. The times are simulated.
512 devices in a mesh: hi: 16 (over z, y_hi), lo: 32 (over x, y_lo, core).
Axes of the slice: x: 4, y: 8 (y_hi: 2, y_lo: 4; y = y_hi * 4 + y_lo), z: 8, core: 2. Of those that a mesh axis runs over, the one named last changes fastest.
Arguments:
- amplitudes: float32 [16, 32, 32, 128, 128], P('hi', 'lo'), may hold values from -6 to 6
- gates: float32 [3, 128, 128], replicated, may hold values from -0.5 to 0.5
- angles: float32 [2], replicated, may hold values from -3.140625 to 3.140625
- cz_pairs: int32 [24, 2], replicated, may hold values from 0 to 18, as said below
Outputs:
- rotated: float32 [16, 32, 32, 128, 128], P('hi', 'lo')
Inputs may be any that keep to these rules, and one draw needn't show every extreme that they name: `cz_pairs`: the two qubits of a row differ.
All inputs are finite; a program needn't handle non-finite values.
Results may differ from a plain program's by a relative error of at most 0.00007.
Values sent between devices are 32-bit elements; how exact they have to be, the bound alone decides.
No kernel may reach another device: no remote copies, remote signals or barrier semaphores. Data moves between devices by JAX's collectives and lax.ppermute only.
A program may use at most 64 MiB of HBM per device.

v0:
```python
import jax
import jax.numpy as jnp
from jax import lax
from jax.sharding import PartitionSpec as P

QG = 7
QM = 5


def partner_2(value, axis, apart):
    return lax.ppermute(value, axis, [(i, i ^ 1 << apart) for i in range(lax.axis_size(axis))])


def group_bits(qubit_index, offset, bit_count):
    inside = ((qubit_index >= offset) & (qubit_index < offset + bit_count)).astype(jnp.int32)
    shifted = jnp.clip(qubit_index - offset, 0, bit_count - 1)
    positions = jnp.arange(2**bit_count, dtype=jnp.int32)
    return (positions[None, :] >> shifted[:, None] & 1) * inside[:, None]


def parity_sign(values):
    return 1.0 - 2.0 * (values % 2).astype(jnp.float32)


def cross_table(left_a, right_b, left_b, right_a):
    return jnp.einsum("pi,pj->ij", left_a, right_b) + jnp.einsum("pi,pj->ij", left_b, right_a)


def cz_sign(cz_pairs):
    first_qubit = cz_pairs[:, 0]
    second_qubit = cz_pairs[:, 1]
    upper_a = group_bits(first_qubit, 2 * QG, QM)
    middle_a = group_bits(first_qubit, QG, QG)
    lowest_a = group_bits(first_qubit, 0, QG)
    upper_b = group_bits(second_qubit, 2 * QG, QM)
    middle_b = group_bits(second_qubit, QG, QG)
    lowest_b = group_bits(second_qubit, 0, QG)
    sign_um = parity_sign(cross_table(upper_a, middle_b, upper_b, middle_a))
    sign_ul = parity_sign(cross_table(upper_a, lowest_b, upper_b, lowest_a))
    sign_ml = parity_sign(cross_table(middle_a, lowest_b, middle_b, lowest_a))
    diag_u = parity_sign(jnp.sum(upper_a * upper_b, 0))
    diag_m = parity_sign(jnp.sum(middle_a * middle_b, 0))
    diag_l = parity_sign(jnp.sum(lowest_a * lowest_b, 0))
    left_table = sign_um * diag_u[:, None]
    right_table = sign_ml * diag_m[:, None] * diag_l[None, :]
    return left_table[:, :, None] * sign_ul[:, None, :] * right_table[None]


def first_gate(vector, matrix):
    return jnp.einsum("mjc,kc->mjk", vector, matrix, precision=lax.Precision.HIGHEST)


def per_device(amplitudes, gates, angles, cz_pairs):
    mid_size = amplitudes.shape[2]
    gate_size = amplitudes.shape[4]
    hi_count = lax.axis_size("hi")
    lo_count = lax.axis_size("lo")
    lo_bit = lo_count.bit_length() - 2
    lo_upper = (lax.axis_index("lo") >> lo_bit & 1).astype(jnp.float32)
    cosine_lo = jnp.cos(angles[0] * 0.5)
    factor_lo = (2.0 * lo_upper - 1.0) * jnp.sin(angles[0] * 0.5)
    vector = amplitudes[0, 0] * cz_sign(cz_pairs)
    vector = first_gate(vector, gates[0])
    partner = partner_2(vector, "lo", lo_bit)
    vector = cosine_lo * vector + factor_lo * partner
    vector = jnp.einsum("jc,mck->mjk", gates[1], vector, precision=lax.Precision.HIGHEST)
    hi_upper = (lax.axis_index("hi") & 1).astype(jnp.float32)
    partner = partner_2(vector, "hi", 0)
    vector = (
        jnp.cos(angles[1] * 0.5) * vector
        + (2.0 * hi_upper - 1.0) * jnp.sin(angles[1] * 0.5) * partner
    )
    blocks = vector.reshape(hi_count, mid_size // hi_count, gate_size, gate_size)
    vector = lax.all_to_all(blocks, "hi", split_axis=0, concat_axis=0, tiled=True).reshape(
        mid_size, gate_size, gate_size
    )
    flattened = vector.reshape(gate_size, mid_size * gate_size)
    result = jnp.dot(gates[2], flattened, precision=lax.Precision.HIGHEST)
    return result.reshape(1, 1, mid_size, gate_size, gate_size)


def solution(mesh):
    placed = (P("hi", "lo", None, None, None), P(), P(), P())
    return jax.shard_map(
        per_device,
        mesh=mesh,
        in_specs=placed,
        out_specs=P("hi", "lo", None, None, None),
        check_vma=False,
    )
```

profile of v0, /device:TPU:12, one launch (start us, length us, event | category | flops | bytes accessed | tf_op | source)
XLA Modules:
  0.0 249.8 jit_solution(4180023535179009006)
XLA Ops:
  0.0 0.8 fusion.77
  0.8 0.8 clamp_bitcast_fusion.3
  1.5 0.1 multiply_reduce_fusion.2
  1.6 0.3 fusion.39
  1.9 0.3 fusion.40
  2.3 0.4 fusion.38
  2.7 0.1 multiply_reduce_fusion
  2.8 0.3 fusion.37
  3.1 0.3 fusion.33
  3.5 0.5 fusion.22
  3.9 0.0 copy-start.2
  3.9 0.0 copy-start.1
  3.9 3.5 %fusion = f32[32,128,128]{2,1,0:T(8,128)S(1)} fusion(f32[1,1,32,128,128]{4,3,2,1,0:T(8,128)} %param.4, f32[128,128]{1,0:T(8,128)S(1)} %fusion.22, f32[32,128]{1,0:T(8,128)S(1)} %fusion.37, f32[32,128]{1,0:T(8,128)S(1)} %fusion.33, f32[3,128,128]{2,1,0:T(8,128)} %param.5), kind=kOutput, calls=%fused_computation.1 | convolution fusion | flops 806879232 | bytes 4358144 | tf_op jit(solution)/shard_map/mjc,kc->mjk/dot_general | solution.py:50
  7.5 0.0 copy-start
  7.5 2.4 collective-permute-start
  9.9 0.0 copy-done.2
  9.9 0.6 fusion.99
  11.3 47.0 %collective-permute-done = f32[32,128,128]{2,1,0:T(8,128)} collective-permute-done((f32[32,128,128]{2,1,0:T(8,128)S(1)}, f32[32,128,128]{2,1,0:T(8,128)}, u32[]{:S(2)}, u32[]{:S(2)}) %collective-permute-start) | collective-permute-done | bytes 2097184 | tf_op jit(solution)/shard_map/ppermute | solution.py:11
  58.4 0.0 copy-done
  58.4 0.0 copy-done.1
  58.4 5.2 %fusion.9 = f32[32,128,128]{1,2,0:T(8,128)S(1)} fusion(f32[32,128,128]{2,1,0:T(8,128)} %collective-permute-done, f32[32,128,128]{2,1,0:T(8,128)} %copy-done, f32[]{:T(128)S(6)} %mul.288, f32[]{:T(128)} %bitcast.1, f32[3,128,128]{2,1,0:T(8,128)S(1)} %copy-done.1), kind=kOutput, calls=%fused_computation.11 | convolution fusion | flops 806879232 | bytes 6357000 | tf_op jit(solution)/shard_map/jc,mck->mjk/dot_general | solution.py:66
  63.6 6.8 %collective-permute-start.1 = (f32[32,128,128]{1,2,0:T(8,128)S(1)}, f32[32,128,128]{1,2,0:T(8,128)}, u32[]{:S(2)}, u32[]{:S(2)}) collective-permute-start(f32[32,128,128]{1,2,0:T(8,128)S(1)} %fusion.9), channel_id=1, source_target_pairs={{0,32},{32,0},{64,96},{96,64},{128,160},{160,128},{192,224},{224,1... | collective-permute-start | bytes 6291464 | tf_op jit(solution)/shard_map/ppermute | solution.py:11
  71.2 89.7 %collective-permute-done.1 = f32[32,128,128]{1,2,0:T(8,128)} collective-permute-done((f32[32,128,128]{1,2,0:T(8,128)S(1)}, f32[32,128,128]{1,2,0:T(8,128)}, u32[]{:S(2)}, u32[]{:S(2)}) %collective-permute-start.1) | collective-permute-done | bytes 2097184 | tf_op jit(solution)/shard_map/ppermute | solution.py:11
  160.9 3.3 %multiply_add_fusion = f32[32,128,128]{1,2,0:T(8,128)} fusion(f32[32,128,128]{1,2,0:T(8,128)} %collective-permute-done.1, f32[32,128,128]{1,2,0:T(8,128)S(1)} %fusion.9, f32[]{:T(128)S(6)} %mul.293, f32[]{:T(128)} %bitcast), kind=kLoop, calls=%fused_computation.3 | loop fusion | flops 1572864 | bytes 6291464 | tf_op jit(solution)/shard_map/add | solution.py:70
  164.2 1.9 copy.10
  166.1 73.7 %all_to_all.5 = f32[16,2,128,128]{3,2,1,0:T(8,128)} all-to-all(f32[16,2,128,128]{3,2,1,0:T(8,128)S(1)} %copy.10), channel_id=1, replica_groups=mesh['hi'=16,'lo'=32] {'hi'}, dimensions={0} | all-to-all | bytes 4194304 | tf_op jit(solution)/shard_map/all_to_all | solution.py:74
  239.9 1.7 reshape_reshape.3
  241.6 4.8 %convolution_bitcast_fusion = f32[128,4096]{0,1:T(8,128)} fusion(f32[128,4096]{1,0:T(8,128)S(1)} %reshape_reshape.3, f32[3,128,128]{2,1,0:T(8,128)S(1)} %copy-done.1), kind=kOutput, calls=%fused_computation | convolution fusion | flops 805306368 | bytes 4259840 | tf_op jit(solution)/shard_map/dot_general | solution.py:78
  246.4 1.9 copy.11
  248.3 1.5 reshape.73
  (3 shorter events, 0.0 us)
Async XLA Ops:
  3.9 6.0 %copy-start.2 = (f32[2]{0:T(128)S(1)}, f32[2]{0:T(128)}, u32[]{:S(2)}) copy-start(f32[2]{0:T(128)} %param.6) | copy-start | bytes 28
  3.9 54.5 %copy-start.1 = (f32[3,128,128]{2,1,0:T(8,128)S(1)}, f32[3,128,128]{2,1,0:T(8,128)}, u32[]{:S(2)}) copy-start(f32[3,128,128]{2,1,0:T(8,128)} %param.5) | copy-start | bytes 589828
  7.5 50.9 %copy-start = (f32[32,128,128]{2,1,0:T(8,128)}, f32[32,128,128]{2,1,0:T(8,128)S(1)}, u32[]{:S(2)}) copy-start(f32[32,128,128]{2,1,0:T(8,128)S(1)} %fusion) | copy-start | bytes 6291460
  7.5 50.9 %collective-permute-start = (f32[32,128,128]{2,1,0:T(8,128)S(1)}, f32[32,128,128]{2,1,0:T(8,128)}, u32[]{:S(2)}, u32[]{:S(2)}) collective-permute-start(f32[32,128,128]{2,1,0:T(8,128)S(1)} %fusion), channel_id=1, source_target_pairs={{0,16},{1,17},{2,18},{3,19},{4,20},{5,21},{6,22},{7,23},{8,24},{9,... | collective-permute-start | bytes 6291464 | tf_op jit(solution)/shard_map/ppermute | solution.py:11
  63.6 97.3 %collective-permute-start.1 = (f32[32,128,128]{1,2,0:T(8,128)S(1)}, f32[32,128,128]{1,2,0:T(8,128)}, u32[]{:S(2)}, u32[]{:S(2)}) collective-permute-start(f32[32,128,128]{1,2,0:T(8,128)S(1)} %fusion.9), channel_id=1, source_target_pairs={{0,32},{32,0},{64,96},{96,64},{128,160},{160,128},{192,224},{224,1... | collective-permute-start | bytes 6291464 | tf_op jit(solution)/shard_map/ppermute | solution.py:11
where the time goes:
time: 250 us
  waiting for transfers between devices  137 us (55%)
  blocking collectives  73.7 us (29%)
  matrix products  15.6 us (6%)
  starting transfers between devices  9.25 us (4%)
  local copies, waits for them, and re-layouts  7.71 us (3%)
  other arithmetic  5.02 us (2%)
    ppermute x2, waiting for transfers between devices, partner_2(): lax.ppermute(value, axis, [(i, i ^ 1 << apart) for i in range(lax.axis_si...  137 us
    all_to_all x1, blocking collectives, per_device(): lax.all_to_all(blocks, 'hi', split_axis=0, concat_axis=0, tiled=True)  73.7 us
    ppermute x2, starting transfers between devices, partner_2(): lax.ppermute(value, axis, [(i, i ^ 1 << apart) for i in range(lax.axis_si...  9.25 us
    dot_general x1, matrix products, per_device(): jnp.einsum('jc,mck->mjk', gates[1], vector, precision=lax.Precision.HIGHEST)  5.19 us
  transfers between devices with their start and end apart: 2, of which 2 were waited for; matrix products, arithmetic and copies ran while one was open for 0% of the time, Pallas kernels for 0%

commit v1 on v0

v1 whole, which is shorter than its diff:
```python
import jax
import jax.numpy as jnp
from jax import lax
from jax.experimental import pallas as pl
from jax.experimental.pallas import tpu as pltpu
from jax.sharding import PartitionSpec as P

QL = 14
QU = 5
QUBITS = QL + QU
PARTS = 2


def split(value):
    top = value.astype(jnp.bfloat16)
    return top, (value - top.astype(jnp.float32)).astype(jnp.bfloat16)


def fold_parity(bits):
    for step in (8, 4, 2, 1):
        bits = bits ^ (bits >> step)
    return bits & 1


def mm(left, right):
    return lax.dot_general(left, right, (((1,), (0,)), ((), ())), preferred_element_type=jnp.float32)


def local_kernel(step_t, cz_ref, x_ref, g_ref, *rest):
    outs = rest[:PARTS]
    adj, masks, flips, low_sign, right0, left1 = rest[PARTS:]
    step = pl.program_id(0)

    @pl.when(step == 0)
    def _():
        for q in range(QUBITS):
            adj[q] = 0
        for p in range(cz_ref.shape[0]):
            a = cz_ref[p, 0]
            b = cz_ref[p, 1]
            q = jnp.maximum(a, b)
            adj[q] = adj[q] ^ (1 << jnp.minimum(a, b))
        masks[0] = 0
        flips[0] = 0
        for u in range(QU):
            row = adj[QL + u]
            for m in range(1 << u):
                masks[m + (1 << u)] = masks[m] ^ (row & ((1 << QL) - 1))
                flips[m + (1 << u)] = flips[m] ^ fold_parity((row >> QL) & m)
        row_id = lax.broadcasted_iota(jnp.int32, (128, 128), 0)
        lane_id = lax.broadcasted_iota(jnp.int32, (128, 128), 1)
        index = row_id * 128 + lane_id
        partner = jnp.zeros_like(index)
        for q in range(1, QL):
            partner = partner ^ jnp.where((index >> q & 1) == 1, adj[q], 0)
        low_sign[...] = 1.0 - 2.0 * fold_parity(index & partner).astype(jnp.float32)
        hi0, lo0 = split(g_ref[0].T)
        right0[0:128, 0:128] = hi0
        right0[0:128, 128:256] = lo0
        right0[128:256, 0:128] = hi0
        right0[128:256, 128:256] = jnp.zeros((128, 128), jnp.bfloat16)
        hi1, lo1 = split(g_ref[1])
        row = lax.broadcasted_iota(jnp.int32, (256, 128), 0)
        column = lax.broadcasted_iota(jnp.int32, (256, 128), 1)
        choose = jnp.where(column == (row & 3) * 32 + (row >> 3), 1.0, 0.0).astype(jnp.bfloat16)
        first = (row >> 2 & 1) == 0
        for i, part in enumerate((hi1, lo1)):
            picked = mm(choose, part)
            left1[i, :, 0:128] = jnp.where(first, picked, 0.0).astype(jnp.bfloat16)
            left1[i, :, 128:256] = jnp.where(first, 0.0, picked).astype(jnp.bfloat16)

    small = lax.broadcasted_iota(jnp.int32, (8, 128), 0) * 128 + lax.broadcasted_iota(jnp.int32, (8, 128), 1)
    for t in range(0, step_t, 2):
        tops = []
        lows = []
        for i in range(2):
            signed = []
            for r in range(2):
                m = (step * step_t + t + i) * 2 + r
                mask = masks[m]
                sign = 1.0 - 2.0 * (fold_parity(small & mask) ^ flips[m]).astype(jnp.float32)
                for q in range(10, QL):
                    flip = 1.0 - 2.0 * (mask >> q & 1).astype(jnp.float32)
                    sign = jnp.concatenate((sign, sign * flip), 0)
                signed.append(x_ref[t + i, r] * sign * low_sign[...])
            top, low = split(jnp.concatenate(signed, 0))
            both = mm(jnp.concatenate((top, low), 1), right0[...])
            top, low = split(both[:, 0:128] + both[:, 128:256])
            tops.append(top)
            lows.append(low)
        upper = jnp.concatenate(tops, 1)
        wide = mm(left1[0], jnp.concatenate((upper, *lows), 1))
        result = wide[:, 0:256] + wide[:, 256:512] + mm(left1[1], upper)
        size = 256 // PARTS
        for i in range(2):
            for c in range(PARTS):
                outs[c][t + i] = result[c * size : (c + 1) * size, i * 128 : (i + 1) * 128].reshape(size // 8, 8, 128)


def local_gates(x, gates, cz_pairs):
    step_t = 4
    part = jax.ShapeDtypeStruct((16, 32 // PARTS, 8, 128), jnp.float32)
    return pl.pallas_call(
        lambda *refs: local_kernel(step_t, *refs),
        out_shape=[part] * PARTS,
        grid=(16 // step_t,),
        in_specs=[
            pl.BlockSpec(memory_space=pltpu.SMEM),
            pl.BlockSpec((step_t, 2, 128, 128), lambda i: (i, 0, 0, 0)),
            pl.BlockSpec((3, 128, 128), lambda i: (0, 0, 0)),
        ],
        out_specs=[pl.BlockSpec((step_t, 32 // PARTS, 8, 128), lambda i: (i, 0, 0, 0))] * PARTS,
        scratch_shapes=[
            pltpu.SMEM((QUBITS,), jnp.int32),
            pltpu.SMEM((1 << QU,), jnp.int32),
            pltpu.SMEM((1 << QU,), jnp.int32),
            pltpu.VMEM((128, 128), jnp.float32),
            pltpu.VMEM((256, 256), jnp.bfloat16),
            pltpu.VMEM((2, 256, 256), jnp.bfloat16),
        ],
        name="local_gates",
    )(cz_pairs, x, gates)


def row_kernel(count, has_partner, has_base, *refs):
    turn_ref, g_ref = refs[:2]
    own_ref = refs[2]
    partner_ref = refs[3] if has_partner else None
    out_ref, left, right, lines = refs[3 + has_partner + has_base :]

    @pl.when(pl.program_id(0) == 0)
    def _():
        gate = g_ref[0]
        lane = lax.broadcasted_iota(jnp.int32, (128, 128), 1)
        odd = (lane >> 3 & 1) == 1
        crossed = jnp.where(odd, pltpu.roll(gate, 8, 1), pltpu.roll(gate, 120, 1))
        turned = turn_ref[2] * gate + jnp.where(odd, -turn_ref[3], turn_ref[3]) * crossed
        top, low = split(turned)
        left[:, 0:128] = top
        left[:, 128:256] = top
        left[:, 256:384] = low

    for s in range(8):
        value = own_ref[:, s].reshape(128, 128)
        if has_partner:
            value = turn_ref[0] * value + turn_ref[1] * partner_ref[:, s].reshape(128, 128)
        top, low = split(value)
        right[0:128, s * 128 : (s + 1) * 128] = top
        right[128:256, s * 128 : (s + 1) * 128] = low
    result = mm(left[:, 0:256], right[...]) + mm(left[:, 256:384], right[0:128, :])
    for s in range(8):
        lines[pl.ds(s, 128, stride=8), :] = result[:, s * 128 : (s + 1) * 128]
    out_ref[...] = lines[...].reshape(128, 1, 8, 128)


def row_gate(turn, gates, own, partner, base, first_group):
    groups = own.shape[1] // 8
    block = pl.BlockSpec((16, 8, 8, 128), lambda i: (0, i, 0, 0))
    operands = [turn, gates, own]
    specs = [
        pl.BlockSpec(memory_space=pltpu.SMEM),
        pl.BlockSpec((1, 128, 128), lambda i: (2, 0, 0)),
        block,
    ]
    if partner is not None:
        operands.append(partner)
        specs.append(block)
    aliases = {}
    if base is not None:
        aliases = {len(operands): 0}
        operands.append(base)
        specs.append(pl.BlockSpec(memory_space=pl.ANY))
    return pl.pallas_call(
        lambda *refs: row_kernel(groups, partner is not None, base is not None, *refs),
        out_shape=jax.ShapeDtypeStruct((128, 4, 8, 128), jnp.float32),
        grid=(groups,),
        in_specs=specs,
        out_specs=pl.BlockSpec((128, 1, 8, 128), lambda i: (0, first_group + i, 0, 0)),
        scratch_shapes=[
            pltpu.VMEM((128, 384), jnp.bfloat16),
            pltpu.VMEM((256, 1024), jnp.bfloat16),
            pltpu.VMEM((1024, 128), jnp.float32),
        ],
        input_output_aliases=aliases,
        name="row_gate",
    )(*operands)


def swap_lo(value, bit):
    return lax.ppermute(value, "lo", [(i, i ^ 1 << bit) for i in range(lax.axis_size("lo"))])


def remap(value):
    return lax.all_to_all(value, "hi", split_axis=0, concat_axis=0, tiled=True)


def per_device(amplitudes, gates, angles, cz_pairs):
    bit = lax.axis_size("lo").bit_length() - 2
    upper = (lax.axis_index("lo") >> bit & 1).astype(jnp.float32)
    cosines = jnp.cos(angles * 0.5)
    sines = jnp.sin(angles * 0.5)
    turn = jnp.stack((cosines[0], (2.0 * upper - 1.0) * sines[0], cosines[1], sines[1]))
    early, late = local_gates(amplitudes.reshape(16, 2, 128, 128), gates, cz_pairs)
    early_partner = swap_lo(early, bit)
    late = remap(late)
    late_partner = swap_lo(late, bit)
    early = remap(turn[0] * early + turn[1] * early_partner)
    result = row_gate(turn, gates, early, None, None, 0)
    result = row_gate(turn, gates, late, late_partner, result, 2)
    return result.reshape(amplitudes.shape)


def solution(mesh):
    placed = (P("hi", "lo", None, None, None), P(), P(), P())
    return jax.shard_map(
        per_device,
        mesh=mesh,
        in_specs=placed,
        out_specs=P("hi", "lo", None, None, None),
        check_vma=False,
    )
```

time: 250 us -> 112 us (0.45)
  the two profiles are of different devices: /device:TPU:12 before, /device:TPU:42 now
where the time goes in v1:
time: 112 us
  waiting for transfers between devices  58 us (52%)
  starting transfers between devices  33.4 us (30%)
  Pallas kernels  11.4 us (10%)
  other arithmetic  4.2 us (4%)
  local copies, waits for them, and re-layouts  4.04 us (4%)
    all_to_all x2, waiting for transfers between devices, remap(): return lax.all_to_all(value, 'hi', split_axis=0, concat_axis=0, tiled=True)  35.6 us
    all_to_all x2, starting transfers between devices, remap(): return lax.all_to_all(value, 'hi', split_axis=0, concat_axis=0, tiled=True)  25.4 us
    ppermute x2, waiting for transfers between devices, swap_lo(): lax.ppermute(value, 'lo', [(i, i ^ 1 << bit) for i in range(lax.axis_size...  22.3 us
    ppermute x2, starting transfers between devices, swap_lo(): lax.ppermute(value, 'lo', [(i, i ^ 1 << bit) for i in range(lax.axis_size...  8.01 us
    pallas_call x2, Pallas kernels, row_gate(): pl.pallas_call(lambda *refs: row_kernel(groups, partner is not None, base...  5.82 us
    pallas_call x1, Pallas kernels, local_gates(): pl.pallas_call(lambda *refs: local_kernel(step_t, *refs), out_shape=[part...  5.54 us
    unnamed x11, local copies, waits for them, and re-layouts  3.36 us
    another operation x1, other arithmetic, per_device(): jnp.stack((cosines[0], (2.0 * upper - 1.0) * sines[0], cosines[1], sines[...  2.5 us
  transfers between devices with their start and end apart: 4, of which 3 were waited for; matrix products, arithmetic and copies ran while one was open for 4% of the time, Pallas kernels for 2%

profile of v1, /device:TPU:42, one launch (start us, length us, event | category | flops | bytes accessed | tf_op | source)
XLA Modules:
  0.0 111.7 jit_solution(13529284090764038838)
XLA Ops:
  0.0 1.4 %copy.6.refs_0_ = s32[24,2]{1,0:T(8,128)} copy(s32[24,2]{0,1:T(2,128)} %param.7) | data formatting | bytes 384 | tf_op args[3]
  1.4 0.0 copy-start.4
  1.4 5.5 %local_gates.1 = (f32[16,16,8,128]{3,2,1,0:T(8,128)}, f32[16,16,8,128]{3,2,1,0:T(8,128)}) custom-call(s32[24,2]{1,0:T(8,128)} %copy.6.refs_0_, f32[16,2,128,128]{3,2,1,0:T(8,128)} %bitcast.5, f32[3,128,128]{2,1,0:T(8,128)} %refs_1_.3), custom_call_target="tpu_custom_call" | custom-call | tf_op jit(solution)/shard_map/local_gates/pallas_call | solution.py:103
  6.9 0.0 copy-start.3
  6.9 15.8 %all-to-all-start = ((f32[16,16,8,128]{3,2,1,0:T(8,128)}), f32[16,16,8,128]{3,2,1,0:T(8,128)S(1)}, u32[]{:S(2)}, u32[]{:S(2)}) async-start(f32[16,16,8,128]{3,2,1,0:T(8,128)} %get-tuple-element.7), calls=%async_computation | async-start | bytes 2097152 | tf_op jit(solution)/shard_map/all_to_all | solution.py:194
  22.7 0.0 copy-done.3
  22.7 4.0 %collective-permute-start.1 = (f32[16,16,8,128]{3,2,1,0:T(8,128)S(1)}, f32[16,16,8,128]{3,2,1,0:T(8,128)S(1)}, u32[]{:S(2)}, u32[]{:S(2)}) collective-permute-start(f32[16,16,8,128]{3,2,1,0:T(8,128)S(1)} %copy-done.3), channel_id=1, source_target_pairs={{0,16},{1,17},{2,18},{3,19},{4,20},{5,21},{6,22},{7,23},{8,24},{9,... | collective-permute-start | bytes 3145736 | tf_op jit(solution)/shard_map/ppermute | solution.py:190
  26.8 0.0 copy-done.4
  26.8 0.7 fusion
  28.2 22.3 %collective-permute-done.1 = f32[16,16,8,128]{3,2,1,0:T(8,128)S(1)} collective-permute-done((f32[16,16,8,128]{3,2,1,0:T(8,128)S(1)}, f32[16,16,8,128]{3,2,1,0:T(8,128)S(1)}, u32[]{:S(2)}, u32[]{:S(2)}) %collective-permute-start.1) | collective-permute-done | bytes 1048608 | tf_op jit(solution)/shard_map/ppermute | solution.py:190
  50.5 1.7 %multiply_add_fusion = f32[16,16,8,128]{3,2,1,0:T(8,128)} fusion(f32[16,16,8,128]{3,2,1,0:T(8,128)S(1)} %collective-permute-done.1, f32[16,16,8,128]{3,2,1,0:T(8,128)S(1)} %copy-done.3, f32[]{:T(128)} %mul.20, f32[]{:T(128)} %bitcast.3), kind=kLoop, calls=%fused_computation | loop fusion | flops 786432 | bytes 3145736 | tf_op jit(solution)/shard_map/add | solution.py:207
  52.1 10.4 %all-to-all-done.refs_2_ = f32[16,16,8,128]{3,2,1,0:T(8,128)S(1)} async-done(((f32[16,16,8,128]{3,2,1,0:T(8,128)}), f32[16,16,8,128]{3,2,1,0:T(8,128)S(1)}, u32[]{:S(2)}, u32[]{:S(2)}) %all-to-all-start) | async-done | bytes 1048608 | tf_op jit(solution)/shard_map/all_to_all | solution.py:194
  62.6 0.0 copy-start
  62.6 9.6 %all-to-all-start.1 = ((f32[16,16,8,128]{3,2,1,0:T(8,128)}), f32[16,16,8,128]{3,2,1,0:T(8,128)S(1)}, u32[]{:S(2)}, u32[]{:S(2)}) async-start(f32[16,16,8,128]{3,2,1,0:T(8,128)} %multiply_add_fusion), calls=%async_computation.1 | async-start | bytes 2097152 | tf_op jit(solution)/shard_map/all_to_all | solution.py:194
  72.1 4.0 %collective-permute-start = (f32[16,16,8,128]{3,2,1,0:T(8,128)S(1)}, f32[16,16,8,128]{3,2,1,0:T(8,128)S(1)}, u32[]{:S(2)}, u32[]{:S(2)}) collective-permute-start(f32[16,16,8,128]{3,2,1,0:T(8,128)S(1)} %all-to-all-done.refs_2_), channel_id=1, source_target_pairs={{0,16},{1,17},{2,18},{3,19},{4,20},{5,21},{6,22},{7,23},{8,24},{9,... | collective-permute-start | bytes 3145736 | tf_op jit(solution)/shard_map/ppermute | solution.py:190
  76.1 2.5 %pad_maximum_fusion.refs_0_ = f32[4]{0:T(128)} fusion(f32[1]{0:T(128)} %get-tuple-element.15, f32[1]{0:T(128)} %get-tuple-element.10, f32[1]{0:T(128)} %bitcast.1, f32[1]{0:T(128)} %get-tuple-element.9), kind=kLoop, calls=%fused_computation.1 | loop fusion | flops 12 | bytes 32 | tf_op jit(solution)/shard_map/stack | solution.py:202
  78.6 25.2 %all-to-all-done.1.refs_2_ = f32[16,16,8,128]{3,2,1,0:T(8,128)S(1)} async-done(((f32[16,16,8,128]{3,2,1,0:T(8,128)}), f32[16,16,8,128]{3,2,1,0:T(8,128)S(1)}, u32[]{:S(2)}, u32[]{:S(2)}) %all-to-all-start.1) | async-done | bytes 1048608 | tf_op jit(solution)/shard_map/all_to_all | solution.py:194
  103.8 0.0 copy-start.1
  103.8 1.0 copy-done.1
  104.8 2.8 %row_gate.2.refs_4_ = f32[128,4,8,128]{3,2,1,0:T(8,128)} custom-call(f32[4]{0:T(128)} %pad_maximum_fusion.refs_0_, f32[3,128,128]{2,1,0:T(8,128)} %refs_1_.3, f32[16,16,8,128]{3,2,1,0:T(8,128)} %copy-done.1), custom_call_target="tpu_custom_call" | custom-call | tf_op jit(solution)/shard_map/row_gate/pallas_call | solution.py:173
  107.6 0.0 copy-done
  107.6 0.0 collective-permute-done.refs_3_
  107.6 0.0 copy-start.2
  107.6 1.0 copy-done.2
  108.6 3.1 %row_gate.3 = f32[128,4,8,128]{3,2,1,0:T(8,128)} custom-call(f32[4]{0:T(128)} %pad_maximum_fusion.refs_0_, f32[3,128,128]{2,1,0:T(8,128)} %refs_1_.3, f32[16,16,8,128]{3,2,1,0:T(8,128)} %copy-done, f32[16,16,8,128]{3,2,1,0:T(8,128)} %copy-done.2, f32[128,4,8,128]{3,2,1,0:T(8,128)} %row_gate.2.refs_4_), custom_call_target="tpu_custom_call", output_to_operand_aliasing={{}: (4, {})} | custom-call | tf_op jit(solution)/shard_map/row_gate/pallas_call | solution.py:173
  (1 shorter events, 0.0 us)
Async XLA Ops:
  1.4 25.4 %copy-start.4 = (f32[2]{0:T(128)S(1)}, f32[2]{0:T(128)}, u32[]{:S(2)}) copy-start(f32[2]{0:T(128)} %param.6) | copy-start | bytes 28
  6.9 15.8 %copy-start.3 = (f32[16,16,8,128]{3,2,1,0:T(8,128)S(1)}, f32[16,16,8,128]{3,2,1,0:T(8,128)}, u32[]{:S(2)}) copy-start(f32[16,16,8,128]{3,2,1,0:T(8,128)} %get-tuple-element.8) | copy-start | bytes 3145732
  6.9 55.7 %all-to-all-start = ((f32[16,16,8,128]{3,2,1,0:T(8,128)}), f32[16,16,8,128]{3,2,1,0:T(8,128)S(1)}, u32[]{:S(2)}, u32[]{:S(2)}) async-start(f32[16,16,8,128]{3,2,1,0:T(8,128)} %get-tuple-element.7), calls=%async_computation | async-start | bytes 2097152 | tf_op jit(solution)/shard_map/all_to_all | solution.py:194
  22.7 27.7 %collective-permute-start.1 = (f32[16,16,8,128]{3,2,1,0:T(8,128)S(1)}, f32[16,16,8,128]{3,2,1,0:T(8,128)S(1)}, u32[]{:S(2)}, u32[]{:S(2)}) collective-permute-start(f32[16,16,8,128]{3,2,1,0:T(8,128)S(1)} %copy-done.3), channel_id=1, source_target_pairs={{0,16},{1,17},{2,18},{3,19},{4,20},{5,21},{6,22},{7,23},{8,24},{9,... | collective-permute-start | bytes 3145736 | tf_op jit(solution)/shard_map/ppermute | solution.py:190
  62.6 45.0 %copy-start = (f32[16,16,8,128]{3,2,1,0:T(8,128)}, f32[16,16,8,128]{3,2,1,0:T(8,128)S(1)}, u32[]{:S(2)}) copy-start(f32[16,16,8,128]{3,2,1,0:T(8,128)S(1)} %all-to-all-done.refs_2_) | copy-start | bytes 3145732
  62.6 41.3 %all-to-all-start.1 = ((f32[16,16,8,128]{3,2,1,0:T(8,128)}), f32[16,16,8,128]{3,2,1,0:T(8,128)S(1)}, u32[]{:S(2)}, u32[]{:S(2)}) async-start(f32[16,16,8,128]{3,2,1,0:T(8,128)} %multiply_add_fusion), calls=%async_computation.1 | async-start | bytes 2097152 | tf_op jit(solution)/shard_map/all_to_all | solution.py:194
  72.1 35.5 %collective-permute-start = (f32[16,16,8,128]{3,2,1,0:T(8,128)S(1)}, f32[16,16,8,128]{3,2,1,0:T(8,128)S(1)}, u32[]{:S(2)}, u32[]{:S(2)}) collective-permute-start(f32[16,16,8,128]{3,2,1,0:T(8,128)S(1)} %all-to-all-done.refs_2_), channel_id=1, source_target_pairs={{0,16},{1,17},{2,18},{3,19},{4,20},{5,21},{6,22},{7,23},{8,24},{9,... | collective-permute-start | bytes 3145736 | tf_op jit(solution)/shard_map/ppermute | solution.py:190
  103.8 1.0 copy-start.1
  107.6 1.0 copy-start.2

commit v2 on v1

v2 whole, which is shorter than its diff:
```python
import jax
import jax.numpy as jnp
from jax import lax
from jax.experimental import pallas as pl
from jax.experimental.pallas import tpu as pltpu
from jax.sharding import PartitionSpec as P

QL = 14
QU = 5
QUBITS = QL + QU
STEP = 2
SMEM = pl.BlockSpec(memory_space=pltpu.SMEM)
VMEM = pl.BlockSpec(memory_space=pltpu.VMEM)
ANY = pl.BlockSpec(memory_space=pl.ANY)
BOTH = (8, 2, 16, 8, 128)
ONE = (8, 16, 8, 128)


def split(value):
    top = value.astype(jnp.bfloat16)
    return top, (value - top.astype(jnp.float32)).astype(jnp.bfloat16)


def fold_parity(bits):
    for step in (8, 4, 2, 1):
        bits = bits ^ (bits >> step)
    return bits & 1


def mm(left, right):
    return lax.dot_general(left, right, (((1,), (0,)), ((), ())), preferred_element_type=jnp.float32)


def on_chip(value):
    return pltpu.with_memory_space_constraint(value, pltpu.VMEM)


def off_chip(value):
    return pltpu.with_memory_space_constraint(value, pltpu.HBM)


def gate_pair(left, upper, lower):
    wide = mm(left[0], jnp.concatenate((upper, lower), 1))
    return wide[:, 0:256] + wide[:, 256:512] + mm(left[1], upper)


def local_kernel(cz_ref, hi_ref, x_ref, g_ref, *rest):
    keep_ref, send_ref, upper_ref, lower_ref, late_left_ref = rest[:5]
    adj, masks, flips, low_sign, right0, left1 = rest[5:]
    step = pl.program_id(0)
    odd = hi_ref[0] & 1

    @pl.when(step == 0)
    def _():
        for q in range(QUBITS):
            adj[q] = 0
        for p in range(cz_ref.shape[1]):
            a = cz_ref[0, p]
            b = cz_ref[1, p]
            q = jnp.maximum(a, b)
            adj[q] = adj[q] ^ (1 << jnp.minimum(a, b))
        masks[0] = 0
        flips[0] = 0
        for u in range(QU):
            row = adj[QL + u]
            for m in range(1 << u):
                masks[m + (1 << u)] = masks[m] ^ (row & ((1 << QL) - 1))
                flips[m + (1 << u)] = flips[m] ^ fold_parity((row >> QL) & m)
        row_id = lax.broadcasted_iota(jnp.int32, (128, 128), 0)
        lane_id = lax.broadcasted_iota(jnp.int32, (128, 128), 1)
        index = row_id * 128 + lane_id
        partner = jnp.zeros_like(index)
        for q in range(1, QL):
            partner = partner ^ jnp.where((index >> q & 1) == 1, adj[q], 0)
        low_sign[...] = 1.0 - 2.0 * fold_parity(index & partner).astype(jnp.float32)
        hi0, lo0 = split(g_ref[0].T)
        right0[0:128, 0:128] = hi0
        right0[0:128, 128:256] = lo0
        right0[128:256, 0:128] = hi0
        right0[128:256, 128:256] = jnp.zeros((128, 128), jnp.bfloat16)
        hi1, lo1 = split(g_ref[1])
        row = lax.broadcasted_iota(jnp.int32, (256, 128), 0)
        column = lax.broadcasted_iota(jnp.int32, (256, 128), 1)
        choose = jnp.where(column == (row & 3) * 32 + (row >> 3), 1.0, 0.0).astype(jnp.bfloat16)
        first = (row >> 2 & 1) == 0
        for i, part in enumerate((hi1, lo1)):
            picked = mm(choose, part)
            one = jnp.where(first, picked, 0.0).astype(jnp.bfloat16)
            other = jnp.where(first, 0.0, picked).astype(jnp.bfloat16)
            left1[i, :, 0:128] = one[0:128]
            left1[i, :, 128:256] = other[0:128]
            late_left_ref[i, :, 0:128] = one[128:256]
            late_left_ref[i, :, 128:256] = other[128:256]

    small = lax.broadcasted_iota(jnp.int32, (8, 128), 0) * 128 + lax.broadcasted_iota(jnp.int32, (8, 128), 1)
    for local in range(STEP):
        z = step * STEP + local
        tops = []
        lows = []
        for s in range(2):
            signed = []
            y = odd ^ s
            for r in range(2):
                m = z * 4 + y * 2 + r
                mask = masks[m]
                sign = 1.0 - 2.0 * (fold_parity(small & mask) ^ flips[m]).astype(jnp.float32)
                for q in range(10, QL):
                    flip = 1.0 - 2.0 * (mask >> q & 1).astype(jnp.float32)
                    sign = jnp.concatenate((sign, sign * flip), 0)
                signed.append(x_ref[local, y, r] * sign * low_sign[...])
            top, low = split(jnp.concatenate(signed, 0))
            both = mm(jnp.concatenate((top, low), 1), right0[...])
            top, low = split(both[:, 0:128] + both[:, 128:256])
            tops.append(top)
            lows.append(low)
        upper = jnp.concatenate(tops, 1)
        lower = jnp.concatenate(lows, 1)
        upper_ref[z] = upper
        lower_ref[z] = lower
        result = gate_pair(left1, upper, lower)
        keep_ref[z] = result[:, 0:128].reshape(16, 8, 128)
        send_ref[z] = result[:, 128:256].reshape(16, 8, 128)


def local_gates(x, gates, cz_pairs, hi):
    held = pltpu.VMEM((8, 256, 256), jnp.bfloat16)
    return pl.pallas_call(
        local_kernel,
        out_shape=[
            pltpu.VMEM(ONE, jnp.float32),
            pltpu.VMEM(ONE, jnp.float32),
            held,
            held,
            pltpu.VMEM((2, 128, 256), jnp.bfloat16),
        ],
        grid=(8 // STEP,),
        in_specs=[
            SMEM,
            SMEM,
            pl.BlockSpec((STEP, 2, 2, 128, 128), lambda i: (i, 0, 0, 0, 0)),
            pl.BlockSpec((3, 128, 128), lambda i: (0, 0, 0)),
        ],
        out_specs=[VMEM] * 5,
        scratch_shapes=[
            pltpu.SMEM((QUBITS,), jnp.int32),
            pltpu.SMEM((1 << QU,), jnp.int32),
            pltpu.SMEM((1 << QU,), jnp.int32),
            pltpu.VMEM((128, 128), jnp.float32),
            pltpu.VMEM((256, 256), jnp.bfloat16),
            pltpu.VMEM((2, 128, 256), jnp.bfloat16),
        ],
        compiler_params=pltpu.CompilerParams(vmem_limit_bytes=16 << 20),
        name="local_gates",
    )(cz_pairs.T, hi, off_chip(x), off_chip(gates))


def late_kernel(upper_ref, lower_ref, left_ref, late_ref):
    for i in range(STEP):
        z = pl.program_id(0) * STEP + i
        result = gate_pair(left_ref, upper_ref[z], lower_ref[z])
        for s in range(2):
            late_ref[i, s] = result[:, s * 128 : (s + 1) * 128].reshape(16, 8, 128)


def late_gate(upper, lower, left):
    return pl.pallas_call(
        late_kernel,
        out_shape=jax.ShapeDtypeStruct(BOTH, jnp.float32),
        grid=(8 // STEP,),
        in_specs=[VMEM] * 3,
        out_specs=pl.BlockSpec((STEP, 2, 16, 8, 128), lambda i: (i, 0, 0, 0, 0)),
        compiler_params=pltpu.CompilerParams(vmem_limit_bytes=6 << 20),
        name="late_gate",
    )(on_chip(upper), on_chip(lower), on_chip(left))


def lo_turn(cos_ref, sin_ref, lo_ref):
    sine = sin_ref[0]
    return cos_ref[0], jnp.where((lo_ref[0] >> 4 & 1) == 1, sine, -sine)


def merge_kernel(cos_ref, sin_ref, lo_ref, keep, keep_partner, other, other_partner, late_keep, out_ref):
    c, f = lo_turn(cos_ref, sin_ref, lo_ref)
    part = pl.ds(pl.program_id(0) * STEP, STEP)
    out_ref[:, 0] = c * keep[part] + f * keep_partner[part]
    out_ref[:, 1] = c * other[part] + f * other_partner[part]


def merge(turn, parts, late_keep):
    return pl.pallas_call(
        merge_kernel,
        out_shape=jax.ShapeDtypeStruct(BOTH, jnp.float32),
        grid=(8 // STEP,),
        in_specs=[SMEM] * 3 + [VMEM] * 5,
        out_specs=pl.BlockSpec((STEP, 2, 16, 8, 128), lambda i: (i, 0, 0, 0, 0)),
        compiler_params=pltpu.CompilerParams(vmem_limit_bytes=6 << 20),
        name="merge",
    )(*turn, *map(on_chip, parts), on_chip(late_keep))


def cut_kernel(in_ref, left_ref, keep_ref, send_ref):
    keep_ref[...] = in_ref[:, 0]
    send_ref[...] = in_ref[:, 1]


def cut(value, left):
    return pl.pallas_call(
        cut_kernel,
        out_shape=[pltpu.VMEM(ONE, jnp.float32)] * 2,
        in_specs=[VMEM, VMEM],
        out_specs=[VMEM] * 2,
        compiler_params=pltpu.CompilerParams(vmem_limit_bytes=4 << 20),
        name="cut",
    )(on_chip(value), on_chip(left))


def matrix_kernel(cos_ref, sin_ref, hi_ref, g_ref, keep_partner, other, left_ref):
    gate = g_ref[0]
    lane = lax.broadcasted_iota(jnp.int32, (128, 128), 1)
    upper = (lane >> 3 & 1) == 1
    crossed = jnp.where(upper, pltpu.roll(gate, 8, 1), pltpu.roll(gate, 120, 1))
    cosine = cos_ref[1]
    sine = jnp.where(upper, -sin_ref[1], sin_ref[1])
    turned = jnp.where((hi_ref[0] & 1) == 1, cosine * crossed - sine * gate, cosine * gate + sine * crossed)
    top, low = split(turned)
    left_ref[:, 0:128] = top
    left_ref[:, 128:256] = top
    left_ref[:, 256:384] = low


def row_matrix(cosines, sines, hi, gates, *after):
    return pl.pallas_call(
        matrix_kernel,
        out_shape=pltpu.VMEM((128, 384), jnp.bfloat16),
        grid=(1,),
        in_specs=[SMEM] * 3 + [pl.BlockSpec((1, 128, 128), lambda i: (2, 0, 0))] + [VMEM] * len(after),
        out_specs=VMEM,
        cost_estimate=pl.CostEstimate(flops=10**11, transcendentals=0, bytes_accessed=10**5),
        compiler_params=pltpu.CompilerParams(vmem_limit_bytes=2 << 20),
        name="row_matrix",
    )(cosines, sines, hi, off_chip(gates), *map(on_chip, after))


def hold_kernel(in_ref, keep_partner, other, out_ref):
    out_ref[...] = in_ref[...]


def hold(left, *after):
    return pl.pallas_call(
        hold_kernel,
        out_shape=pltpu.VMEM(left.shape, left.dtype),
        in_specs=[VMEM] * (1 + len(after)),
        out_specs=VMEM,
        compiler_params=pltpu.CompilerParams(vmem_limit_bytes=2 << 20),
        cost_estimate=pl.CostEstimate(flops=10**11, transcendentals=0, bytes_accessed=10**5),
        name="hold",
    )(*map(on_chip, (left, *after)))


def write_rows(left, values, right, lines, out_ref):
    for s, value in enumerate(values):
        top, low = split(value)
        right[0:128, s * 128 : (s + 1) * 128] = top
        right[128:256, s * 128 : (s + 1) * 128] = low
    result = mm(left[:, 0:256], right[...]) + mm(left[:, 256:384], right[0:128, :])
    for s in range(8):
        lines[pl.ds(s, 128, stride=8), :] = result[:, s * 128 : (s + 1) * 128]
    out_ref[...] = lines[...].reshape(128, 1, 8, 128)


def joined(keep, other):
    return jnp.concatenate((keep[:, None], other[:, None]), 1).reshape(128, 128)


def rows_whole(left, own, *rest):
    out_ref, right, lines = rest[-3:]
    start = pl.program_id(0) * 8
    write_rows(left, [own[:, :, start + s].reshape(128, 128) for s in range(8)], right, lines, out_ref)


def rows_turning(cos_ref, sin_ref, lo_ref, left, keep, keep_partner, other, other_partner, *rest):
    out_ref, right, lines = rest[-3:]
    c, f = lo_turn(cos_ref, sin_ref, lo_ref)
    start = pl.program_id(0) * 8
    values = []
    for s in [start + i for i in range(8)]:
        values.append(joined(c * keep[:, s] + f * keep_partner[:, s], c * other[:, s] + f * other_partner[:, s]))
    write_rows(left, values, right, lines, out_ref)


def row_gate(body, scalars, left, parts, base, group):
    operands = [*scalars, on_chip(left), *map(on_chip, parts)]
    specs = [SMEM] * len(scalars) + [VMEM] * (1 + len(parts))
    aliases = {}
    if base is not None:
        aliases = {len(operands): 0}
        operands.append(base)
        specs.append(ANY)
    return pl.pallas_call(
        body,
        out_shape=jax.ShapeDtypeStruct((128, 4, 8, 128), jnp.float32),
        grid=(2,),
        in_specs=specs,
        out_specs=pl.BlockSpec((128, 1, 8, 128), lambda i: (0, group + i, 0, 0)),
        scratch_shapes=[pltpu.VMEM((256, 1024), jnp.bfloat16), pltpu.VMEM((1024, 128), jnp.float32)],
        input_output_aliases=aliases,
        compiler_params=pltpu.CompilerParams(vmem_limit_bytes=8 << 20),
        name="row_gate",
    )(*operands)


def swap_lo(value):
    count = lax.axis_size("lo")
    return lax.ppermute(value, "lo", [(i, i ^ count // 2) for i in range(count)])


def swap_hi(value):
    return lax.ppermute(value, "hi", [(i, i ^ 1) for i in range(lax.axis_size("hi"))])


def remap(value):
    count = lax.axis_size("hi")
    groups = [list(range(y, count, 2)) for y in range(2)]
    return lax.all_to_all(value, "hi", split_axis=0, concat_axis=0, tiled=True, axis_index_groups=groups)


def per_device(amplitudes, gates, angles, cz_pairs):
    hi = lax.axis_index("hi").reshape(1)
    lo = lax.axis_index("lo").reshape(1)
    cosines = jnp.cos(angles * 0.5)
    sines = jnp.sin(angles * 0.5)
    turn = (cosines, sines, lo)
    keep, send, upper, lower, late_left = local_gates(amplitudes.reshape(8, 2, 2, 128, 128), gates, cz_pairs, hi)
    other = swap_hi(send)
    keep_partner = swap_lo(keep)
    late = remap(late_gate(upper, lower, late_left))
    left = row_matrix(cosines, sines, hi, gates, keep_partner, other)
    early_parts = (keep, keep_partner, other, swap_lo(other))
    keep, send = cut(late, left)
    early = remap(merge(turn, early_parts, keep))
    other = swap_hi(send)
    keep_partner = swap_lo(keep)
    left = hold(left, keep_partner, other)
    result = row_gate(rows_turning, turn, left, (keep, keep_partner, other, swap_lo(other)), None, 2)
    result = row_gate(rows_whole, (), left, (early,), result, 0)
    return result.reshape(amplitudes.shape)


def solution(mesh):
    placed = (P("hi", "lo", None, None, None), P(), P(), P())
    return jax.shard_map(
        per_device,
        mesh=mesh,
        in_specs=placed,
        out_specs=P("hi", "lo", None, None, None),
        check_vma=False,
    )
```

time: 112 us -> 110 us (0.982)
  the two profiles are of different devices: /device:TPU:42 before, /device:TPU:8 now
where the time goes in v2:
time: 110 us
  waiting for transfers between devices  53.8 us (49%)
  starting transfers between devices  38.2 us (35%)
  Pallas kernels  15.7 us (14%)
  local copies, waits for them, and re-layouts  1.72 us (2%)
    ppermute x2, waiting for transfers between devices, swap_hi(): lax.ppermute(value, 'hi', [(i, i ^ 1) for i in range(lax.axis_size('hi'))])  23.2 us
    all_to_all x2, waiting for transfers between devices, remap(): lax.all_to_all(value, 'hi', split_axis=0, concat_axis=0, tiled=True, axis...  16.2 us
    ppermute x4, starting transfers between devices, swap_lo(): lax.ppermute(value, 'lo', [(i, i ^ count // 2) for i in range(count)])  14.6 us
    ppermute x4, waiting for transfers between devices, swap_lo(): lax.ppermute(value, 'lo', [(i, i ^ count // 2) for i in range(count)])  14.3 us
    all_to_all x2, starting transfers between devices, remap(): lax.all_to_all(value, 'hi', split_axis=0, concat_axis=0, tiled=True, axis...  13.9 us
    ppermute x2, starting transfers between devices, swap_hi(): lax.ppermute(value, 'hi', [(i, i ^ 1) for i in range(lax.axis_size('hi'))])  9.74 us
    pallas_call x1, Pallas kernels, local_gates(): pl.pallas_call(local_kernel, out_shape=[pltpu.VMEM(ONE, jnp.float32), plt...  4.54 us
    pallas_call x2, Pallas kernels, row_gate(): pl.pallas_call(body, out_shape=jax.ShapeDtypeStruct((128, 4, 8, 128), jnp...  3.85 us
  transfers between devices with their start and end apart: 8, of which 4 were waited for; matrix products, arithmetic and copies ran while one was open for 0% of the time, Pallas kernels for 9%

profile of v2, /device:TPU:8, one launch (start us, length us, event | category | flops | bytes accessed | tf_op | source)
XLA Modules:
  0.0 109.6 jit_solution(16104632343780513939)
XLA Ops:
  0.0 0.0 copy-start.2
  0.0 0.7 copy-done.2
  0.7 4.5 %local_gates.1 = (f32[8,16,8,128]{3,2,1,0:T(8,128)S(1)}, f32[8,16,8,128]{3,2,1,0:T(8,128)S(1)}, bf16[8,256,256]{2,1,0:T(8,128)(2,1)S(1)}, bf16[8,256,256]{2,1,0:T(8,128)(2,1)S(1)}, bf16[2,128,256]{2,1,0:T(8,128)(2,1)S(1)}) custom-call(s32[2,24]{1,0:T(2,128)S(1)} %bitcast.5, s32[1]{0:T(128)} %bitcast.hi_ref, f32[8,2,2,128,128]{4,3,2,1,0:T(8,128)} %bitcast.6, ...), custom_call_target="tpu_custom_call" | custom-call | tf_op jit(solution)/shard_map/local_gates/pallas_call | solution.py:127
  5.2 6.8 %collective-permute-start.1 = (f32[8,16,8,128]{3,2,1,0:T(8,128)S(1)}, f32[8,16,8,128]{3,2,1,0:T(8,128)}, u32[]{:S(2)}, u32[]{:S(2)}) collective-permute-start(f32[8,16,8,128]{3,2,1,0:T(8,128)S(1)} %get-tuple-element.13), channel_id=1, source_target_pairs={{0,32},{32,0},{64,96},{96,64},{128,160},{160,128},{192,224},{224,1... | collective-permute-start | bytes 1572872 | tf_op jit(solution)/shard_map/ppermute | solution.py:318
  12.1 4.9 %collective-permute-start = (f32[8,16,8,128]{3,2,1,0:T(8,128)S(1)}, f32[8,16,8,128]{3,2,1,0:T(8,128)S(1)}, u32[]{:S(2)}, u32[]{:S(2)}) collective-permute-start(f32[8,16,8,128]{3,2,1,0:T(8,128)S(1)} %get-tuple-element.12.keep), channel_id=1, source_target_pairs={{0,16},{1,17},{2,18},{3,19},{4,20},{5,21},{6,22},{7,23},{8,24},{9,... | collective-permute-start | bytes 1572872 | tf_op jit(solution)/shard_map/ppermute | solution.py:314
  17.0 0.0 copy-start.3
  17.0 2.3 %late_gate.1 = f32[8,2,16,8,128]{4,3,2,1,0:T(8,128)} custom-call(bf16[8,256,256]{2,1,0:T(8,128)(2,1)S(1)} %get-tuple-element.14.upper_ref, bf16[8,256,256]{2,1,0:T(8,128)(2,1)S(1)} %get-tuple-element.15.lower_ref, bf16[2,128,256]{2,1,0:T(8,128)(2,1)S(1)} %get-tuple-element.16.left_ref), custom_call_target="tpu_custom_call" | custom-call | tf_op jit(solution)/shard_map/late_gate/pallas_call | solution.py:166
  19.3 10.3 %all-to-all-start = ((f32[8,2,16,8,128]{4,3,2,1,0:T(8,128)}), f32[8,2,16,8,128]{4,3,2,1,0:T(8,128)S(1)}, u32[]{:S(2)}, u32[]{:S(2)}) async-start(f32[8,2,16,8,128]{4,3,2,1,0:T(8,128)} %late_gate.1), calls=%async_computation | async-start | bytes 2097152 | tf_op jit(solution)/shard_map/all_to_all | solution.py:324
  29.6 0.0 copy-done.3
  29.6 5.6 %collective-permute-done.1.other = f32[8,16,8,128]{3,2,1,0:T(8,128)} collective-permute-done((f32[8,16,8,128]{3,2,1,0:T(8,128)S(1)}, f32[8,16,8,128]{3,2,1,0:T(8,128)}, u32[]{:S(2)}, u32[]{:S(2)}) %collective-permute-start.1) | collective-permute-done | bytes 524320 | tf_op jit(solution)/shard_map/ppermute | solution.py:318
  35.2 4.9 %collective-permute-start.4 = (f32[8,16,8,128]{3,2,1,0:T(8,128)}, f32[8,16,8,128]{3,2,1,0:T(8,128)}, u32[]{:S(2)}, u32[]{:S(2)}) collective-permute-start(f32[8,16,8,128]{3,2,1,0:T(8,128)} %collective-permute-done.1.other), channel_id=1, source_target_pairs={{0,16},{1,17},{2,18},{3,19},{4,20},{5,21},{6,22},{7,23},{8,24},{9,... | collective-permute-start | bytes 1572872 | tf_op jit(solution)/shard_map/ppermute | solution.py:314
  40.1 0.0 collective-permute-done.keep_partner
  40.1 0.0 copy-start
  40.1 1.4 %row_matrix.1.left_ref.in_ref = bf16[128,384]{1,0:T(8,128)(2,1)S(1)} custom-call(f32[2]{0:T(128)S(1)} %get-tuple-element.20.cos_ref, f32[2]{0:T(128)S(1)} %get-tuple-element.19.sin_ref, s32[1]{0:T(128)} %bitcast.hi_ref, f32[3,128,128]{2,1,0:T(8,128)} %g_ref.3, f32[8,16,8,128]{3,2,1,0:T(8,128)S(1)} %collective-permute-done.keep_partner, ...), custom_call_target="tpu_custom_call" | custom-call | flops 99999997952 | bytes 100000 | tf_op jit(solution)/shard_map/row_matrix/pallas_call | solution.py:232
  41.5 0.0 copy-done
  41.5 16.2 %all-to-all-done.in_ref = f32[8,2,16,8,128]{4,3,2,1,0:T(8,128)S(1)} async-done(((f32[8,2,16,8,128]{4,3,2,1,0:T(8,128)}), f32[8,2,16,8,128]{4,3,2,1,0:T(8,128)S(1)}, u32[]{:S(2)}, u32[]{:S(2)}) %all-to-all-start) | async-done | bytes 1048608 | tf_op jit(solution)/shard_map/all_to_all | solution.py:324
  57.8 0.9 cut.1
  58.6 2.9 %collective-permute-start.3 = (f32[8,16,8,128]{3,2,1,0:T(8,128)}, f32[8,16,8,128]{3,2,1,0:T(8,128)S(1)}, u32[]{:S(2)}, u32[]{:S(2)}) collective-permute-start(f32[8,16,8,128]{3,2,1,0:T(8,128)} %get-tuple-element.18), channel_id=1, source_target_pairs={{0,32},{32,0},{64,96},{96,64},{128,160},{160,128},{192,224},{224,1... | collective-permute-start | bytes 1572872 | tf_op jit(solution)/shard_map/ppermute | solution.py:318
  61.5 2.4 %collective-permute-start.2 = (f32[8,16,8,128]{3,2,1,0:T(8,128)S(1)}, f32[8,16,8,128]{3,2,1,0:T(8,128)S(1)}, u32[]{:S(2)}, u32[]{:S(2)}) collective-permute-start(f32[8,16,8,128]{3,2,1,0:T(8,128)S(1)} %get-tuple-element.17.late_keep.keep), channel_id=1, source_target_pairs={{0,16},{1,17},{2,18},{3,19},{4,20},{5,21},{6,22},{7,23},{8,24},{9,... | collective-permute-start | bytes 1572872 | tf_op jit(solution)/shard_map/ppermute | solution.py:314
  64.0 0.0 collective-permute-done.4.other_partner
  64.0 0.0 copy-start.1
  64.0 1.0 copy-done.1
  65.0 2.8 %merge.1 = f32[8,2,16,8,128]{4,3,2,1,0:T(8,128)} custom-call(f32[2]{0:T(128)S(1)} %get-tuple-element.20.cos_ref, f32[2]{0:T(128)S(1)} %get-tuple-element.19.sin_ref, s32[1]{0:T(128)} %bitcast.3.lo_ref, f32[8,16,8,128]{3,2,1,0:T(8,128)S(1)} %get-tuple-element.12.keep, f32[8,16,8,128]{3,2,1,0:T(8,128)S(1)} %copy-done.1, ...), custom_call_target="tpu_custom_call" | custom-call | tf_op jit(solution)/shard_map/merge/pallas_call | solution.py:190
  67.8 3.6 %all-to-all-start.1 = ((f32[8,2,16,8,128]{4,3,2,1,0:T(8,128)}), f32[8,2,16,8,128]{4,3,2,1,0:T(8,128)S(1)}, u32[]{:S(2)}, u32[]{:S(2)}) async-start(f32[8,2,16,8,128]{4,3,2,1,0:T(8,128)} %merge.1), calls=%async_computation.1 | async-start | bytes 2097152 | tf_op jit(solution)/shard_map/all_to_all | solution.py:324
  71.4 17.7 %collective-permute-done.3.other = f32[8,16,8,128]{3,2,1,0:T(8,128)S(1)} collective-permute-done((f32[8,16,8,128]{3,2,1,0:T(8,128)}, f32[8,16,8,128]{3,2,1,0:T(8,128)S(1)}, u32[]{:S(2)}, u32[]{:S(2)}) %collective-permute-start.3) | collective-permute-done | bytes 524320 | tf_op jit(solution)/shard_map/ppermute | solution.py:318
  89.0 2.4 %collective-permute-start.5 = (f32[8,16,8,128]{3,2,1,0:T(8,128)S(1)}, f32[8,16,8,128]{3,2,1,0:T(8,128)S(1)}, u32[]{:S(2)}, u32[]{:S(2)}) collective-permute-start(f32[8,16,8,128]{3,2,1,0:T(8,128)S(1)} %collective-permute-done.3.other), channel_id=1, source_target_pairs={{0,16},{1,17},{2,18},{3,19},{4,20},{5,21},{6,22},{7,23},{8,24},{9,... | collective-permute-start | bytes 1572872 | tf_op jit(solution)/shard_map/ppermute | solution.py:314
  91.4 0.0 collective-permute-done.2.keep_partner
  91.4 14.3 %collective-permute-done.5.other_partner = f32[8,16,8,128]{3,2,1,0:T(8,128)S(1)} collective-permute-done((f32[8,16,8,128]{3,2,1,0:T(8,128)S(1)}, f32[8,16,8,128]{3,2,1,0:T(8,128)S(1)}, u32[]{:S(2)}, u32[]{:S(2)}) %collective-permute-start.5) | collective-permute-done | bytes 524320 | tf_op jit(solution)/shard_map/ppermute | solution.py:314
  105.7 2.3 %row_gate.2.rest_0_ = f32[128,4,8,128]{3,2,1,0:T(8,128)} custom-call(f32[2]{0:T(128)S(1)} %get-tuple-element.20.cos_ref, f32[2]{0:T(128)S(1)} %get-tuple-element.19.sin_ref, s32[1]{0:T(128)} %bitcast.3.lo_ref, bf16[128,384]{1,0:T(8,128)(2,1)S(1)} %hold.1.left, f32[8,16,8,128]{3,2,1,0:T(8,128)S(1)} %get-tuple-element.17.late_keep.keep, ...), custom_call_target="tpu_custom_call" | custom-call | tf_op jit(solution)/shard_map/row_gate/pallas_call | solution.py:299
  108.0 0.0 all-to-all-done.1.own
  108.0 1.6 %row_gate.3 = f32[128,4,8,128]{3,2,1,0:T(8,128)} custom-call(bf16[128,384]{1,0:T(8,128)(2,1)S(1)} %hold.1.left, f32[8,2,16,8,128]{4,3,2,1,0:T(8,128)S(1)} %all-to-all-done.1.own, f32[128,4,8,128]{3,2,1,0:T(8,128)} %row_gate.2.rest_0_), custom_call_target="tpu_custom_call", output_to_operand_aliasing={{}: (2, {})} | custom-call | tf_op jit(solution)/shard_map/row_gate/pallas_call | solution.py:299
  (2 shorter events, 0.1 us)
Async XLA Ops:
  0.0 0.7 copy-start.2
  5.2 30.0 %collective-permute-start.1 = (f32[8,16,8,128]{3,2,1,0:T(8,128)S(1)}, f32[8,16,8,128]{3,2,1,0:T(8,128)}, u32[]{:S(2)}, u32[]{:S(2)}) collective-permute-start(f32[8,16,8,128]{3,2,1,0:T(8,128)S(1)} %get-tuple-element.13), channel_id=1, source_target_pairs={{0,32},{32,0},{64,96},{96,64},{128,160},{160,128},{192,224},{224,1... | collective-permute-start | bytes 1572872 | tf_op jit(solution)/shard_map/ppermute | solution.py:318
  12.1 28.1 %collective-permute-start = (f32[8,16,8,128]{3,2,1,0:T(8,128)S(1)}, f32[8,16,8,128]{3,2,1,0:T(8,128)S(1)}, u32[]{:S(2)}, u32[]{:S(2)}) collective-permute-start(f32[8,16,8,128]{3,2,1,0:T(8,128)S(1)} %get-tuple-element.12.keep), channel_id=1, source_target_pairs={{0,16},{1,17},{2,18},{3,19},{4,20},{5,21},{6,22},{7,23},{8,24},{9,... | collective-permute-start | bytes 1572872 | tf_op jit(solution)/shard_map/ppermute | solution.py:314
  17.0 12.6 %copy-start.3 = (f32[2]{0:T(128)S(1)}, f32[2]{0:T(128)}, u32[]{:S(2)}) copy-start(f32[2]{0:T(128)} %param.6) | copy-start | bytes 28
  19.3 38.5 %all-to-all-start = ((f32[8,2,16,8,128]{4,3,2,1,0:T(8,128)}), f32[8,2,16,8,128]{4,3,2,1,0:T(8,128)S(1)}, u32[]{:S(2)}, u32[]{:S(2)}) async-start(f32[8,2,16,8,128]{4,3,2,1,0:T(8,128)} %late_gate.1), calls=%async_computation | async-start | bytes 2097152 | tf_op jit(solution)/shard_map/all_to_all | solution.py:324
  35.2 28.8 %collective-permute-start.4 = (f32[8,16,8,128]{3,2,1,0:T(8,128)}, f32[8,16,8,128]{3,2,1,0:T(8,128)}, u32[]{:S(2)}, u32[]{:S(2)}) collective-permute-start(f32[8,16,8,128]{3,2,1,0:T(8,128)} %collective-permute-done.1.other), channel_id=1, source_target_pairs={{0,16},{1,17},{2,18},{3,19},{4,20},{5,21},{6,22},{7,23},{8,24},{9,... | collective-permute-start | bytes 1572872 | tf_op jit(solution)/shard_map/ppermute | solution.py:314
  40.1 1.4 %copy-start = (f32[8,16,8,128]{3,2,1,0:T(8,128)}, f32[8,16,8,128]{3,2,1,0:T(8,128)S(1)}, u32[]{:S(2)}) copy-start(f32[8,16,8,128]{3,2,1,0:T(8,128)S(1)} %collective-permute-done.keep_partner) | copy-start | bytes 1572868
  58.6 30.4 %collective-permute-start.3 = (f32[8,16,8,128]{3,2,1,0:T(8,128)}, f32[8,16,8,128]{3,2,1,0:T(8,128)S(1)}, u32[]{:S(2)}, u32[]{:S(2)}) collective-permute-start(f32[8,16,8,128]{3,2,1,0:T(8,128)} %get-tuple-element.18), channel_id=1, source_target_pairs={{0,32},{32,0},{64,96},{96,64},{128,160},{160,128},{192,224},{224,1... | collective-permute-start | bytes 1572872 | tf_op jit(solution)/shard_map/ppermute | solution.py:318
  61.5 29.9 %collective-permute-start.2 = (f32[8,16,8,128]{3,2,1,0:T(8,128)S(1)}, f32[8,16,8,128]{3,2,1,0:T(8,128)S(1)}, u32[]{:S(2)}, u32[]{:S(2)}) collective-permute-start(f32[8,16,8,128]{3,2,1,0:T(8,128)S(1)} %get-tuple-element.17.late_keep.keep), channel_id=1, source_target_pairs={{0,16},{1,17},{2,18},{3,19},{4,20},{5,21},{6,22},{7,23},{8,24},{9,... | collective-permute-start | bytes 1572872 | tf_op jit(solution)/shard_map/ppermute | solution.py:314
  64.0 1.0 copy-start.1
  67.8 40.2 %all-to-all-start.1 = ((f32[8,2,16,8,128]{4,3,2,1,0:T(8,128)}), f32[8,2,16,8,128]{4,3,2,1,0:T(8,128)S(1)}, u32[]{:S(2)}, u32[]{:S(2)}) async-start(f32[8,2,16,8,128]{4,3,2,1,0:T(8,128)} %merge.1), calls=%async_computation.1 | async-start | bytes 2097152 | tf_op jit(solution)/shard_map/all_to_all | solution.py:324
  89.0 16.7 %collective-permute-start.5 = (f32[8,16,8,128]{3,2,1,0:T(8,128)S(1)}, f32[8,16,8,128]{3,2,1,0:T(8,128)S(1)}, u32[]{:S(2)}, u32[]{:S(2)}) collective-permute-start(f32[8,16,8,128]{3,2,1,0:T(8,128)S(1)} %collective-permute-done.3.other), channel_id=1, source_target_pairs={{0,16},{1,17},{2,18},{3,19},{4,20},{5,21},{6,22},{7,23},{8,24},{9,... | collective-permute-start | bytes 1572872 | tf_op jit(solution)/shard_map/ppermute | solution.py:314

commit v3 on v2

--- a/solution.py
+++ b/solution.py
@@ -155,20 +155,18 @@
 
 
 def late_kernel(upper_ref, lower_ref, left_ref, late_ref):
-    for i in range(STEP):
-        z = pl.program_id(0) * STEP + i
+    for z in range(8):
         result = gate_pair(left_ref, upper_ref[z], lower_ref[z])
         for s in range(2):
-            late_ref[i, s] = result[:, s * 128 : (s + 1) * 128].reshape(16, 8, 128)
+            late_ref[z, s] = result[:, s * 128 : (s + 1) * 128].reshape(16, 8, 128)
 
 
 def late_gate(upper, lower, left):
     return pl.pallas_call(
         late_kernel,
         out_shape=jax.ShapeDtypeStruct(BOTH, jnp.float32),
-        grid=(8 // STEP,),
         in_specs=[VMEM] * 3,
-        out_specs=pl.BlockSpec((STEP, 2, 16, 8, 128), lambda i: (i, 0, 0, 0, 0)),
+        out_specs=VMEM,
         compiler_params=pltpu.CompilerParams(vmem_limit_bytes=6 << 20),
         name="late_gate",
     )(on_chip(upper), on_chip(lower), on_chip(left))
@@ -181,19 +179,17 @@
 
 def merge_kernel(cos_ref, sin_ref, lo_ref, keep, keep_partner, other, other_partner, late_keep, out_ref):
     c, f = lo_turn(cos_ref, sin_ref, lo_ref)
-    part = pl.ds(pl.program_id(0) * STEP, STEP)
-    out_ref[:, 0] = c * keep[part] + f * keep_partner[part]
-    out_ref[:, 1] = c * other[part] + f * other_partner[part]
+    out_ref[:, 0] = c * keep[...] + f * keep_partner[...]
+    out_ref[:, 1] = c * other[...] + f * other_partner[...]
 
 
 def merge(turn, parts, late_keep):
     return pl.pallas_call(
         merge_kernel,
         out_shape=jax.ShapeDtypeStruct(BOTH, jnp.float32),
-        grid=(8 // STEP,),
         in_specs=[SMEM] * 3 + [VMEM] * 5,
-        out_specs=pl.BlockSpec((STEP, 2, 16, 8, 128), lambda i: (i, 0, 0, 0, 0)),
-        compiler_params=pltpu.CompilerParams(vmem_limit_bytes=6 << 20),
+        out_specs=VMEM,
+        compiler_params=pltpu.CompilerParams(vmem_limit_bytes=4 << 20),
         name="merge",
     )(*turn, *map(on_chip, parts), on_chip(late_keep))
 
@@ -214,7 +210,7 @@
     )(on_chip(value), on_chip(left))
 
 
-def matrix_kernel(cos_ref, sin_ref, hi_ref, g_ref, keep_partner, other, left_ref):
+def matrix_kernel(cos_ref, sin_ref, hi_ref, g_ref, other, left_ref):
     gate = g_ref[0]
     lane = lax.broadcasted_iota(jnp.int32, (128, 128), 1)
     upper = (lane >> 3 & 1) == 1
@@ -235,13 +231,13 @@
         grid=(1,),
         in_specs=[SMEM] * 3 + [pl.BlockSpec((1, 128, 128), lambda i: (2, 0, 0))] + [VMEM] * len(after),
         out_specs=VMEM,
-        cost_estimate=pl.CostEstimate(flops=10**11, transcendentals=0, bytes_accessed=10**5),
+        cost_estimate=pl.CostEstimate(flops=15 * 10**9, transcendentals=0, bytes_accessed=10**5),
         compiler_params=pltpu.CompilerParams(vmem_limit_bytes=2 << 20),
         name="row_matrix",
     )(cosines, sines, hi, off_chip(gates), *map(on_chip, after))
 
 
-def hold_kernel(in_ref, keep_partner, other, out_ref):
+def hold_kernel(in_ref, other, out_ref):
     out_ref[...] = in_ref[...]
 
 
@@ -252,7 +248,7 @@
         in_specs=[VMEM] * (1 + len(after)),
         out_specs=VMEM,
         compiler_params=pltpu.CompilerParams(vmem_limit_bytes=2 << 20),
-        cost_estimate=pl.CostEstimate(flops=10**11, transcendentals=0, bytes_accessed=10**5),
+        cost_estimate=pl.CostEstimate(flops=15 * 10**9, transcendentals=0, bytes_accessed=10**5),
         name="hold",
     )(*map(on_chip, (left, *after)))
 
@@ -334,15 +330,15 @@
     other = swap_hi(send)
     keep_partner = swap_lo(keep)
     late = remap(late_gate(upper, lower, late_left))
-    left = row_matrix(cosines, sines, hi, gates, keep_partner, other)
+    left = row_matrix(cosines, sines, hi, gates, other)
     early_parts = (keep, keep_partner, other, swap_lo(other))
     keep, send = cut(late, left)
     early = remap(merge(turn, early_parts, keep))
     other = swap_hi(send)
     keep_partner = swap_lo(keep)
-    left = hold(left, keep_partner, other)
-    result = row_gate(rows_turning, turn, left, (keep, keep_partner, other, swap_lo(other)), None, 2)
-    result = row_gate(rows_whole, (), left, (early,), result, 0)
+    left = hold(left, other)
+    result = row_gate(rows_whole, (), left, (early,), None, 0)
+    result = row_gate(rows_turning, turn, left, (keep, keep_partner, other, swap_lo(other)), result, 2)
     return result.reshape(amplitudes.shape)
 
 

time: 110 us -> 104 us (0.945)
  the two profiles are of different devices: /device:TPU:8 before, /device:TPU:10 now
where the time goes in v3:
time: 104 us
  waiting for transfers between devices  45.7 us (44%)
  starting transfers between devices  41.5 us (40%)
  Pallas kernels  15.5 us (15%)
    ppermute x2, waiting for transfers between devices, swap_hi(): lax.ppermute(value, 'hi', [(i, i ^ 1) for i in range(lax.axis_size('hi'))])  23 us
    ppermute x4, starting transfers between devices, swap_lo(): lax.ppermute(value, 'lo', [(i, i ^ count // 2) for i in range(count)])  16.1 us
    all_to_all x2, starting transfers between devices, remap(): lax.all_to_all(value, 'hi', split_axis=0, concat_axis=0, tiled=True, axis...  15.7 us
    all_to_all x2, waiting for transfers between devices, remap(): lax.all_to_all(value, 'hi', split_axis=0, concat_axis=0, tiled=True, axis...  14.2 us
    ppermute x2, starting transfers between devices, swap_hi(): lax.ppermute(value, 'hi', [(i, i ^ 1) for i in range(lax.axis_size('hi'))])  9.74 us
    ppermute x4, waiting for transfers between devices, swap_lo(): lax.ppermute(value, 'lo', [(i, i ^ count // 2) for i in range(count)])  8.42 us
    pallas_call x1, Pallas kernels, local_gates(): pl.pallas_call(local_kernel, out_shape=[pltpu.VMEM(ONE, jnp.float32), plt...  4.54 us
    pallas_call x2, Pallas kernels, row_gate(): pl.pallas_call(body, out_shape=jax.ShapeDtypeStruct((128, 4, 8, 128), jnp...  4.35 us
  transfers between devices with their start and end apart: 8, of which 5 were waited for; matrix products, arithmetic and copies ran while one was open for 0% of the time, Pallas kernels for 8%

profile of v3, /device:TPU:10, one launch (start us, length us, event | category | flops | bytes accessed | tf_op | source)
XLA Modules:
  0.0 103.5 jit_solution(2921443774304301832)
XLA Ops:
  0.0 0.0 copy-start
  0.0 0.7 copy-done
  0.7 4.5 %local_gates.1 = (f32[8,16,8,128]{3,2,1,0:T(8,128)S(1)}, f32[8,16,8,128]{3,2,1,0:T(8,128)S(1)}, bf16[8,256,256]{2,1,0:T(8,128)(2,1)S(1)}, bf16[8,256,256]{2,1,0:T(8,128)(2,1)S(1)}, bf16[2,128,256]{2,1,0:T(8,128)(2,1)S(1)}) custom-call(s32[2,24]{1,0:T(2,128)S(1)} %bitcast.5, s32[1]{0:T(128)} %bitcast.1.hi_ref, f32[8,2,2,128,128]{4,3,2,1,0:T(8,128)} %bitcast.6, ...), custom_call_target="tpu_custom_call" | custom-call | tf_op jit(solution)/shard_map/local_gates/pallas_call | solution.py:127
  5.2 6.8 %collective-permute-start = (f32[8,16,8,128]{3,2,1,0:T(8,128)S(1)}, f32[8,16,8,128]{3,2,1,0:T(8,128)S(1)}, u32[]{:S(2)}, u32[]{:S(2)}) collective-permute-start(f32[8,16,8,128]{3,2,1,0:T(8,128)S(1)} %get-tuple-element.12), channel_id=1, source_target_pairs={{0,32},{32,0},{64,96},{96,64},{128,160},{160,128},{192,224},{224,1... | collective-permute-start | bytes 1572872 | tf_op jit(solution)/shard_map/ppermute | solution.py:314
  12.1 0.0 copy-start.1
  12.1 1.6 %late_gate.1 = f32[8,2,16,8,128]{4,3,2,1,0:T(8,128)} custom-call(bf16[8,256,256]{2,1,0:T(8,128)(2,1)S(1)} %get-tuple-element.13.upper_ref, bf16[8,256,256]{2,1,0:T(8,128)(2,1)S(1)} %get-tuple-element.14.lower_ref, bf16[2,128,256]{2,1,0:T(8,128)(2,1)S(1)} %get-tuple-element.15.left_ref), custom_call_target="tpu_custom_call" | custom-call | tf_op jit(solution)/shard_map/late_gate/pallas_call | solution.py:165
  13.6 10.3 %all-to-all-start = ((f32[8,2,16,8,128]{4,3,2,1,0:T(8,128)}), f32[8,2,16,8,128]{4,3,2,1,0:T(8,128)S(1)}, u32[]{:S(2)}, u32[]{:S(2)}) async-start(f32[8,2,16,8,128]{4,3,2,1,0:T(8,128)} %late_gate.1), calls=%async_computation | async-start | bytes 2097152 | tf_op jit(solution)/shard_map/all_to_all | solution.py:320
  24.0 4.0 %collective-permute-start.4 = (f32[8,16,8,128]{3,2,1,0:T(8,128)S(1)}, f32[8,16,8,128]{3,2,1,0:T(8,128)S(1)}, u32[]{:S(2)}, u32[]{:S(2)}) collective-permute-start(f32[8,16,8,128]{3,2,1,0:T(8,128)S(1)} %get-tuple-element.18.keep), channel_id=1, source_target_pairs={{0,16},{1,17},{2,18},{3,19},{4,20},{5,21},{6,22},{7,23},{8,24},{9,... | collective-permute-start | bytes 1572872 | tf_op jit(solution)/shard_map/ppermute | solution.py:310
  28.0 0.0 copy-done.1
  28.0 7.0 %collective-permute-done.other = f32[8,16,8,128]{3,2,1,0:T(8,128)S(1)} collective-permute-done((f32[8,16,8,128]{3,2,1,0:T(8,128)S(1)}, f32[8,16,8,128]{3,2,1,0:T(8,128)S(1)}, u32[]{:S(2)}, u32[]{:S(2)}) %collective-permute-start) | collective-permute-done | bytes 524320 | tf_op jit(solution)/shard_map/ppermute | solution.py:314
  35.1 4.0 %collective-permute-start.5 = (f32[8,16,8,128]{3,2,1,0:T(8,128)S(1)}, f32[8,16,8,128]{3,2,1,0:T(8,128)}, u32[]{:S(2)}, u32[]{:S(2)}) collective-permute-start(f32[8,16,8,128]{3,2,1,0:T(8,128)S(1)} %collective-permute-done.other), channel_id=1, source_target_pairs={{0,16},{1,17},{2,18},{3,19},{4,20},{5,21},{6,22},{7,23},{8,24},{9,... | collective-permute-start | bytes 1572872 | tf_op jit(solution)/shard_map/ppermute | solution.py:310
  39.1 1.0 row_matrix.1.left_ref.in_ref
  40.1 12.3 %all-to-all-done.in_ref = f32[8,2,16,8,128]{4,3,2,1,0:T(8,128)S(1)} async-done(((f32[8,2,16,8,128]{4,3,2,1,0:T(8,128)}), f32[8,2,16,8,128]{4,3,2,1,0:T(8,128)S(1)}, u32[]{:S(2)}, u32[]{:S(2)}) %all-to-all-start) | async-done | bytes 1048608 | tf_op jit(solution)/shard_map/all_to_all | solution.py:320
  52.4 0.9 cut.1
  53.3 2.9 %collective-permute-start.1 = (f32[8,16,8,128]{3,2,1,0:T(8,128)}, f32[8,16,8,128]{3,2,1,0:T(8,128)}, u32[]{:S(2)}, u32[]{:S(2)}) collective-permute-start(f32[8,16,8,128]{3,2,1,0:T(8,128)} %get-tuple-element.16), channel_id=1, source_target_pairs={{0,32},{32,0},{64,96},{96,64},{128,160},{160,128},{192,224},{224,1... | collective-permute-start | bytes 1572872 | tf_op jit(solution)/shard_map/ppermute | solution.py:314
  56.2 0.0 collective-permute-done.4.keep_partner
  56.2 0.0 collective-permute-done.5.other_partner
  56.2 2.1 %merge.1 = f32[8,2,16,8,128]{4,3,2,1,0:T(8,128)} custom-call(f32[2]{0:T(128)S(1)} %get-tuple-element.20.cos_ref, f32[2]{0:T(128)S(1)} %get-tuple-element.19.sin_ref, s32[1]{0:T(128)} %bitcast.lo_ref, f32[8,16,8,128]{3,2,1,0:T(8,128)S(1)} %get-tuple-element.18.keep, f32[8,16,8,128]{3,2,1,0:T(8,128)S(1)} %collective-permute-done.4.keep_partner, ...), custom_call_target="tpu_custom_call" | custom-call | tf_op jit(solution)/shard_map/merge/pallas_call | solution.py:187
  58.3 5.4 %all-to-all-start.1 = ((f32[8,2,16,8,128]{4,3,2,1,0:T(8,128)}), f32[8,2,16,8,128]{4,3,2,1,0:T(8,128)S(1)}, u32[]{:S(2)}, u32[]{:S(2)}) async-start(f32[8,2,16,8,128]{4,3,2,1,0:T(8,128)} %merge.1), calls=%async_computation.1 | async-start | bytes 2097152 | tf_op jit(solution)/shard_map/all_to_all | solution.py:320
  63.8 4.0 %collective-permute-start.2 = (f32[8,16,8,128]{3,2,1,0:T(8,128)S(1)}, f32[8,16,8,128]{3,2,1,0:T(8,128)S(1)}, u32[]{:S(2)}, u32[]{:S(2)}) collective-permute-start(f32[8,16,8,128]{3,2,1,0:T(8,128)S(1)} %get-tuple-element.17.late_keep.keep), channel_id=1, source_target_pairs={{0,16},{1,17},{2,18},{3,19},{4,20},{5,21},{6,22},{7,23},{8,24},{9,... | collective-permute-start | bytes 1572872 | tf_op jit(solution)/shard_map/ppermute | solution.py:310
  67.8 16.0 %collective-permute-done.1.other = f32[8,16,8,128]{3,2,1,0:T(8,128)} collective-permute-done((f32[8,16,8,128]{3,2,1,0:T(8,128)}, f32[8,16,8,128]{3,2,1,0:T(8,128)}, u32[]{:S(2)}, u32[]{:S(2)}) %collective-permute-start.1) | collective-permute-done | bytes 524320 | tf_op jit(solution)/shard_map/ppermute | solution.py:314
  83.8 4.0 %collective-permute-start.3 = (f32[8,16,8,128]{3,2,1,0:T(8,128)}, f32[8,16,8,128]{3,2,1,0:T(8,128)S(1)}, u32[]{:S(2)}, u32[]{:S(2)}) collective-permute-start(f32[8,16,8,128]{3,2,1,0:T(8,128)} %collective-permute-done.1.other), channel_id=1, source_target_pairs={{0,16},{1,17},{2,18},{3,19},{4,20},{5,21},{6,22},{7,23},{8,24},{9,... | collective-permute-start | bytes 1572872 | tf_op jit(solution)/shard_map/ppermute | solution.py:310
  87.8 1.1 %hold.1.left = bf16[128,384]{1,0:T(8,128)(2,1)S(1)} custom-call(bf16[128,384]{1,0:T(8,128)(2,1)S(1)} %row_matrix.1.left_ref.in_ref, f32[8,16,8,128]{3,2,1,0:T(8,128)} %collective-permute-done.1.other), custom_call_target="tpu_custom_call" | custom-call | flops 15000000512 | bytes 100000 | tf_op jit(solution)/shard_map/hold/pallas_call | solution.py:245
  88.9 1.9 %all-to-all-done.1.own = f32[8,2,16,8,128]{4,3,2,1,0:T(8,128)S(1)} async-done(((f32[8,2,16,8,128]{4,3,2,1,0:T(8,128)}), f32[8,2,16,8,128]{4,3,2,1,0:T(8,128)S(1)}, u32[]{:S(2)}, u32[]{:S(2)}) %all-to-all-start.1) | async-done | bytes 1048608 | tf_op jit(solution)/shard_map/all_to_all | solution.py:320
  90.7 1.6 %row_gate.2.rest_0_ = f32[128,4,8,128]{3,2,1,0:T(8,128)} custom-call(bf16[128,384]{1,0:T(8,128)(2,1)S(1)} %hold.1.left, f32[8,2,16,8,128]{4,3,2,1,0:T(8,128)S(1)} %all-to-all-done.1.own), custom_call_target="tpu_custom_call" | custom-call | tf_op jit(solution)/shard_map/row_gate/pallas_call | solution.py:295
  92.3 0.0 collective-permute-done.2.keep_partner
  92.3 8.4 %collective-permute-done.3.other_partner = f32[8,16,8,128]{3,2,1,0:T(8,128)S(1)} collective-permute-done((f32[8,16,8,128]{3,2,1,0:T(8,128)}, f32[8,16,8,128]{3,2,1,0:T(8,128)S(1)}, u32[]{:S(2)}, u32[]{:S(2)}) %collective-permute-start.3) | collective-permute-done | bytes 524320 | tf_op jit(solution)/shard_map/ppermute | solution.py:310
  100.7 2.8 %row_gate.3 = f32[128,4,8,128]{3,2,1,0:T(8,128)} custom-call(f32[2]{0:T(128)S(1)} %get-tuple-element.20.cos_ref, f32[2]{0:T(128)S(1)} %get-tuple-element.19.sin_ref, s32[1]{0:T(128)} %bitcast.lo_ref, bf16[128,384]{1,0:T(8,128)(2,1)S(1)} %hold.1.left, f32[8,16,8,128]{3,2,1,0:T(8,128)S(1)} %get-tuple-element.17.late_keep.keep, ...), custom_call_target="tpu_custom_call", output_to_operand_aliasing={{}: (8, {})} | custom-call | tf_op jit(solution)/shard_map/row_gate/pallas_call | solution.py:295
  (1 shorter events, 0.0 us)
Async XLA Ops:
  0.0 0.7 copy-start
  5.2 29.8 %collective-permute-start = (f32[8,16,8,128]{3,2,1,0:T(8,128)S(1)}, f32[8,16,8,128]{3,2,1,0:T(8,128)S(1)}, u32[]{:S(2)}, u32[]{:S(2)}) collective-permute-start(f32[8,16,8,128]{3,2,1,0:T(8,128)S(1)} %get-tuple-element.12), channel_id=1, source_target_pairs={{0,32},{32,0},{64,96},{96,64},{128,160},{160,128},{192,224},{224,1... | collective-permute-start | bytes 1572872 | tf_op jit(solution)/shard_map/ppermute | solution.py:314
  12.1 15.9 %copy-start.1 = (f32[2]{0:T(128)S(1)}, f32[2]{0:T(128)}, u32[]{:S(2)}) copy-start(f32[2]{0:T(128)} %param.6) | copy-start | bytes 28
  13.6 38.8 %all-to-all-start = ((f32[8,2,16,8,128]{4,3,2,1,0:T(8,128)}), f32[8,2,16,8,128]{4,3,2,1,0:T(8,128)S(1)}, u32[]{:S(2)}, u32[]{:S(2)}) async-start(f32[8,2,16,8,128]{4,3,2,1,0:T(8,128)} %late_gate.1), calls=%async_computation | async-start | bytes 2097152 | tf_op jit(solution)/shard_map/all_to_all | solution.py:320
  24.0 32.2 %collective-permute-start.4 = (f32[8,16,8,128]{3,2,1,0:T(8,128)S(1)}, f32[8,16,8,128]{3,2,1,0:T(8,128)S(1)}, u32[]{:S(2)}, u32[]{:S(2)}) collective-permute-start(f32[8,16,8,128]{3,2,1,0:T(8,128)S(1)} %get-tuple-element.18.keep), channel_id=1, source_target_pairs={{0,16},{1,17},{2,18},{3,19},{4,20},{5,21},{6,22},{7,23},{8,24},{9,... | collective-permute-start | bytes 1572872 | tf_op jit(solution)/shard_map/ppermute | solution.py:310
  35.1 21.1 %collective-permute-start.5 = (f32[8,16,8,128]{3,2,1,0:T(8,128)S(1)}, f32[8,16,8,128]{3,2,1,0:T(8,128)}, u32[]{:S(2)}, u32[]{:S(2)}) collective-permute-start(f32[8,16,8,128]{3,2,1,0:T(8,128)S(1)} %collective-permute-done.other), channel_id=1, source_target_pairs={{0,16},{1,17},{2,18},{3,19},{4,20},{5,21},{6,22},{7,23},{8,24},{9,... | collective-permute-start | bytes 1572872 | tf_op jit(solution)/shard_map/ppermute | solution.py:310
  53.3 30.5 %collective-permute-start.1 = (f32[8,16,8,128]{3,2,1,0:T(8,128)}, f32[8,16,8,128]{3,2,1,0:T(8,128)}, u32[]{:S(2)}, u32[]{:S(2)}) collective-permute-start(f32[8,16,8,128]{3,2,1,0:T(8,128)} %get-tuple-element.16), channel_id=1, source_target_pairs={{0,32},{32,0},{64,96},{96,64},{128,160},{160,128},{192,224},{224,1... | collective-permute-start | bytes 1572872 | tf_op jit(solution)/shard_map/ppermute | solution.py:314
  58.3 32.4 %all-to-all-start.1 = ((f32[8,2,16,8,128]{4,3,2,1,0:T(8,128)}), f32[8,2,16,8,128]{4,3,2,1,0:T(8,128)S(1)}, u32[]{:S(2)}, u32[]{:S(2)}) async-start(f32[8,2,16,8,128]{4,3,2,1,0:T(8,128)} %merge.1), calls=%async_computation.1 | async-start | bytes 2097152 | tf_op jit(solution)/shard_map/all_to_all | solution.py:320
  63.8 28.5 %collective-permute-start.2 = (f32[8,16,8,128]{3,2,1,0:T(8,128)S(1)}, f32[8,16,8,128]{3,2,1,0:T(8,128)S(1)}, u32[]{:S(2)}, u32[]{:S(2)}) collective-permute-start(f32[8,16,8,128]{3,2,1,0:T(8,128)S(1)} %get-tuple-element.17.late_keep.keep), channel_id=1, source_target_pairs={{0,16},{1,17},{2,18},{3,19},{4,20},{5,21},{6,22},{7,23},{8,24},{9,... | collective-permute-start | bytes 1572872 | tf_op jit(solution)/shard_map/ppermute | solution.py:310
  83.8 16.9 %collective-permute-start.3 = (f32[8,16,8,128]{3,2,1,0:T(8,128)}, f32[8,16,8,128]{3,2,1,0:T(8,128)S(1)}, u32[]{:S(2)}, u32[]{:S(2)}) collective-permute-start(f32[8,16,8,128]{3,2,1,0:T(8,128)} %collective-permute-done.1.other), channel_id=1, source_target_pairs={{0,16},{1,17},{2,18},{3,19},{4,20},{5,21},{6,22},{7,23},{8,24},{9,... | collective-permute-start | bytes 1572872 | tf_op jit(solution)/shard_map/ppermute | solution.py:310

commit v4 on v3

--- a/solution.py
+++ b/solution.py
@@ -14,6 +14,7 @@
 ANY = pl.BlockSpec(memory_space=pl.ANY)
 BOTH = (8, 2, 16, 8, 128)
 ONE = (8, 16, 8, 128)
+PART = (8, 8, 8, 128)
 
 
 def split(value):
@@ -45,8 +46,8 @@
 
 
 def local_kernel(cz_ref, hi_ref, x_ref, g_ref, *rest):
-    keep_ref, send_ref, upper_ref, lower_ref, late_left_ref = rest[:5]
-    adj, masks, flips, low_sign, right0, left1 = rest[5:]
+    keep_ref, send1_ref, send2_ref, upper_ref, lower_ref, late_left_ref = rest[:6]
+    adj, masks, flips, low_sign, right0, left1 = rest[6:]
     step = pl.program_id(0)
     odd = hi_ref[0] & 1
 
@@ -119,7 +120,8 @@
         lower_ref[z] = lower
         result = gate_pair(left1, upper, lower)
         keep_ref[z] = result[:, 0:128].reshape(16, 8, 128)
-        send_ref[z] = result[:, 128:256].reshape(16, 8, 128)
+        send1_ref[z] = result[0:64, 128:256].reshape(8, 8, 128)
+        send2_ref[z] = result[64:128, 128:256].reshape(8, 8, 128)
 
 
 def local_gates(x, gates, cz_pairs, hi):
@@ -128,7 +130,8 @@
         local_kernel,
         out_shape=[
             pltpu.VMEM(ONE, jnp.float32),
-            pltpu.VMEM(ONE, jnp.float32),
+            pltpu.VMEM(PART, jnp.float32),
+            pltpu.VMEM(PART, jnp.float32),
             held,
             held,
             pltpu.VMEM((2, 128, 256), jnp.bfloat16),
@@ -140,7 +143,7 @@
             pl.BlockSpec((STEP, 2, 2, 128, 128), lambda i: (i, 0, 0, 0, 0)),
             pl.BlockSpec((3, 128, 128), lambda i: (0, 0, 0)),
         ],
-        out_specs=[VMEM] * 5,
+        out_specs=[VMEM] * 6,
         scratch_shapes=[
             pltpu.SMEM((QUBITS,), jnp.int32),
             pltpu.SMEM((1 << QU,), jnp.int32),
@@ -177,40 +180,68 @@
     return cos_ref[0], jnp.where((lo_ref[0] >> 4 & 1) == 1, sine, -sine)
 
 
-def merge_kernel(cos_ref, sin_ref, lo_ref, keep, keep_partner, other, other_partner, late_keep, out_ref):
+def turn_kernel(cos_ref, sin_ref, lo_ref, own_ref, partner_ref, out_ref):
+    c, f = lo_turn(cos_ref, sin_ref, lo_ref)
+    out_ref[...] = c * own_ref[...] + f * partner_ref[...]
+
+
+def turn_part(turn, own):
+    return pl.pallas_call(
+        turn_kernel,
+        out_shape=pltpu.VMEM(own.shape, own.dtype),
+        in_specs=[SMEM] * 3 + [VMEM] * 2,
+        out_specs=VMEM,
+        compiler_params=pltpu.CompilerParams(vmem_limit_bytes=2 << 20),
+        name="turn_part",
+    )(*turn, on_chip(own), on_chip(swap_lo(own)))
+
+
+def merge_kernel(cos_ref, sin_ref, lo_ref, keep, keep_partner, first, first_partner, second, *rest):
+    out_ref = rest[-1]
     c, f = lo_turn(cos_ref, sin_ref, lo_ref)
     out_ref[:, 0] = c * keep[...] + f * keep_partner[...]
-    out_ref[:, 1] = c * other[...] + f * other_partner[...]
-
-
-def merge(turn, parts, late_keep):
+    out_ref[:, 1, 0:8] = c * first[...] + f * first_partner[...]
+    out_ref[:, 1, 8:16] = second[...]
+
+
+def merge(turn, parts, after):
     return pl.pallas_call(
         merge_kernel,
         out_shape=jax.ShapeDtypeStruct(BOTH, jnp.float32),
-        in_specs=[SMEM] * 3 + [VMEM] * 5,
+        in_specs=[SMEM] * 3 + [VMEM] * (5 + len(after)),
         out_specs=VMEM,
         compiler_params=pltpu.CompilerParams(vmem_limit_bytes=4 << 20),
         name="merge",
-    )(*turn, *map(on_chip, parts), on_chip(late_keep))
-
-
-def cut_kernel(in_ref, left_ref, keep_ref, send_ref):
-    keep_ref[...] = in_ref[:, 0]
-    send_ref[...] = in_ref[:, 1]
-
-
-def cut(value, left):
+    )(*turn, *map(on_chip, (*parts, *after)))
+
+
+def cut_kernel(in_ref, *rest):
+    keep_ref, first_ref, second_ref, sems = rest[-4:]
+    copies = [
+        pltpu.make_async_copy(in_ref.at[:, 1, pl.ds(8, 8)], second_ref, sems.at[0]),
+        pltpu.make_async_copy(in_ref.at[:, 1, pl.ds(0, 8)], first_ref, sems.at[1]),
+        pltpu.make_async_copy(in_ref.at[:, 0], keep_ref, sems.at[2]),
+    ]
+    for copy in copies:
+        copy.start()
+    for copy in copies:
+        copy.wait()
+
+
+def cut(value, after):
     return pl.pallas_call(
         cut_kernel,
-        out_shape=[pltpu.VMEM(ONE, jnp.float32)] * 2,
-        in_specs=[VMEM, VMEM],
-        out_specs=[VMEM] * 2,
+        out_shape=[pltpu.VMEM(ONE, jnp.float32), pltpu.VMEM(PART, jnp.float32), pltpu.VMEM(PART, jnp.float32)],
+        in_specs=[ANY] + [VMEM] * len(after),
+        out_specs=[VMEM] * 3,
+        scratch_shapes=[pltpu.SemaphoreType.DMA((3,))],
         compiler_params=pltpu.CompilerParams(vmem_limit_bytes=4 << 20),
         name="cut",
-    )(on_chip(value), on_chip(left))
-
-
-def matrix_kernel(cos_ref, sin_ref, hi_ref, g_ref, other, left_ref):
+    )(off_chip(value), *map(on_chip, after))
+
+
+def matrix_kernel(cos_ref, sin_ref, hi_ref, g_ref, *rest):
+    left_ref = rest[-1]
     gate = g_ref[0]
     lane = lax.broadcasted_iota(jnp.int32, (128, 128), 1)
     upper = (lane >> 3 & 1) == 1
@@ -231,14 +262,14 @@
         grid=(1,),
         in_specs=[SMEM] * 3 + [pl.BlockSpec((1, 128, 128), lambda i: (2, 0, 0))] + [VMEM] * len(after),
         out_specs=VMEM,
-        cost_estimate=pl.CostEstimate(flops=15 * 10**9, transcendentals=0, bytes_accessed=10**5),
+        cost_estimate=pl.CostEstimate(flops=10**6, transcendentals=0, bytes_accessed=10**5),
         compiler_params=pltpu.CompilerParams(vmem_limit_bytes=2 << 20),
         name="row_matrix",
     )(cosines, sines, hi, off_chip(gates), *map(on_chip, after))
 
 
-def hold_kernel(in_ref, other, out_ref):
-    out_ref[...] = in_ref[...]
+def hold_kernel(in_ref, *rest):
+    rest[-1][...] = in_ref[...]
 
 
 def hold(left, *after):
@@ -248,7 +279,7 @@
         in_specs=[VMEM] * (1 + len(after)),
         out_specs=VMEM,
         compiler_params=pltpu.CompilerParams(vmem_limit_bytes=2 << 20),
-        cost_estimate=pl.CostEstimate(flops=15 * 10**9, transcendentals=0, bytes_accessed=10**5),
+        cost_estimate=pl.CostEstimate(flops=10**11, transcendentals=0, bytes_accessed=10**5),
         name="hold",
     )(*map(on_chip, (left, *after)))
 
@@ -274,14 +305,19 @@
     write_rows(left, [own[:, :, start + s].reshape(128, 128) for s in range(8)], right, lines, out_ref)
 
 
-def rows_turning(cos_ref, sin_ref, lo_ref, left, keep, keep_partner, other, other_partner, *rest):
+def rows_turning(cos_ref, sin_ref, lo_ref, left, keep, keep_partner, first, first_partner, second, *rest):
     out_ref, right, lines = rest[-3:]
     c, f = lo_turn(cos_ref, sin_ref, lo_ref)
-    start = pl.program_id(0) * 8
-    values = []
-    for s in [start + i for i in range(8)]:
-        values.append(joined(c * keep[:, s] + f * keep_partner[:, s], c * other[:, s] + f * other_partner[:, s]))
-    write_rows(left, values, right, lines, out_ref)
+    for group in range(2):
+
+        @pl.when(pl.program_id(0) == group)
+        def _():
+            values = []
+            for s in range(8):
+                j = group * 8 + s
+                other = second[:, s] if group else c * first[:, s] + f * first_partner[:, s]
+                values.append(joined(c * keep[:, j] + f * keep_partner[:, j], other))
+            write_rows(left, values, right, lines, out_ref)
 
 
 def row_gate(body, scalars, left, parts, base, group):
@@ -320,25 +356,30 @@
     return lax.all_to_all(value, "hi", split_axis=0, concat_axis=0, tiled=True, axis_index_groups=groups)
 
 
+def cross(turn, keep, first, second):
+    first_other = swap_hi(first)
+    second = turn_part(turn, second)
+    return (keep, swap_lo(keep), first_other, swap_lo(first_other), swap_hi(second)), second
+
+
 def per_device(amplitudes, gates, angles, cz_pairs):
     hi = lax.axis_index("hi").reshape(1)
     lo = lax.axis_index("lo").reshape(1)
     cosines = jnp.cos(angles * 0.5)
     sines = jnp.sin(angles * 0.5)
     turn = (cosines, sines, lo)
-    keep, send, upper, lower, late_left = local_gates(amplitudes.reshape(8, 2, 2, 128, 128), gates, cz_pairs, hi)
-    other = swap_hi(send)
-    keep_partner = swap_lo(keep)
+    keep, first, second, upper, lower, late_left = local_gates(
+        amplitudes.reshape(8, 2, 2, 128, 128), gates, cz_pairs, hi
+    )
     late = remap(late_gate(upper, lower, late_left))
-    left = row_matrix(cosines, sines, hi, gates, other)
-    early_parts = (keep, keep_partner, other, swap_lo(other))
-    keep, send = cut(late, left)
-    early = remap(merge(turn, early_parts, keep))
-    other = swap_hi(send)
-    keep_partner = swap_lo(keep)
-    left = hold(left, other)
-    result = row_gate(rows_whole, (), left, (early,), None, 0)
-    result = row_gate(rows_turning, turn, left, (keep, keep_partner, other, swap_lo(other)), result, 2)
+    early_parts, turned = cross(turn, keep, first, second)
+    left = row_matrix(cosines, sines, hi, gates)
+    late_keep, late_first, late_second = cut(late, (left, early_parts[3]))
+    early = remap(merge(turn, early_parts, (late_first,)))
+    late_parts, late_turned = cross(turn, late_keep, late_first, late_second)
+    left = hold(left, late_parts[2], late_turned)
+    result = row_gate(rows_turning, turn, left, late_parts, None, 2)
+    result = row_gate(rows_whole, (), left, (early,), result, 0)
     return result.reshape(amplitudes.shape)
 
 

time: 104 us -> 98 us (0.942)
  the two profiles are of different devices: /device:TPU:10 before, /device:TPU:56 now
where the time goes in v4:
time: 98 us; the launch traced here: 97.4 us
  starting transfers between devices  60.1 us (61%)
  waiting for transfers between devices  20.7 us (21%)
  Pallas kernels  15.6 us (16%)
    ppermute x6, starting transfers between devices, swap_lo(): lax.ppermute(value, 'lo', [(i, i ^ count // 2) for i in range(count)])  24.5 us
    ppermute x4, starting transfers between devices, swap_hi(): lax.ppermute(value, 'hi', [(i, i ^ 1) for i in range(lax.axis_size('hi'))])  18.3 us
    all_to_all x2, starting transfers between devices, remap(): lax.all_to_all(value, 'hi', split_axis=0, concat_axis=0, tiled=True, axis...  17.2 us
    ppermute x6, waiting for transfers between devices, swap_lo(): lax.ppermute(value, 'lo', [(i, i ^ count // 2) for i in range(count)])  9.46 us
    ppermute x4, waiting for transfers between devices, swap_hi(): lax.ppermute(value, 'hi', [(i, i ^ 1) for i in range(lax.axis_size('hi'))])  7.4 us
    pallas_call x1, Pallas kernels, local_gates(): pl.pallas_call(local_kernel, out_shape=[pltpu.VMEM(ONE, jnp.float32), plt...  4.54 us
    all_to_all x2, waiting for transfers between devices, remap(): lax.all_to_all(value, 'hi', split_axis=0, concat_axis=0, tiled=True, axis...  3.88 us
    pallas_call x2, Pallas kernels, row_gate(): pl.pallas_call(body, out_shape=jax.ShapeDtypeStruct((128, 4, 8, 128), jnp...  3.82 us
  transfers between devices with their start and end apart: 12, of which 5 were waited for; matrix products, arithmetic and copies ran while one was open for 0% of the time, Pallas kernels for 8%

profile of v4, /device:TPU:56, one launch (start us, length us, event | category | flops | bytes accessed | tf_op | source)
XLA Modules:
  0.0 97.4 jit_solution(6264659729393265574)
XLA Ops:
  0.0 0.0 copy-start
  0.0 0.7 copy-done
  0.7 4.5 %local_gates.1 = (f32[8,16,8,128]{3,2,1,0:T(8,128)S(1)}, f32[8,8,8,128]{3,2,1,0:T(8,128)S(1)}, f32[8,8,8,128]{3,2,1,0:T(8,128)S(1)}, bf16[8,256,256]{2,1,0:T(8,1...) custom-call(s32[2,24]{1,0:T(2,128)S(1)} %bitcast.5, s32[1]{0:T(128)} %bitcast.hi_ref, ...), custom_call_target="tpu_custom_call" | custom-call | tf_op jit(solution)/shard_map/local_gates/pallas_call | solution.py:129
  5.2 0.0 copy-start.1
  5.2 1.6 %late_gate.1 = f32[8,2,16,8,128]{4,3,2,1,0:T(8,128)} custom-call(bf16[8,256,256]{2,1,0:T(8,128)(2,1)S(1)} %get-tuple-element.14.upper_ref, bf16[8,256,256]{2,1,0:T(8,128)(2,1)S(1)} %get-tuple-element.15.lower_ref, bf16[2,128,256]{2,1,0:T(8,128)(2,1)S(1)} %get-tuple-element.16.left_ref), custom_call_target="tpu_custom_call" | custom-call | tf_op jit(solution)/shard_map/late_gate/pallas_call | solution.py:168
  6.8 10.3 %all-to-all-start = ((f32[8,2,16,8,128]{4,3,2,1,0:T(8,128)}), f32[8,2,16,8,128]{4,3,2,1,0:T(8,128)}, u32[]{:S(2)}, u32[]{:S(2)}) async-start(f32[8,2,16,8,128]{4,3,2,1,0:T(8,128)} %late_gate.1), calls=%async_computation | async-start | bytes 2097152 | tf_op jit(solution)/shard_map/all_to_all | solution.py:356
  17.1 4.7 %collective-permute-start = (f32[8,8,8,128]{3,2,1,0:T(8,128)S(1)}, f32[8,8,8,128]{3,2,1,0:T(8,128)S(1)}, u32[]{:S(2)}, u32[]{:S(2)}) collective-permute-start(f32[8,8,8,128]{3,2,1,0:T(8,128)S(1)} %get-tuple-element.17), channel_id=1, source_target_pairs={{0,32},{32,0},{64,96},{96,64},{128,160},{160,128},{192,224},{224,1... | collective-permute-start | bytes 786440 | tf_op jit(solution)/shard_map/ppermute | solution.py:350
  21.8 4.9 %collective-permute-start.5 = (f32[8,8,8,128]{3,2,1,0:T(8,128)S(1)}, f32[8,8,8,128]{3,2,1,0:T(8,128)S(1)}, u32[]{:S(2)}, u32[]{:S(2)}) collective-permute-start(f32[8,8,8,128]{3,2,1,0:T(8,128)S(1)} %get-tuple-element.21.own_ref), channel_id=1, source_target_pairs={{0,16},{1,17},{2,18},{3,19},{4,20},{5,21},{6,22},{7,23},{8,24},{9,... | collective-permute-start | bytes 786440 | tf_op jit(solution)/shard_map/ppermute | solution.py:346
  26.8 2.4 %collective-permute-start.4 = (f32[8,16,8,128]{3,2,1,0:T(8,128)S(1)}, f32[8,16,8,128]{3,2,1,0:T(8,128)S(1)}, u32[]{:S(2)}, u32[]{:S(2)}) collective-permute-start(f32[8,16,8,128]{3,2,1,0:T(8,128)S(1)} %get-tuple-element.20.keep), channel_id=1, source_target_pairs={{0,16},{1,17},{2,18},{3,19},{4,20},{5,21},{6,22},{7,23},{8,24},{9,... | collective-permute-start | bytes 1572872 | tf_op jit(solution)/shard_map/ppermute | solution.py:346
  29.2 7.1 %collective-permute-done.first = f32[8,8,8,128]{3,2,1,0:T(8,128)S(1)} collective-permute-done((f32[8,8,8,128]{3,2,1,0:T(8,128)S(1)}, f32[8,8,8,128]{3,2,1,0:T(8,128)S(1)}, u32[]{:S(2)}, u32[]{:S(2)}) %collective-permute-start) | collective-permute-done | bytes 262176 | tf_op jit(solution)/shard_map/ppermute | solution.py:350
  36.3 4.9 %collective-permute-start.1 = (f32[8,8,8,128]{3,2,1,0:T(8,128)S(1)}, f32[8,8,8,128]{3,2,1,0:T(8,128)S(1)}, u32[]{:S(2)}, u32[]{:S(2)}) collective-permute-start(f32[8,8,8,128]{3,2,1,0:T(8,128)S(1)} %collective-permute-done.first), channel_id=1, source_target_pairs={{0,16},{1,17},{2,18},{3,19},{4,20},{5,21},{6,22},{7,23},{8,24},{9,... | collective-permute-start | bytes 786440 | tf_op jit(solution)/shard_map/ppermute | solution.py:346
  41.3 0.0 copy-done.1
  41.3 1.0 row_matrix.1.rest_0_.in_ref
  42.3 0.0 collective-permute-done.5.partner_ref
  42.3 1.3 %turn_part.3 = f32[8,8,8,128]{3,2,1,0:T(8,128)} custom-call(f32[2]{0:T(128)S(1)} %get-tuple-element.24.cos_ref, f32[2]{0:T(128)S(1)} %get-tuple-element.23.sin_ref, s32[1]{0:T(128)} %bitcast.3.lo_ref, f32[8,8,8,128]{3,2,1,0:T(8,128)S(1)} %get-tuple-element.21.own_ref, f32[8,8,8,128]{3,2,1,0:T(8,128)S(1)} %collective-permute-done.5.partner_ref), custom_call_target="tpu_custom_call" | custom-call | tf_op jit(solution)/shard_map/turn_part/pallas_call | solution.py:189
  43.6 3.9 %collective-permute-start.6 = (f32[8,8,8,128]{3,2,1,0:T(8,128)}, f32[8,8,8,128]{3,2,1,0:T(8,128)S(1)}, u32[]{:S(2)}, u32[]{:S(2)}) collective-permute-start(f32[8,8,8,128]{3,2,1,0:T(8,128)} %turn_part.3), channel_id=1, source_target_pairs={{0,32},{32,0},{64,96},{96,64},{128,160},{160,128},{192,224},{224,1... | collective-permute-start | bytes 786440 | tf_op jit(solution)/shard_map/ppermute | solution.py:350
  47.5 2.1 %collective-permute-done.1.rest_1_.first_partner = f32[8,8,8,128]{3,2,1,0:T(8,128)S(1)} collective-permute-done((f32[8,8,8,128]{3,2,1,0:T(8,128)S(1)}, f32[8,8,8,128]{3,2,1,0:T(8,128)S(1)}, u32[]{:S(2)}, u32[]{:S(2)}) %collective-permute-start.1) | collective-permute-done | bytes 262176 | tf_op jit(solution)/shard_map/ppermute | solution.py:346
  49.6 0.0 all-to-all-done.in_ref
  49.6 1.2 %cut.1 = (f32[8,16,8,128]{3,2,1,0:T(8,128)S(1)}, f32[8,8,8,128]{3,2,1,0:T(8,128)S(1)}, f32[8,8,8,128]{3,2,1,0:T(8,128)S(1)}) custom-call(f32[8,2,16,8,128]{4,3,2,1,0:T(8,128)} %all-to-all-done.in_ref, bf16[128,384]{1,0:T(8,128)(2,1)S(1)} %row_matrix.1.rest_0_.in_ref, f32[8,8,8,128]{3,2,1,0:T(8,128)S(1)} %collective-permute-done.1.rest_1_.first_partner), custom_call_target="tpu_custom_call" | custom-call | tf_op jit(solution)/shard_map/cut/pallas_call | solution.py:232
  50.8 4.9 %collective-permute-start.3 = (f32[8,8,8,128]{3,2,1,0:T(8,128)S(1)}, f32[8,8,8,128]{3,2,1,0:T(8,128)S(1)}, u32[]{:S(2)}, u32[]{:S(2)}) collective-permute-start(f32[8,8,8,128]{3,2,1,0:T(8,128)S(1)} %get-tuple-element.19.own_ref), channel_id=1, source_target_pairs={{0,16},{1,17},{2,18},{3,19},{4,20},{5,21},{6,22},{7,23},{8,24},{9,... | collective-permute-start | bytes 786440 | tf_op jit(solution)/shard_map/ppermute | solution.py:346
  55.7 5.0 %collective-permute-start.2 = (f32[8,8,8,128]{3,2,1,0:T(8,128)S(1)}, f32[8,8,8,128]{3,2,1,0:T(8,128)S(1)}, u32[]{:S(2)}, u32[]{:S(2)}) collective-permute-start(f32[8,8,8,128]{3,2,1,0:T(8,128)S(1)} %get-tuple-element.18.rest_0_), channel_id=1, source_target_pairs={{0,32},{32,0},{64,96},{96,64},{128,160},{160,128},{192,224},{224,1... | collective-permute-start | bytes 786440 | tf_op jit(solution)/shard_map/ppermute | solution.py:350
  60.8 0.0 collective-permute-done.4.keep_partner
  60.8 0.0 collective-permute-done.6.second
  60.8 1.6 %merge.1 = f32[8,2,16,8,128]{4,3,2,1,0:T(8,128)} custom-call(f32[2]{0:T(128)S(1)} %get-tuple-element.24.cos_ref, f32[2]{0:T(128)S(1)} %get-tuple-element.23.sin_ref, s32[1]{0:T(128)} %bitcast.3.lo_ref, f32[8,16,8,128]{3,2,1,0:T(8,128)S(1)} %get-tuple-element.20.keep, f32[8,16,8,128]{3,2,1,0:T(8,128)S(1)} %collective-permute-done.4.keep_partner, ...), custom_call_target="tpu_custom_call" | custom-call | tf_op jit(solution)/shard_map/merge/pallas_call | solution.py:208
  62.4 6.9 %all-to-all-start.1 = ((f32[8,2,16,8,128]{4,3,2,1,0:T(8,128)}), f32[8,2,16,8,128]{4,3,2,1,0:T(8,128)S(1)}, u32[]{:S(2)}, u32[]{:S(2)}) async-start(f32[8,2,16,8,128]{4,3,2,1,0:T(8,128)} %merge.1), calls=%async_computation.1 | async-start | bytes 2097152 | tf_op jit(solution)/shard_map/all_to_all | solution.py:356
  69.4 2.4 %collective-permute-start.7 = (f32[8,16,8,128]{3,2,1,0:T(8,128)S(1)}, f32[8,16,8,128]{3,2,1,0:T(8,128)S(1)}, u32[]{:S(2)}, u32[]{:S(2)}) collective-permute-start(f32[8,16,8,128]{3,2,1,0:T(8,128)S(1)} %get-tuple-element.22.keep), channel_id=1, source_target_pairs={{0,16},{1,17},{2,18},{3,19},{4,20},{5,21},{6,22},{7,23},{8,24},{9,... | collective-permute-start | bytes 1572872 | tf_op jit(solution)/shard_map/ppermute | solution.py:346
  71.8 0.0 collective-permute-done.3.partner_ref
  71.8 0.6 turn_part.2.rest_1_
  72.4 4.7 %collective-permute-start.9 = (f32[8,8,8,128]{3,2,1,0:T(8,128)S(1)}, f32[8,8,8,128]{3,2,1,0:T(8,128)S(1)}, u32[]{:S(2)}, u32[]{:S(2)}) collective-permute-start(f32[8,8,8,128]{3,2,1,0:T(8,128)S(1)} %turn_part.2.rest_1_), channel_id=1, source_target_pairs={{0,32},{32,0},{64,96},{96,64},{128,160},{160,128},{192,224},{224,1... | collective-permute-start | bytes 786440 | tf_op jit(solution)/shard_map/ppermute | solution.py:350
  77.1 0.0 collective-permute-done.2.rest_0_.first
  77.1 4.9 %collective-permute-start.8 = (f32[8,8,8,128]{3,2,1,0:T(8,128)S(1)}, f32[8,8,8,128]{3,2,1,0:T(8,128)S(1)}, u32[]{:S(2)}, u32[]{:S(2)}) collective-permute-start(f32[8,8,8,128]{3,2,1,0:T(8,128)S(1)} %collective-permute-done.2.rest_0_.first), channel_id=1, source_target_pairs={{0,16},{1,17},{2,18},{3,19},{4,20},{5,21},{6,22},{7,23},{8,24},{9,... | collective-permute-start | bytes 786440 | tf_op jit(solution)/shard_map/ppermute | solution.py:346
  82.1 7.4 %collective-permute-done.8.first_partner = f32[8,8,8,128]{3,2,1,0:T(8,128)S(1)} collective-permute-done((f32[8,8,8,128]{3,2,1,0:T(8,128)S(1)}, f32[8,8,8,128]{3,2,1,0:T(8,128)S(1)}, u32[]{:S(2)}, u32[]{:S(2)}) %collective-permute-start.8) | collective-permute-done | bytes 262176 | tf_op jit(solution)/shard_map/ppermute | solution.py:346
  89.4 0.2 collective-permute-done.9.second
  89.7 0.0 collective-permute-done.7.keep_partner
  89.7 2.3 %row_gate.2.rest_0_ = f32[128,4,8,128]{3,2,1,0:T(8,128)} custom-call(f32[2]{0:T(128)S(1)} %get-tuple-element.24.cos_ref, f32[2]{0:T(128)S(1)} %get-tuple-element.23.sin_ref, s32[1]{0:T(128)} %bitcast.3.lo_ref, bf16[128,384]{1,0:T(8,128)(2,1)S(1)} %hold.1.left, f32[8,16,8,128]{3,2,1,0:T(8,128)S(1)} %get-tuple-element.22.keep, ...), custom_call_target="tpu_custom_call" | custom-call | tf_op jit(solution)/shard_map/row_gate/pallas_call | solution.py:331
  91.9 3.9 %all-to-all-done.1.own = f32[8,2,16,8,128]{4,3,2,1,0:T(8,128)S(1)} async-done(((f32[8,2,16,8,128]{4,3,2,1,0:T(8,128)}), f32[8,2,16,8,128]{4,3,2,1,0:T(8,128)S(1)}, u32[]{:S(2)}, u32[]{:S(2)}) %all-to-all-start.1) | async-done | bytes 1048608 | tf_op jit(solution)/shard_map/all_to_all | solution.py:356
  95.8 1.6 %row_gate.3 = f32[128,4,8,128]{3,2,1,0:T(8,128)} custom-call(bf16[128,384]{1,0:T(8,128)(2,1)S(1)} %hold.1.left, f32[8,2,16,8,128]{4,3,2,1,0:T(8,128)S(1)} %all-to-all-done.1.own, f32[128,4,8,128]{3,2,1,0:T(8,128)} %row_gate.2.rest_0_), custom_call_target="tpu_custom_call", output_to_operand_aliasing={{}: (2, {})} | custom-call | tf_op jit(solution)/shard_map/row_gate/pallas_call | solution.py:331
  (2 shorter events, 0.1 us)
Async XLA Ops:
  0.0 0.7 copy-start
  5.2 36.0 %copy-start.1 = (f32[2]{0:T(128)S(1)}, f32[2]{0:T(128)}, u32[]{:S(2)}) copy-start(f32[2]{0:T(128)} %param.6) | copy-start | bytes 28
  6.8 42.8 %all-to-all-start = ((f32[8,2,16,8,128]{4,3,2,1,0:T(8,128)}), f32[8,2,16,8,128]{4,3,2,1,0:T(8,128)}, u32[]{:S(2)}, u32[]{:S(2)}) async-start(f32[8,2,16,8,128]{4,3,2,1,0:T(8,128)} %late_gate.1), calls=%async_computation | async-start | bytes 2097152 | tf_op jit(solution)/shard_map/all_to_all | solution.py:356
  17.1 19.2 %collective-permute-start = (f32[8,8,8,128]{3,2,1,0:T(8,128)S(1)}, f32[8,8,8,128]{3,2,1,0:T(8,128)S(1)}, u32[]{:S(2)}, u32[]{:S(2)}) collective-permute-start(f32[8,8,8,128]{3,2,1,0:T(8,128)S(1)} %get-tuple-element.17), channel_id=1, source_target_pairs={{0,32},{32,0},{64,96},{96,64},{128,160},{160,128},{192,224},{224,1... | collective-permute-start | bytes 786440 | tf_op jit(solution)/shard_map/ppermute | solution.py:350
  21.8 20.5 %collective-permute-start.5 = (f32[8,8,8,128]{3,2,1,0:T(8,128)S(1)}, f32[8,8,8,128]{3,2,1,0:T(8,128)S(1)}, u32[]{:S(2)}, u32[]{:S(2)}) collective-permute-start(f32[8,8,8,128]{3,2,1,0:T(8,128)S(1)} %get-tuple-element.21.own_ref), channel_id=1, source_target_pairs={{0,16},{1,17},{2,18},{3,19},{4,20},{5,21},{6,22},{7,23},{8,24},{9,... | collective-permute-start | bytes 786440 | tf_op jit(solution)/shard_map/ppermute | solution.py:346
  26.8 34.0 %collective-permute-start.4 = (f32[8,16,8,128]{3,2,1,0:T(8,128)S(1)}, f32[8,16,8,128]{3,2,1,0:T(8,128)S(1)}, u32[]{:S(2)}, u32[]{:S(2)}) collective-permute-start(f32[8,16,8,128]{3,2,1,0:T(8,128)S(1)} %get-tuple-element.20.keep), channel_id=1, source_target_pairs={{0,16},{1,17},{2,18},{3,19},{4,20},{5,21},{6,22},{7,23},{8,24},{9,... | collective-permute-start | bytes 1572872 | tf_op jit(solution)/shard_map/ppermute | solution.py:346
  36.3 13.2 %collective-permute-start.1 = (f32[8,8,8,128]{3,2,1,0:T(8,128)S(1)}, f32[8,8,8,128]{3,2,1,0:T(8,128)S(1)}, u32[]{:S(2)}, u32[]{:S(2)}) collective-permute-start(f32[8,8,8,128]{3,2,1,0:T(8,128)S(1)} %collective-permute-done.first), channel_id=1, source_target_pairs={{0,16},{1,17},{2,18},{3,19},{4,20},{5,21},{6,22},{7,23},{8,24},{9,... | collective-permute-start | bytes 786440 | tf_op jit(solution)/shard_map/ppermute | solution.py:346
  43.6 17.2 %collective-permute-start.6 = (f32[8,8,8,128]{3,2,1,0:T(8,128)}, f32[8,8,8,128]{3,2,1,0:T(8,128)S(1)}, u32[]{:S(2)}, u32[]{:S(2)}) collective-permute-start(f32[8,8,8,128]{3,2,1,0:T(8,128)} %turn_part.3), channel_id=1, source_target_pairs={{0,32},{32,0},{64,96},{96,64},{128,160},{160,128},{192,224},{224,1... | collective-permute-start | bytes 786440 | tf_op jit(solution)/shard_map/ppermute | solution.py:350
  50.8 21.0 %collective-permute-start.3 = (f32[8,8,8,128]{3,2,1,0:T(8,128)S(1)}, f32[8,8,8,128]{3,2,1,0:T(8,128)S(1)}, u32[]{:S(2)}, u32[]{:S(2)}) collective-permute-start(f32[8,8,8,128]{3,2,1,0:T(8,128)S(1)} %get-tuple-element.19.own_ref), channel_id=1, source_target_pairs={{0,16},{1,17},{2,18},{3,19},{4,20},{5,21},{6,22},{7,23},{8,24},{9,... | collective-permute-start | bytes 786440 | tf_op jit(solution)/shard_map/ppermute | solution.py:346
  55.7 21.4 %collective-permute-start.2 = (f32[8,8,8,128]{3,2,1,0:T(8,128)S(1)}, f32[8,8,8,128]{3,2,1,0:T(8,128)S(1)}, u32[]{:S(2)}, u32[]{:S(2)}) collective-permute-start(f32[8,8,8,128]{3,2,1,0:T(8,128)S(1)} %get-tuple-element.18.rest_0_), channel_id=1, source_target_pairs={{0,32},{32,0},{64,96},{96,64},{128,160},{160,128},{192,224},{224,1... | collective-permute-start | bytes 786440 | tf_op jit(solution)/shard_map/ppermute | solution.py:350
  62.4 33.4 %all-to-all-start.1 = ((f32[8,2,16,8,128]{4,3,2,1,0:T(8,128)}), f32[8,2,16,8,128]{4,3,2,1,0:T(8,128)S(1)}, u32[]{:S(2)}, u32[]{:S(2)}) async-start(f32[8,2,16,8,128]{4,3,2,1,0:T(8,128)} %merge.1), calls=%async_computation.1 | async-start | bytes 2097152 | tf_op jit(solution)/shard_map/all_to_all | solution.py:356
  69.4 20.3 %collective-permute-start.7 = (f32[8,16,8,128]{3,2,1,0:T(8,128)S(1)}, f32[8,16,8,128]{3,2,1,0:T(8,128)S(1)}, u32[]{:S(2)}, u32[]{:S(2)}) collective-permute-start(f32[8,16,8,128]{3,2,1,0:T(8,128)S(1)} %get-tuple-element.22.keep), channel_id=1, source_target_pairs={{0,16},{1,17},{2,18},{3,19},{4,20},{5,21},{6,22},{7,23},{8,24},{9,... | collective-permute-start | bytes 1572872 | tf_op jit(solution)/shard_map/ppermute | solution.py:346
  72.4 17.3 %collective-permute-start.9 = (f32[8,8,8,128]{3,2,1,0:T(8,128)S(1)}, f32[8,8,8,128]{3,2,1,0:T(8,128)S(1)}, u32[]{:S(2)}, u32[]{:S(2)}) collective-permute-start(f32[8,8,8,128]{3,2,1,0:T(8,128)S(1)} %turn_part.2.rest_1_), channel_id=1, source_target_pairs={{0,32},{32,0},{64,96},{96,64},{128,160},{160,128},{192,224},{224,1... | collective-permute-start | bytes 786440 | tf_op jit(solution)/shard_map/ppermute | solution.py:350
  77.1 12.3 %collective-permute-start.8 = (f32[8,8,8,128]{3,2,1,0:T(8,128)S(1)}, f32[8,8,8,128]{3,2,1,0:T(8,128)S(1)}, u32[]{:S(2)}, u32[]{:S(2)}) collective-permute-start(f32[8,8,8,128]{3,2,1,0:T(8,128)S(1)} %collective-permute-done.2.rest_0_.first), channel_id=1, source_target_pairs={{0,16},{1,17},{2,18},{3,19},{4,20},{5,21},{6,22},{7,23},{8,24},{9,... | collective-permute-start | bytes 786440 | tf_op jit(solution)/shard_map/ppermute | solution.py:346

commit v5 on v4

--- a/solution.py
+++ b/solution.py
@@ -8,7 +8,7 @@
 QL = 14
 QU = 5
 QUBITS = QL + QU
-STEP = 2
+STEP = 4
 SMEM = pl.BlockSpec(memory_space=pltpu.SMEM)
 VMEM = pl.BlockSpec(memory_space=pltpu.VMEM)
 ANY = pl.BlockSpec(memory_space=pl.ANY)
@@ -46,8 +46,8 @@
 
 
 def local_kernel(cz_ref, hi_ref, x_ref, g_ref, *rest):
-    keep_ref, send1_ref, send2_ref, upper_ref, lower_ref, late_left_ref = rest[:6]
-    adj, masks, flips, low_sign, right0, left1 = rest[6:]
+    keep_ref, send1_ref, send2_ref, late_ref = rest[:4]
+    adj, masks, flips, low_sign, right0, left1 = rest[4:]
     step = pl.program_id(0)
     odd = hi_ref[0] & 1
 
@@ -88,10 +88,8 @@
             picked = mm(choose, part)
             one = jnp.where(first, picked, 0.0).astype(jnp.bfloat16)
             other = jnp.where(first, 0.0, picked).astype(jnp.bfloat16)
-            left1[i, :, 0:128] = one[0:128]
-            left1[i, :, 128:256] = other[0:128]
-            late_left_ref[i, :, 0:128] = one[128:256]
-            late_left_ref[i, :, 128:256] = other[128:256]
+            left1[i, :, 0:128] = one
+            left1[i, :, 128:256] = other
 
     small = lax.broadcasted_iota(jnp.int32, (8, 128), 0) * 128 + lax.broadcasted_iota(jnp.int32, (8, 128), 1)
     for local in range(STEP):
@@ -116,25 +114,22 @@
             lows.append(low)
         upper = jnp.concatenate(tops, 1)
         lower = jnp.concatenate(lows, 1)
-        upper_ref[z] = upper
-        lower_ref[z] = lower
         result = gate_pair(left1, upper, lower)
-        keep_ref[z] = result[:, 0:128].reshape(16, 8, 128)
+        keep_ref[z] = result[0:128, 0:128].reshape(16, 8, 128)
         send1_ref[z] = result[0:64, 128:256].reshape(8, 8, 128)
         send2_ref[z] = result[64:128, 128:256].reshape(8, 8, 128)
+        for s in range(2):
+            late_ref[local, s] = result[128:256, s * 128 : (s + 1) * 128].reshape(16, 8, 128)
 
 
 def local_gates(x, gates, cz_pairs, hi):
-    held = pltpu.VMEM((8, 256, 256), jnp.bfloat16)
     return pl.pallas_call(
         local_kernel,
         out_shape=[
             pltpu.VMEM(ONE, jnp.float32),
             pltpu.VMEM(PART, jnp.float32),
             pltpu.VMEM(PART, jnp.float32),
-            held,
-            held,
-            pltpu.VMEM((2, 128, 256), jnp.bfloat16),
+            jax.ShapeDtypeStruct(BOTH, jnp.float32),
         ],
         grid=(8 // STEP,),
         in_specs=[
@@ -143,36 +138,18 @@
             pl.BlockSpec((STEP, 2, 2, 128, 128), lambda i: (i, 0, 0, 0, 0)),
             pl.BlockSpec((3, 128, 128), lambda i: (0, 0, 0)),
         ],
-        out_specs=[VMEM] * 6,
+        out_specs=[VMEM] * 3 + [pl.BlockSpec((STEP, 2, 16, 8, 128), lambda i: (i, 0, 0, 0, 0))],
         scratch_shapes=[
             pltpu.SMEM((QUBITS,), jnp.int32),
             pltpu.SMEM((1 << QU,), jnp.int32),
             pltpu.SMEM((1 << QU,), jnp.int32),
             pltpu.VMEM((128, 128), jnp.float32),
             pltpu.VMEM((256, 256), jnp.bfloat16),
-            pltpu.VMEM((2, 128, 256), jnp.bfloat16),
+            pltpu.VMEM((2, 256, 256), jnp.bfloat16),
         ],
         compiler_params=pltpu.CompilerParams(vmem_limit_bytes=16 << 20),
         name="local_gates",
-    )(cz_pairs.T, hi, off_chip(x), off_chip(gates))
-
-
-def late_kernel(upper_ref, lower_ref, left_ref, late_ref):
-    for z in range(8):
-        result = gate_pair(left_ref, upper_ref[z], lower_ref[z])
-        for s in range(2):
-            late_ref[z, s] = result[:, s * 128 : (s + 1) * 128].reshape(16, 8, 128)
-
-
-def late_gate(upper, lower, left):
-    return pl.pallas_call(
-        late_kernel,
-        out_shape=jax.ShapeDtypeStruct(BOTH, jnp.float32),
-        in_specs=[VMEM] * 3,
-        out_specs=VMEM,
-        compiler_params=pltpu.CompilerParams(vmem_limit_bytes=6 << 20),
-        name="late_gate",
-    )(on_chip(upper), on_chip(lower), on_chip(left))
+    )(off_chip(cz_pairs.T), hi, off_chip(x), off_chip(gates))
 
 
 def lo_turn(cos_ref, sin_ref, lo_ref):
@@ -262,26 +239,10 @@
         grid=(1,),
         in_specs=[SMEM] * 3 + [pl.BlockSpec((1, 128, 128), lambda i: (2, 0, 0))] + [VMEM] * len(after),
         out_specs=VMEM,
-        cost_estimate=pl.CostEstimate(flops=10**6, transcendentals=0, bytes_accessed=10**5),
+        cost_estimate=pl.CostEstimate(flops=10**11, transcendentals=0, bytes_accessed=10**5),
         compiler_params=pltpu.CompilerParams(vmem_limit_bytes=2 << 20),
         name="row_matrix",
     )(cosines, sines, hi, off_chip(gates), *map(on_chip, after))
-
-
-def hold_kernel(in_ref, *rest):
-    rest[-1][...] = in_ref[...]
-
-
-def hold(left, *after):
-    return pl.pallas_call(
-        hold_kernel,
-        out_shape=pltpu.VMEM(left.shape, left.dtype),
-        in_specs=[VMEM] * (1 + len(after)),
-        out_specs=VMEM,
-        compiler_params=pltpu.CompilerParams(vmem_limit_bytes=2 << 20),
-        cost_estimate=pl.CostEstimate(flops=10**11, transcendentals=0, bytes_accessed=10**5),
-        name="hold",
-    )(*map(on_chip, (left, *after)))
 
 
 def write_rows(left, values, right, lines, out_ref):
@@ -368,16 +329,15 @@
     cosines = jnp.cos(angles * 0.5)
     sines = jnp.sin(angles * 0.5)
     turn = (cosines, sines, lo)
-    keep, first, second, upper, lower, late_left = local_gates(
+    keep, first, second, late = local_gates(
         amplitudes.reshape(8, 2, 2, 128, 128), gates, cz_pairs, hi
     )
-    late = remap(late_gate(upper, lower, late_left))
+    late = remap(late)
     early_parts, turned = cross(turn, keep, first, second)
-    left = row_matrix(cosines, sines, hi, gates)
-    late_keep, late_first, late_second = cut(late, (left, early_parts[3]))
+    late_keep, late_first, late_second = cut(late, (early_parts[3],))
     early = remap(merge(turn, early_parts, (late_first,)))
     late_parts, late_turned = cross(turn, late_keep, late_first, late_second)
-    left = hold(left, late_parts[2], late_turned)
+    left = row_matrix(cosines, sines, hi, gates, late_parts[2], late_turned)
     result = row_gate(rows_turning, turn, left, late_parts, None, 2)
     result = row_gate(rows_whole, (), left, (early,), result, 0)
     return result.reshape(amplitudes.shape)

time: 98 us -> 95.9 us (0.979)
  Pallas kernels: 15.6 us -> 14.3 us
    pallas_call x2 -> x0, Pallas kernels: 1.57 us -> none  [the longest x1 1.56 us: late_gate(): pl.pallas_call(late_kernel, out_shape=jax.ShapeDtypeStruct(BOTH, jnp.floa...]
where the time goes in v5:
time: 95.9 us; the launch traced here: 95.4 us
  starting transfers between devices  60.1 us (63%)
  waiting for transfers between devices  20.7 us (22%)
  Pallas kernels  14.3 us (15%)
    ppermute x6, starting transfers between devices, swap_lo(): lax.ppermute(value, 'lo', [(i, i ^ count // 2) for i in range(count)])  24.5 us
    ppermute x4, starting transfers between devices, swap_hi(): lax.ppermute(value, 'hi', [(i, i ^ 1) for i in range(lax.axis_size('hi'))])  18.4 us
    all_to_all x2, starting transfers between devices, remap(): lax.all_to_all(value, 'hi', split_axis=0, concat_axis=0, tiled=True, axis...  17.2 us
    ppermute x6, waiting for transfers between devices, swap_lo(): lax.ppermute(value, 'lo', [(i, i ^ count // 2) for i in range(count)])  9.45 us
    ppermute x4, waiting for transfers between devices, swap_hi(): lax.ppermute(value, 'hi', [(i, i ^ 1) for i in range(lax.axis_size('hi'))])  7.4 us
    pallas_call x1, Pallas kernels, local_gates(): pl.pallas_call(local_kernel, out_shape=[pltpu.VMEM(ONE, jnp.float32), plt...  4.78 us
    all_to_all x2, waiting for transfers between devices, remap(): lax.all_to_all(value, 'hi', split_axis=0, concat_axis=0, tiled=True, axis...  3.89 us
    pallas_call x2, Pallas kernels, row_gate(): pl.pallas_call(body, out_shape=jax.ShapeDtypeStruct((128, 4, 8, 128), jnp...  3.82 us
  transfers between devices with their start and end apart: 12, of which 5 were waited for; matrix products, arithmetic and copies ran while one was open for 0% of the time, Pallas kernels for 8%

profile of v5, /device:TPU:56, one launch (start us, length us, event | category | flops | bytes accessed | tf_op | source)
XLA Modules:
  0.0 95.4 jit_solution(17402102116050545770)
XLA Ops:
  0.0 0.0 copy-start
  0.0 4.8 %local_gates.1 = (f32[8,16,8,128]{3,2,1,0:T(8,128)S(1)}, f32[8,8,8,128]{3,2,1,0:T(8,128)S(1)}, f32[8,8,8,128]{3,2,1,0:T(8,128)S(1)}, f32[8,2,16,8,128]{4,3,2,1,0:T(8,128)}) custom-call(s32[2,24]{1,0:T(2,128)} %bitcast.6, s32[1]{0:T(128)} %bitcast.hi_ref, f32[8,2,2,128,128]{4,3,2,1,0:T(8,128)} %bitcast.5, f32[3,128,128]{2,1,0:T(8,128)} %g_ref.3), custom_call_target="tpu_custom_call" | custom-call | tf_op jit(solution)/shard_map/local_gates/pallas_call | solution.py:126
  4.8 10.3 %all-to-all-start = ((f32[8,2,16,8,128]{4,3,2,1,0:T(8,128)}), f32[8,2,16,8,128]{4,3,2,1,0:T(8,128)}, u32[]{:S(2)}, u32[]{:S(2)}) async-start(f32[8,2,16,8,128]{4,3,2,1,0:T(8,128)} %get-tuple-element.12), calls=%async_computation | async-start | bytes 2097152 | tf_op jit(solution)/shard_map/all_to_all | solution.py:317
  15.1 4.7 %collective-permute-start = (f32[8,8,8,128]{3,2,1,0:T(8,128)S(1)}, f32[8,8,8,128]{3,2,1,0:T(8,128)S(1)}, u32[]{:S(2)}, u32[]{:S(2)}) collective-permute-start(f32[8,8,8,128]{3,2,1,0:T(8,128)S(1)} %get-tuple-element.13), channel_id=1, source_target_pairs={{0,32},{32,0},{64,96},{96,64},{128,160},{160,128},{192,224},{224,1... | collective-permute-start | bytes 786440 | tf_op jit(solution)/shard_map/ppermute | solution.py:311
  19.8 4.9 %collective-permute-start.5 = (f32[8,8,8,128]{3,2,1,0:T(8,128)S(1)}, f32[8,8,8,128]{3,2,1,0:T(8,128)S(1)}, u32[]{:S(2)}, u32[]{:S(2)}) collective-permute-start(f32[8,8,8,128]{3,2,1,0:T(8,128)S(1)} %get-tuple-element.17.own_ref), channel_id=1, source_target_pairs={{0,16},{1,17},{2,18},{3,19},{4,20},{5,21},{6,22},{7,23},{8,24},{9,... | collective-permute-start | bytes 786440 | tf_op jit(solution)/shard_map/ppermute | solution.py:307
  24.7 2.4 %collective-permute-start.4 = (f32[8,16,8,128]{3,2,1,0:T(8,128)S(1)}, f32[8,16,8,128]{3,2,1,0:T(8,128)S(1)}, u32[]{:S(2)}, u32[]{:S(2)}) collective-permute-start(f32[8,16,8,128]{3,2,1,0:T(8,128)S(1)} %get-tuple-element.16.keep), channel_id=1, source_target_pairs={{0,16},{1,17},{2,18},{3,19},{4,20},{5,21},{6,22},{7,23},{8,24},{9,... | collective-permute-start | bytes 1572872 | tf_op jit(solution)/shard_map/ppermute | solution.py:307
  27.2 7.1 %collective-permute-done.first = f32[8,8,8,128]{3,2,1,0:T(8,128)S(1)} collective-permute-done((f32[8,8,8,128]{3,2,1,0:T(8,128)S(1)}, f32[8,8,8,128]{3,2,1,0:T(8,128)S(1)}, u32[]{:S(2)}, u32[]{:S(2)}) %collective-permute-start) | collective-permute-done | bytes 262176 | tf_op jit(solution)/shard_map/ppermute | solution.py:311
  34.3 4.9 %collective-permute-start.1 = (f32[8,8,8,128]{3,2,1,0:T(8,128)S(1)}, f32[8,8,8,128]{3,2,1,0:T(8,128)S(1)}, u32[]{:S(2)}, u32[]{:S(2)}) collective-permute-start(f32[8,8,8,128]{3,2,1,0:T(8,128)S(1)} %collective-permute-done.first), channel_id=1, source_target_pairs={{0,16},{1,17},{2,18},{3,19},{4,20},{5,21},{6,22},{7,23},{8,24},{9,... | collective-permute-start | bytes 786440 | tf_op jit(solution)/shard_map/ppermute | solution.py:307
  39.2 0.0 copy-done
  39.3 0.0 collective-permute-done.5.partner_ref
  39.3 1.3 %turn_part.3 = f32[8,8,8,128]{3,2,1,0:T(8,128)} custom-call(f32[2]{0:T(128)S(1)} %get-tuple-element.20.cos_ref, f32[2]{0:T(128)S(1)} %get-tuple-element.19.sin_ref, s32[1]{0:T(128)} %bitcast.3.lo_ref, f32[8,8,8,128]{3,2,1,0:T(8,128)S(1)} %get-tuple-element.17.own_ref, f32[8,8,8,128]{3,2,1,0:T(8,128)S(1)} %collective-permute-done.5.partner_ref), custom_call_target="tpu_custom_call" | custom-call | tf_op jit(solution)/shard_map/turn_part/pallas_call | solution.py:166
  40.6 3.9 %collective-permute-start.6 = (f32[8,8,8,128]{3,2,1,0:T(8,128)}, f32[8,8,8,128]{3,2,1,0:T(8,128)S(1)}, u32[]{:S(2)}, u32[]{:S(2)}) collective-permute-start(f32[8,8,8,128]{3,2,1,0:T(8,128)} %turn_part.3), channel_id=1, source_target_pairs={{0,32},{32,0},{64,96},{96,64},{128,160},{160,128},{192,224},{224,1... | collective-permute-start | bytes 786440 | tf_op jit(solution)/shard_map/ppermute | solution.py:311
  44.5 3.0 %collective-permute-done.1.rest_0_.first_partner = f32[8,8,8,128]{3,2,1,0:T(8,128)S(1)} collective-permute-done((f32[8,8,8,128]{3,2,1,0:T(8,128)S(1)}, f32[8,8,8,128]{3,2,1,0:T(8,128)S(1)}, u32[]{:S(2)}, u32[]{:S(2)}) %collective-permute-start.1) | collective-permute-done | bytes 262176 | tf_op jit(solution)/shard_map/ppermute | solution.py:307
  47.5 0.0 all-to-all-done.in_ref
  47.5 1.2 %cut.1 = (f32[8,16,8,128]{3,2,1,0:T(8,128)S(1)}, f32[8,8,8,128]{3,2,1,0:T(8,128)S(1)}, f32[8,8,8,128]{3,2,1,0:T(8,128)S(1)}) custom-call(f32[8,2,16,8,128]{4,3,2,1,0:T(8,128)} %all-to-all-done.in_ref, f32[8,8,8,128]{3,2,1,0:T(8,128)S(1)} %collective-permute-done.1.rest_0_.first_partner), custom_call_target="tpu_custom_call" | custom-call | tf_op jit(solution)/shard_map/cut/pallas_call | solution.py:209
  48.8 4.9 %collective-permute-start.3 = (f32[8,8,8,128]{3,2,1,0:T(8,128)S(1)}, f32[8,8,8,128]{3,2,1,0:T(8,128)S(1)}, u32[]{:S(2)}, u32[]{:S(2)}) collective-permute-start(f32[8,8,8,128]{3,2,1,0:T(8,128)S(1)} %get-tuple-element.15.own_ref), channel_id=1, source_target_pairs={{0,16},{1,17},{2,18},{3,19},{4,20},{5,21},{6,22},{7,23},{8,24},{9,... | collective-permute-start | bytes 786440 | tf_op jit(solution)/shard_map/ppermute | solution.py:307
  53.7 5.0 %collective-permute-start.2 = (f32[8,8,8,128]{3,2,1,0:T(8,128)S(1)}, f32[8,8,8,128]{3,2,1,0:T(8,128)S(1)}, u32[]{:S(2)}, u32[]{:S(2)}) collective-permute-start(f32[8,8,8,128]{3,2,1,0:T(8,128)S(1)} %get-tuple-element.14.rest_0_), channel_id=1, source_target_pairs={{0,32},{32,0},{64,96},{96,64},{128,160},{160,128},{192,224},{224,1... | collective-permute-start | bytes 786440 | tf_op jit(solution)/shard_map/ppermute | solution.py:311
  58.8 0.0 collective-permute-done.4.keep_partner
  58.8 0.0 collective-permute-done.6.second
  58.8 1.6 %merge.1 = f32[8,2,16,8,128]{4,3,2,1,0:T(8,128)} custom-call(f32[2]{0:T(128)S(1)} %get-tuple-element.20.cos_ref, f32[2]{0:T(128)S(1)} %get-tuple-element.19.sin_ref, s32[1]{0:T(128)} %bitcast.3.lo_ref, f32[8,16,8,128]{3,2,1,0:T(8,128)S(1)} %get-tuple-element.16.keep, f32[8,16,8,128]{3,2,1,0:T(8,128)S(1)} %collective-permute-done.4.keep_partner, ...), custom_call_target="tpu_custom_call" | custom-call | tf_op jit(solution)/shard_map/merge/pallas_call | solution.py:185
  60.4 6.9 %all-to-all-start.1 = ((f32[8,2,16,8,128]{4,3,2,1,0:T(8,128)}), f32[8,2,16,8,128]{4,3,2,1,0:T(8,128)S(1)}, u32[]{:S(2)}, u32[]{:S(2)}) async-start(f32[8,2,16,8,128]{4,3,2,1,0:T(8,128)} %merge.1), calls=%async_computation.1 | async-start | bytes 2097152 | tf_op jit(solution)/shard_map/all_to_all | solution.py:317
  67.4 2.4 %collective-permute-start.7 = (f32[8,16,8,128]{3,2,1,0:T(8,128)S(1)}, f32[8,16,8,128]{3,2,1,0:T(8,128)S(1)}, u32[]{:S(2)}, u32[]{:S(2)}) collective-permute-start(f32[8,16,8,128]{3,2,1,0:T(8,128)S(1)} %get-tuple-element.18.keep), channel_id=1, source_target_pairs={{0,16},{1,17},{2,18},{3,19},{4,20},{5,21},{6,22},{7,23},{8,24},{9,... | collective-permute-start | bytes 1572872 | tf_op jit(solution)/shard_map/ppermute | solution.py:307
  69.8 0.0 collective-permute-done.3.partner_ref
  69.8 0.6 turn_part.2.rest_1_
  70.4 4.7 %collective-permute-start.9 = (f32[8,8,8,128]{3,2,1,0:T(8,128)S(1)}, f32[8,8,8,128]{3,2,1,0:T(8,128)S(1)}, u32[]{:S(2)}, u32[]{:S(2)}) collective-permute-start(f32[8,8,8,128]{3,2,1,0:T(8,128)S(1)} %turn_part.2.rest_1_), channel_id=1, source_target_pairs={{0,32},{32,0},{64,96},{96,64},{128,160},{160,128},{192,224},{224,1... | collective-permute-start | bytes 786440 | tf_op jit(solution)/shard_map/ppermute | solution.py:311
  75.1 0.0 collective-permute-done.2.rest_0_.first
  75.1 4.9 %collective-permute-start.8 = (f32[8,8,8,128]{3,2,1,0:T(8,128)S(1)}, f32[8,8,8,128]{3,2,1,0:T(8,128)S(1)}, u32[]{:S(2)}, u32[]{:S(2)}) collective-permute-start(f32[8,8,8,128]{3,2,1,0:T(8,128)S(1)} %collective-permute-done.2.rest_0_.first), channel_id=1, source_target_pairs={{0,16},{1,17},{2,18},{3,19},{4,20},{5,21},{6,22},{7,23},{8,24},{9,... | collective-permute-start | bytes 786440 | tf_op jit(solution)/shard_map/ppermute | solution.py:307
  80.0 1.0 %row_matrix.1.left = bf16[128,384]{1,0:T(8,128)(2,1)S(1)} custom-call(f32[2]{0:T(128)S(1)} %get-tuple-element.20.cos_ref, f32[2]{0:T(128)S(1)} %get-tuple-element.19.sin_ref, s32[1]{0:T(128)} %bitcast.hi_ref, f32[3,128,128]{2,1,0:T(8,128)} %g_ref.3, f32[8,8,8,128]{3,2,1,0:T(8,128)S(1)} %collective-permute-done.2.rest_0_.first, ...), custom_call_target="tpu_custom_call" | custom-call | flops 99999997952 | bytes 100000 | tf_op jit(solution)/shard_map/row_matrix/pallas_call | solution.py:236
  81.0 6.4 %collective-permute-done.8.first_partner = f32[8,8,8,128]{3,2,1,0:T(8,128)S(1)} collective-permute-done((f32[8,8,8,128]{3,2,1,0:T(8,128)S(1)}, f32[8,8,8,128]{3,2,1,0:T(8,128)S(1)}, u32[]{:S(2)}, u32[]{:S(2)}) %collective-permute-start.8) | collective-permute-done | bytes 262176 | tf_op jit(solution)/shard_map/ppermute | solution.py:307
  87.4 0.2 collective-permute-done.9.second
  87.7 0.0 collective-permute-done.7.keep_partner
  87.7 2.3 %row_gate.2.rest_0_ = f32[128,4,8,128]{3,2,1,0:T(8,128)} custom-call(f32[2]{0:T(128)S(1)} %get-tuple-element.20.cos_ref, f32[2]{0:T(128)S(1)} %get-tuple-element.19.sin_ref, s32[1]{0:T(128)} %bitcast.3.lo_ref, bf16[128,384]{1,0:T(8,128)(2,1)S(1)} %row_matrix.1.left, f32[8,16,8,128]{3,2,1,0:T(8,128)S(1)} %get-tuple-element.18.keep, ...), custom_call_target="tpu_custom_call" | custom-call | tf_op jit(solution)/shard_map/row_gate/pallas_call | solution.py:292
  89.9 3.9 %all-to-all-done.1.own = f32[8,2,16,8,128]{4,3,2,1,0:T(8,128)S(1)} async-done(((f32[8,2,16,8,128]{4,3,2,1,0:T(8,128)}), f32[8,2,16,8,128]{4,3,2,1,0:T(8,128)S(1)}, u32[]{:S(2)}, u32[]{:S(2)}) %all-to-all-start.1) | async-done | bytes 1048608 | tf_op jit(solution)/shard_map/all_to_all | solution.py:317
  93.8 1.6 %row_gate.3 = f32[128,4,8,128]{3,2,1,0:T(8,128)} custom-call(bf16[128,384]{1,0:T(8,128)(2,1)S(1)} %row_matrix.1.left, f32[8,2,16,8,128]{4,3,2,1,0:T(8,128)S(1)} %all-to-all-done.1.own, f32[128,4,8,128]{3,2,1,0:T(8,128)} %row_gate.2.rest_0_), custom_call_target="tpu_custom_call", output_to_operand_aliasing={{}: (2, {})} | custom-call | tf_op jit(solution)/shard_map/row_gate/pallas_call | solution.py:292
  (1 shorter events, 0.0 us)
Async XLA Ops:
  0.0 39.3 %copy-start = (f32[2]{0:T(128)S(1)}, f32[2]{0:T(128)}, u32[]{:S(2)}) copy-start(f32[2]{0:T(128)} %param.6) | copy-start | bytes 28
  4.8 42.8 %all-to-all-start = ((f32[8,2,16,8,128]{4,3,2,1,0:T(8,128)}), f32[8,2,16,8,128]{4,3,2,1,0:T(8,128)}, u32[]{:S(2)}, u32[]{:S(2)}) async-start(f32[8,2,16,8,128]{4,3,2,1,0:T(8,128)} %get-tuple-element.12), calls=%async_computation | async-start | bytes 2097152 | tf_op jit(solution)/shard_map/all_to_all | solution.py:317
  15.1 19.2 %collective-permute-start = (f32[8,8,8,128]{3,2,1,0:T(8,128)S(1)}, f32[8,8,8,128]{3,2,1,0:T(8,128)S(1)}, u32[]{:S(2)}, u32[]{:S(2)}) collective-permute-start(f32[8,8,8,128]{3,2,1,0:T(8,128)S(1)} %get-tuple-element.13), channel_id=1, source_target_pairs={{0,32},{32,0},{64,96},{96,64},{128,160},{160,128},{192,224},{224,1... | collective-permute-start | bytes 786440 | tf_op jit(solution)/shard_map/ppermute | solution.py:311
  19.8 19.5 %collective-permute-start.5 = (f32[8,8,8,128]{3,2,1,0:T(8,128)S(1)}, f32[8,8,8,128]{3,2,1,0:T(8,128)S(1)}, u32[]{:S(2)}, u32[]{:S(2)}) collective-permute-start(f32[8,8,8,128]{3,2,1,0:T(8,128)S(1)} %get-tuple-element.17.own_ref), channel_id=1, source_target_pairs={{0,16},{1,17},{2,18},{3,19},{4,20},{5,21},{6,22},{7,23},{8,24},{9,... | collective-permute-start | bytes 786440 | tf_op jit(solution)/shard_map/ppermute | solution.py:307
  24.7 34.0 %collective-permute-start.4 = (f32[8,16,8,128]{3,2,1,0:T(8,128)S(1)}, f32[8,16,8,128]{3,2,1,0:T(8,128)S(1)}, u32[]{:S(2)}, u32[]{:S(2)}) collective-permute-start(f32[8,16,8,128]{3,2,1,0:T(8,128)S(1)} %get-tuple-element.16.keep), channel_id=1, source_target_pairs={{0,16},{1,17},{2,18},{3,19},{4,20},{5,21},{6,22},{7,23},{8,24},{9,... | collective-permute-start | bytes 1572872 | tf_op jit(solution)/shard_map/ppermute | solution.py:307
  34.3 13.2 %collective-permute-start.1 = (f32[8,8,8,128]{3,2,1,0:T(8,128)S(1)}, f32[8,8,8,128]{3,2,1,0:T(8,128)S(1)}, u32[]{:S(2)}, u32[]{:S(2)}) collective-permute-start(f32[8,8,8,128]{3,2,1,0:T(8,128)S(1)} %collective-permute-done.first), channel_id=1, source_target_pairs={{0,16},{1,17},{2,18},{3,19},{4,20},{5,21},{6,22},{7,23},{8,24},{9,... | collective-permute-start | bytes 786440 | tf_op jit(solution)/shard_map/ppermute | solution.py:307
  40.6 18.2 %collective-permute-start.6 = (f32[8,8,8,128]{3,2,1,0:T(8,128)}, f32[8,8,8,128]{3,2,1,0:T(8,128)S(1)}, u32[]{:S(2)}, u32[]{:S(2)}) collective-permute-start(f32[8,8,8,128]{3,2,1,0:T(8,128)} %turn_part.3), channel_id=1, source_target_pairs={{0,32},{32,0},{64,96},{96,64},{128,160},{160,128},{192,224},{224,1... | collective-permute-start | bytes 786440 | tf_op jit(solution)/shard_map/ppermute | solution.py:311
  48.8 21.0 %collective-permute-start.3 = (f32[8,8,8,128]{3,2,1,0:T(8,128)S(1)}, f32[8,8,8,128]{3,2,1,0:T(8,128)S(1)}, u32[]{:S(2)}, u32[]{:S(2)}) collective-permute-start(f32[8,8,8,128]{3,2,1,0:T(8,128)S(1)} %get-tuple-element.15.own_ref), channel_id=1, source_target_pairs={{0,16},{1,17},{2,18},{3,19},{4,20},{5,21},{6,22},{7,23},{8,24},{9,... | collective-permute-start | bytes 786440 | tf_op jit(solution)/shard_map/ppermute | solution.py:307
  53.7 21.4 %collective-permute-start.2 = (f32[8,8,8,128]{3,2,1,0:T(8,128)S(1)}, f32[8,8,8,128]{3,2,1,0:T(8,128)S(1)}, u32[]{:S(2)}, u32[]{:S(2)}) collective-permute-start(f32[8,8,8,128]{3,2,1,0:T(8,128)S(1)} %get-tuple-element.14.rest_0_), channel_id=1, source_target_pairs={{0,32},{32,0},{64,96},{96,64},{128,160},{160,128},{192,224},{224,1... | collective-permute-start | bytes 786440 | tf_op jit(solution)/shard_map/ppermute | solution.py:311
  60.4 33.4 %all-to-all-start.1 = ((f32[8,2,16,8,128]{4,3,2,1,0:T(8,128)}), f32[8,2,16,8,128]{4,3,2,1,0:T(8,128)S(1)}, u32[]{:S(2)}, u32[]{:S(2)}) async-start(f32[8,2,16,8,128]{4,3,2,1,0:T(8,128)} %merge.1), calls=%async_computation.1 | async-start | bytes 2097152 | tf_op jit(solution)/shard_map/all_to_all | solution.py:317
  67.4 20.3 %collective-permute-start.7 = (f32[8,16,8,128]{3,2,1,0:T(8,128)S(1)}, f32[8,16,8,128]{3,2,1,0:T(8,128)S(1)}, u32[]{:S(2)}, u32[]{:S(2)}) collective-permute-start(f32[8,16,8,128]{3,2,1,0:T(8,128)S(1)} %get-tuple-element.18.keep), channel_id=1, source_target_pairs={{0,16},{1,17},{2,18},{3,19},{4,20},{5,21},{6,22},{7,23},{8,24},{9,... | collective-permute-start | bytes 1572872 | tf_op jit(solution)/shard_map/ppermute | solution.py:307
  70.4 17.3 %collective-permute-start.9 = (f32[8,8,8,128]{3,2,1,0:T(8,128)S(1)}, f32[8,8,8,128]{3,2,1,0:T(8,128)S(1)}, u32[]{:S(2)}, u32[]{:S(2)}) collective-permute-start(f32[8,8,8,128]{3,2,1,0:T(8,128)S(1)} %turn_part.2.rest_1_), channel_id=1, source_target_pairs={{0,32},{32,0},{64,96},{96,64},{128,160},{160,128},{192,224},{224,1... | collective-permute-start | bytes 786440 | tf_op jit(solution)/shard_map/ppermute | solution.py:311
  75.1 12.3 %collective-permute-start.8 = (f32[8,8,8,128]{3,2,1,0:T(8,128)S(1)}, f32[8,8,8,128]{3,2,1,0:T(8,128)S(1)}, u32[]{:S(2)}, u32[]{:S(2)}) collective-permute-start(f32[8,8,8,128]{3,2,1,0:T(8,128)S(1)} %collective-permute-done.2.rest_0_.first), channel_id=1, source_target_pairs={{0,16},{1,17},{2,18},{3,19},{4,20},{5,21},{6,22},{7,23},{8,24},{9,... | collective-permute-start | bytes 786440 | tf_op jit(solution)/shard_map/ppermute | solution.py:307

commit v6 on v5

--- a/solution.py
+++ b/solution.py
@@ -253,7 +253,7 @@
     result = mm(left[:, 0:256], right[...]) + mm(left[:, 256:384], right[0:128, :])
     for s in range(8):
         lines[pl.ds(s, 128, stride=8), :] = result[:, s * 128 : (s + 1) * 128]
-    out_ref[...] = lines[...].reshape(128, 1, 8, 128)
+    out_ref[...] = lines[0:1024].reshape(128, 1, 8, 128)
 
 
 def joined(keep, other):
@@ -295,7 +295,7 @@
         grid=(2,),
         in_specs=specs,
         out_specs=pl.BlockSpec((128, 1, 8, 128), lambda i: (0, group + i, 0, 0)),
-        scratch_shapes=[pltpu.VMEM((256, 1024), jnp.bfloat16), pltpu.VMEM((1024, 128), jnp.float32)],
+        scratch_shapes=[pltpu.VMEM((256, 1024), jnp.bfloat16), pltpu.VMEM((1040, 128), jnp.float32)],
         input_output_aliases=aliases,
         compiler_params=pltpu.CompilerParams(vmem_limit_bytes=8 << 20),
         name="row_gate",
@@ -334,7 +334,7 @@
     )
     late = remap(late)
     early_parts, turned = cross(turn, keep, first, second)
-    late_keep, late_first, late_second = cut(late, (early_parts[3],))
+    late_keep, late_first, late_second = cut(late, (early_parts[3], turned))
     early = remap(merge(turn, early_parts, (late_first,)))
     late_parts, late_turned = cross(turn, late_keep, late_first, late_second)
     left = row_matrix(cosines, sines, hi, gates, late_parts[2], late_turned)

time: 95.9 us -> 96 us (level)
  no operation moved by 1% of the time
where the time goes in v6:
time: 96 us; the launch traced here: 95.4 us
  starting transfers between devices  60.1 us (63%)
  waiting for transfers between devices  21 us (22%)
  Pallas kernels  14 us (15%)
    ppermute x6, starting transfers between devices, swap_lo(): lax.ppermute(value, 'lo', [(i, i ^ count // 2) for i in range(count)])  24.5 us
    ppermute x4, starting transfers between devices, swap_hi(): lax.ppermute(value, 'hi', [(i, i ^ 1) for i in range(lax.axis_size('hi'))])  18.4 us
    all_to_all x2, starting transfers between devices, remap(): lax.all_to_all(value, 'hi', split_axis=0, concat_axis=0, tiled=True, axis...  17.2 us
    ppermute x6, waiting for transfers between devices, swap_lo(): lax.ppermute(value, 'lo', [(i, i ^ count // 2) for i in range(count)])  9.73 us
    ppermute x4, waiting for transfers between devices, swap_hi(): lax.ppermute(value, 'hi', [(i, i ^ 1) for i in range(lax.axis_size('hi'))])  7.82 us
    pallas_call x1, Pallas kernels, local_gates(): pl.pallas_call(local_kernel, out_shape=[pltpu.VMEM(ONE, jnp.float32), plt...  4.78 us
    pallas_call x2, Pallas kernels, row_gate(): pl.pallas_call(body, out_shape=jax.ShapeDtypeStruct((128, 4, 8, 128), jnp...  3.82 us
    all_to_all x2, waiting for transfers between devices, remap(): lax.all_to_all(value, 'hi', split_axis=0, concat_axis=0, tiled=True, axis...  3.46 us
  transfers between devices with their start and end apart: 12, of which 5 were waited for; matrix products, arithmetic and copies ran while one was open for 0% of the time, Pallas kernels for 8%

profile of v6, /device:TPU:56, one launch (start us, length us, event | category | flops | bytes accessed | tf_op | source)
XLA Modules:
  0.0 95.4 jit_solution(10720751331800135652)
XLA Ops:
  0.0 0.0 copy-start
  0.0 4.8 %local_gates.1 = (f32[8,16,8,128]{3,2,1,0:T(8,128)S(1)}, f32[8,8,8,128]{3,2,1,0:T(8,128)S(1)}, f32[8,8,8,128]{3,2,1,0:T(8,128)S(1)}, f32[8,2,16,8,128]{4,3,2,1,0:T(8,128)}) custom-call(s32[2,24]{1,0:T(2,128)} %bitcast.6, s32[1]{0:T(128)} %bitcast.hi_ref, f32[8,2,2,128,128]{4,3,2,1,0:T(8,128)} %bitcast.5, f32[3,128,128]{2,1,0:T(8,128)} %g_ref.3), custom_call_target="tpu_custom_call" | custom-call | tf_op jit(solution)/shard_map/local_gates/pallas_call | solution.py:126
  4.8 10.3 %all-to-all-start = ((f32[8,2,16,8,128]{4,3,2,1,0:T(8,128)}), f32[8,2,16,8,128]{4,3,2,1,0:T(8,128)}, u32[]{:S(2)}, u32[]{:S(2)}) async-start(f32[8,2,16,8,128]{4,3,2,1,0:T(8,128)} %get-tuple-element.12), calls=%async_computation | async-start | bytes 2097152 | tf_op jit(solution)/shard_map/all_to_all | solution.py:317
  15.1 4.7 %collective-permute-start = (f32[8,8,8,128]{3,2,1,0:T(8,128)S(1)}, f32[8,8,8,128]{3,2,1,0:T(8,128)S(1)}, u32[]{:S(2)}, u32[]{:S(2)}) collective-permute-start(f32[8,8,8,128]{3,2,1,0:T(8,128)S(1)} %get-tuple-element.13), channel_id=1, source_target_pairs={{0,32},{32,0},{64,96},{96,64},{128,160},{160,128},{192,224},{224,1... | collective-permute-start | bytes 786440 | tf_op jit(solution)/shard_map/ppermute | solution.py:311
  19.8 4.9 %collective-permute-start.2 = (f32[8,8,8,128]{3,2,1,0:T(8,128)S(1)}, f32[8,8,8,128]{3,2,1,0:T(8,128)S(1)}, u32[]{:S(2)}, u32[]{:S(2)}) collective-permute-start(f32[8,8,8,128]{3,2,1,0:T(8,128)S(1)} %get-tuple-element.14.own_ref), channel_id=1, source_target_pairs={{0,16},{1,17},{2,18},{3,19},{4,20},{5,21},{6,22},{7,23},{8,24},{9,... | collective-permute-start | bytes 786440 | tf_op jit(solution)/shard_map/ppermute | solution.py:307
  24.7 2.4 %collective-permute-start.5 = (f32[8,16,8,128]{3,2,1,0:T(8,128)S(1)}, f32[8,16,8,128]{3,2,1,0:T(8,128)S(1)}, u32[]{:S(2)}, u32[]{:S(2)}) collective-permute-start(f32[8,16,8,128]{3,2,1,0:T(8,128)S(1)} %get-tuple-element.17.keep), channel_id=1, source_target_pairs={{0,16},{1,17},{2,18},{3,19},{4,20},{5,21},{6,22},{7,23},{8,24},{9,... | collective-permute-start | bytes 1572872 | tf_op jit(solution)/shard_map/ppermute | solution.py:307
  27.2 7.1 %collective-permute-done.first = f32[8,8,8,128]{3,2,1,0:T(8,128)S(1)} collective-permute-done((f32[8,8,8,128]{3,2,1,0:T(8,128)S(1)}, f32[8,8,8,128]{3,2,1,0:T(8,128)S(1)}, u32[]{:S(2)}, u32[]{:S(2)}) %collective-permute-start) | collective-permute-done | bytes 262176 | tf_op jit(solution)/shard_map/ppermute | solution.py:311
  34.3 4.9 %collective-permute-start.1 = (f32[8,8,8,128]{3,2,1,0:T(8,128)S(1)}, f32[8,8,8,128]{3,2,1,0:T(8,128)S(1)}, u32[]{:S(2)}, u32[]{:S(2)}) collective-permute-start(f32[8,8,8,128]{3,2,1,0:T(8,128)S(1)} %collective-permute-done.first), channel_id=1, source_target_pairs={{0,16},{1,17},{2,18},{3,19},{4,20},{5,21},{6,22},{7,23},{8,24},{9,... | collective-permute-start | bytes 786440 | tf_op jit(solution)/shard_map/ppermute | solution.py:307
  39.2 0.0 copy-done
  39.3 0.0 collective-permute-done.2.partner_ref
  39.3 0.6 turn_part.2.rest_1_
  39.9 3.9 %collective-permute-start.6 = (f32[8,8,8,128]{3,2,1,0:T(8,128)S(1)}, f32[8,8,8,128]{3,2,1,0:T(8,128)S(1)}, u32[]{:S(2)}, u32[]{:S(2)}) collective-permute-start(f32[8,8,8,128]{3,2,1,0:T(8,128)S(1)} %turn_part.2.rest_1_), channel_id=1, source_target_pairs={{0,32},{32,0},{64,96},{96,64},{128,160},{160,128},{192,224},{224,1... | collective-permute-start | bytes 786440 | tf_op jit(solution)/shard_map/ppermute | solution.py:311
  43.8 3.7 %collective-permute-done.1.rest_0_.first_partner = f32[8,8,8,128]{3,2,1,0:T(8,128)S(1)} collective-permute-done((f32[8,8,8,128]{3,2,1,0:T(8,128)S(1)}, f32[8,8,8,128]{3,2,1,0:T(8,128)S(1)}, u32[]{:S(2)}, u32[]{:S(2)}) %collective-permute-start.1) | collective-permute-done | bytes 262176 | tf_op jit(solution)/shard_map/ppermute | solution.py:307
  47.5 0.0 all-to-all-done.in_ref
  47.5 1.2 %cut.1 = (f32[8,16,8,128]{3,2,1,0:T(8,128)S(1)}, f32[8,8,8,128]{3,2,1,0:T(8,128)S(1)}, f32[8,8,8,128]{3,2,1,0:T(8,128)S(1)}) custom-call(f32[8,2,16,8,128]{4,3,2,1,0:T(8,128)} %all-to-all-done.in_ref, f32[8,8,8,128]{3,2,1,0:T(8,128)S(1)} %collective-permute-done.1.rest_0_.first_partner, f32[8,8,8,128]{3,2,1,0:T(8,128)S(1)} %turn_part.2.rest_1_), custom_call_target="tpu_custom_call" | custom-call | tf_op jit(solution)/shard_map/cut/pallas_call | solution.py:209
  48.8 4.9 %collective-permute-start.4 = (f32[8,8,8,128]{3,2,1,0:T(8,128)S(1)}, f32[8,8,8,128]{3,2,1,0:T(8,128)}, u32[]{:S(2)}, u32[]{:S(2)}) collective-permute-start(f32[8,8,8,128]{3,2,1,0:T(8,128)S(1)} %get-tuple-element.16.own_ref), channel_id=1, source_target_pairs={{0,16},{1,17},{2,18},{3,19},{4,20},{5,21},{6,22},{7,23},{8,24},{9,... | collective-permute-start | bytes 786440 | tf_op jit(solution)/shard_map/ppermute | solution.py:307
  53.7 5.0 %collective-permute-start.3 = (f32[8,8,8,128]{3,2,1,0:T(8,128)S(1)}, f32[8,8,8,128]{3,2,1,0:T(8,128)S(1)}, u32[]{:S(2)}, u32[]{:S(2)}) collective-permute-start(f32[8,8,8,128]{3,2,1,0:T(8,128)S(1)} %get-tuple-element.15.rest_0_), channel_id=1, source_target_pairs={{0,32},{32,0},{64,96},{96,64},{128,160},{160,128},{192,224},{224,1... | collective-permute-start | bytes 786440 | tf_op jit(solution)/shard_map/ppermute | solution.py:311
  58.8 0.0 collective-permute-done.5.keep_partner
  58.8 0.0 collective-permute-done.6.second
  58.8 1.6 %merge.1 = f32[8,2,16,8,128]{4,3,2,1,0:T(8,128)} custom-call(f32[2]{0:T(128)S(1)} %get-tuple-element.20.cos_ref, f32[2]{0:T(128)S(1)} %get-tuple-element.19.sin_ref, s32[1]{0:T(128)} %bitcast.3.lo_ref, f32[8,16,8,128]{3,2,1,0:T(8,128)S(1)} %get-tuple-element.17.keep, f32[8,16,8,128]{3,2,1,0:T(8,128)S(1)} %collective-permute-done.5.keep_partner, ...), custom_call_target="tpu_custom_call" | custom-call | tf_op jit(solution)/shard_map/merge/pallas_call | solution.py:185
  60.4 6.9 %all-to-all-start.1 = ((f32[8,2,16,8,128]{4,3,2,1,0:T(8,128)}), f32[8,2,16,8,128]{4,3,2,1,0:T(8,128)S(1)}, u32[]{:S(2)}, u32[]{:S(2)}) async-start(f32[8,2,16,8,128]{4,3,2,1,0:T(8,128)} %merge.1), calls=%async_computation.1 | async-start | bytes 2097152 | tf_op jit(solution)/shard_map/all_to_all | solution.py:317
  67.4 2.4 %collective-permute-start.7 = (f32[8,16,8,128]{3,2,1,0:T(8,128)S(1)}, f32[8,16,8,128]{3,2,1,0:T(8,128)S(1)}, u32[]{:S(2)}, u32[]{:S(2)}) collective-permute-start(f32[8,16,8,128]{3,2,1,0:T(8,128)S(1)} %get-tuple-element.18.keep), channel_id=1, source_target_pairs={{0,16},{1,17},{2,18},{3,19},{4,20},{5,21},{6,22},{7,23},{8,24},{9,... | collective-permute-start | bytes 1572872 | tf_op jit(solution)/shard_map/ppermute | solution.py:307
  69.8 0.0 collective-permute-done.4.partner_ref
  69.8 1.0 %turn_part.3.rest_1_ = f32[8,8,8,128]{3,2,1,0:T(8,128)S(1)} custom-call(f32[2]{0:T(128)S(1)} %get-tuple-element.20.cos_ref, f32[2]{0:T(128)S(1)} %get-tuple-element.19.sin_ref, s32[1]{0:T(128)} %bitcast.3.lo_ref, f32[8,8,8,128]{3,2,1,0:T(8,128)S(1)} %get-tuple-element.16.own_ref, f32[8,8,8,128]{3,2,1,0:T(8,128)} %collective-permute-done.4.partner_ref), custom_call_target="tpu_custom_call" | custom-call | tf_op jit(solution)/shard_map/turn_part/pallas_call | solution.py:166
  70.8 4.7 %collective-permute-start.9 = (f32[8,8,8,128]{3,2,1,0:T(8,128)S(1)}, f32[8,8,8,128]{3,2,1,0:T(8,128)S(1)}, u32[]{:S(2)}, u32[]{:S(2)}) collective-permute-start(f32[8,8,8,128]{3,2,1,0:T(8,128)S(1)} %turn_part.3.rest_1_), channel_id=1, source_target_pairs={{0,32},{32,0},{64,96},{96,64},{128,160},{160,128},{192,224},{224,1... | collective-permute-start | bytes 786440 | tf_op jit(solution)/shard_map/ppermute | solution.py:311
  75.5 0.0 collective-permute-done.3.rest_0_.first
  75.5 4.9 %collective-permute-start.8 = (f32[8,8,8,128]{3,2,1,0:T(8,128)S(1)}, f32[8,8,8,128]{3,2,1,0:T(8,128)S(1)}, u32[]{:S(2)}, u32[]{:S(2)}) collective-permute-start(f32[8,8,8,128]{3,2,1,0:T(8,128)S(1)} %collective-permute-done.3.rest_0_.first), channel_id=1, source_target_pairs={{0,16},{1,17},{2,18},{3,19},{4,20},{5,21},{6,22},{7,23},{8,24},{9,... | collective-permute-start | bytes 786440 | tf_op jit(solution)/shard_map/ppermute | solution.py:307
  80.5 1.0 %row_matrix.1.left = bf16[128,384]{1,0:T(8,128)(2,1)S(1)} custom-call(f32[2]{0:T(128)S(1)} %get-tuple-element.20.cos_ref, f32[2]{0:T(128)S(1)} %get-tuple-element.19.sin_ref, s32[1]{0:T(128)} %bitcast.hi_ref, f32[3,128,128]{2,1,0:T(8,128)} %g_ref.3, f32[8,8,8,128]{3,2,1,0:T(8,128)S(1)} %collective-permute-done.3.rest_0_.first, ...), custom_call_target="tpu_custom_call" | custom-call | flops 99999997952 | bytes 100000 | tf_op jit(solution)/shard_map/row_matrix/pallas_call | solution.py:236
  81.4 6.0 %collective-permute-done.8.first_partner = f32[8,8,8,128]{3,2,1,0:T(8,128)S(1)} collective-permute-done((f32[8,8,8,128]{3,2,1,0:T(8,128)S(1)}, f32[8,8,8,128]{3,2,1,0:T(8,128)S(1)}, u32[]{:S(2)}, u32[]{:S(2)}) %collective-permute-start.8) | collective-permute-done | bytes 262176 | tf_op jit(solution)/shard_map/ppermute | solution.py:307
  87.4 0.7 collective-permute-done.9.second
  88.1 0.0 collective-permute-done.7.keep_partner
  88.1 2.3 %row_gate.2.rest_0_ = f32[128,4,8,128]{3,2,1,0:T(8,128)} custom-call(f32[2]{0:T(128)S(1)} %get-tuple-element.20.cos_ref, f32[2]{0:T(128)S(1)} %get-tuple-element.19.sin_ref, s32[1]{0:T(128)} %bitcast.3.lo_ref, bf16[128,384]{1,0:T(8,128)(2,1)S(1)} %row_matrix.1.left, f32[8,16,8,128]{3,2,1,0:T(8,128)S(1)} %get-tuple-element.18.keep, ...), custom_call_target="tpu_custom_call" | custom-call | tf_op jit(solution)/shard_map/row_gate/pallas_call | solution.py:292
  90.3 3.5 %all-to-all-done.1.own = f32[8,2,16,8,128]{4,3,2,1,0:T(8,128)S(1)} async-done(((f32[8,2,16,8,128]{4,3,2,1,0:T(8,128)}), f32[8,2,16,8,128]{4,3,2,1,0:T(8,128)S(1)}, u32[]{:S(2)}, u32[]{:S(2)}) %all-to-all-start.1) | async-done | bytes 1048608 | tf_op jit(solution)/shard_map/all_to_all | solution.py:317
  93.8 1.6 %row_gate.3 = f32[128,4,8,128]{3,2,1,0:T(8,128)} custom-call(bf16[128,384]{1,0:T(8,128)(2,1)S(1)} %row_matrix.1.left, f32[8,2,16,8,128]{4,3,2,1,0:T(8,128)S(1)} %all-to-all-done.1.own, f32[128,4,8,128]{3,2,1,0:T(8,128)} %row_gate.2.rest_0_), custom_call_target="tpu_custom_call", output_to_operand_aliasing={{}: (2, {})} | custom-call | tf_op jit(solution)/shard_map/row_gate/pallas_call | solution.py:292
  (1 shorter events, 0.0 us)
Async XLA Ops:
  0.0 39.3 %copy-start = (f32[2]{0:T(128)S(1)}, f32[2]{0:T(128)}, u32[]{:S(2)}) copy-start(f32[2]{0:T(128)} %param.6) | copy-start | bytes 28
  4.8 42.8 %all-to-all-start = ((f32[8,2,16,8,128]{4,3,2,1,0:T(8,128)}), f32[8,2,16,8,128]{4,3,2,1,0:T(8,128)}, u32[]{:S(2)}, u32[]{:S(2)}) async-start(f32[8,2,16,8,128]{4,3,2,1,0:T(8,128)} %get-tuple-element.12), calls=%async_computation | async-start | bytes 2097152 | tf_op jit(solution)/shard_map/all_to_all | solution.py:317
  15.1 19.2 %collective-permute-start = (f32[8,8,8,128]{3,2,1,0:T(8,128)S(1)}, f32[8,8,8,128]{3,2,1,0:T(8,128)S(1)}, u32[]{:S(2)}, u32[]{:S(2)}) collective-permute-start(f32[8,8,8,128]{3,2,1,0:T(8,128)S(1)} %get-tuple-element.13), channel_id=1, source_target_pairs={{0,32},{32,0},{64,96},{96,64},{128,160},{160,128},{192,224},{224,1... | collective-permute-start | bytes 786440 | tf_op jit(solution)/shard_map/ppermute | solution.py:311
  19.8 19.5 %collective-permute-start.2 = (f32[8,8,8,128]{3,2,1,0:T(8,128)S(1)}, f32[8,8,8,128]{3,2,1,0:T(8,128)S(1)}, u32[]{:S(2)}, u32[]{:S(2)}) collective-permute-start(f32[8,8,8,128]{3,2,1,0:T(8,128)S(1)} %get-tuple-element.14.own_ref), channel_id=1, source_target_pairs={{0,16},{1,17},{2,18},{3,19},{4,20},{5,21},{6,22},{7,23},{8,24},{9,... | collective-permute-start | bytes 786440 | tf_op jit(solution)/shard_map/ppermute | solution.py:307
  24.7 34.0 %collective-permute-start.5 = (f32[8,16,8,128]{3,2,1,0:T(8,128)S(1)}, f32[8,16,8,128]{3,2,1,0:T(8,128)S(1)}, u32[]{:S(2)}, u32[]{:S(2)}) collective-permute-start(f32[8,16,8,128]{3,2,1,0:T(8,128)S(1)} %get-tuple-element.17.keep), channel_id=1, source_target_pairs={{0,16},{1,17},{2,18},{3,19},{4,20},{5,21},{6,22},{7,23},{8,24},{9,... | collective-permute-start | bytes 1572872 | tf_op jit(solution)/shard_map/ppermute | solution.py:307
  34.3 13.2 %collective-permute-start.1 = (f32[8,8,8,128]{3,2,1,0:T(8,128)S(1)}, f32[8,8,8,128]{3,2,1,0:T(8,128)S(1)}, u32[]{:S(2)}, u32[]{:S(2)}) collective-permute-start(f32[8,8,8,128]{3,2,1,0:T(8,128)S(1)} %collective-permute-done.first), channel_id=1, source_target_pairs={{0,16},{1,17},{2,18},{3,19},{4,20},{5,21},{6,22},{7,23},{8,24},{9,... | collective-permute-start | bytes 786440 | tf_op jit(solution)/shard_map/ppermute | solution.py:307
  39.9 18.9 %collective-permute-start.6 = (f32[8,8,8,128]{3,2,1,0:T(8,128)S(1)}, f32[8,8,8,128]{3,2,1,0:T(8,128)S(1)}, u32[]{:S(2)}, u32[]{:S(2)}) collective-permute-start(f32[8,8,8,128]{3,2,1,0:T(8,128)S(1)} %turn_part.2.rest_1_), channel_id=1, source_target_pairs={{0,32},{32,0},{64,96},{96,64},{128,160},{160,128},{192,224},{224,1... | collective-permute-start | bytes 786440 | tf_op jit(solution)/shard_map/ppermute | solution.py:311
  48.8 21.0 %collective-permute-start.4 = (f32[8,8,8,128]{3,2,1,0:T(8,128)S(1)}, f32[8,8,8,128]{3,2,1,0:T(8,128)}, u32[]{:S(2)}, u32[]{:S(2)}) collective-permute-start(f32[8,8,8,128]{3,2,1,0:T(8,128)S(1)} %get-tuple-element.16.own_ref), channel_id=1, source_target_pairs={{0,16},{1,17},{2,18},{3,19},{4,20},{5,21},{6,22},{7,23},{8,24},{9,... | collective-permute-start | bytes 786440 | tf_op jit(solution)/shard_map/ppermute | solution.py:307
  53.7 21.8 %collective-permute-start.3 = (f32[8,8,8,128]{3,2,1,0:T(8,128)S(1)}, f32[8,8,8,128]{3,2,1,0:T(8,128)S(1)}, u32[]{:S(2)}, u32[]{:S(2)}) collective-permute-start(f32[8,8,8,128]{3,2,1,0:T(8,128)S(1)} %get-tuple-element.15.rest_0_), channel_id=1, source_target_pairs={{0,32},{32,0},{64,96},{96,64},{128,160},{160,128},{192,224},{224,1... | collective-permute-start | bytes 786440 | tf_op jit(solution)/shard_map/ppermute | solution.py:311
  60.4 33.4 %all-to-all-start.1 = ((f32[8,2,16,8,128]{4,3,2,1,0:T(8,128)}), f32[8,2,16,8,128]{4,3,2,1,0:T(8,128)S(1)}, u32[]{:S(2)}, u32[]{:S(2)}) async-start(f32[8,2,16,8,128]{4,3,2,1,0:T(8,128)} %merge.1), calls=%async_computation.1 | async-start | bytes 2097152 | tf_op jit(solution)/shard_map/all_to_all | solution.py:317
  67.4 20.7 %collective-permute-start.7 = (f32[8,16,8,128]{3,2,1,0:T(8,128)S(1)}, f32[8,16,8,128]{3,2,1,0:T(8,128)S(1)}, u32[]{:S(2)}, u32[]{:S(2)}) collective-permute-start(f32[8,16,8,128]{3,2,1,0:T(8,128)S(1)} %get-tuple-element.18.keep), channel_id=1, source_target_pairs={{0,16},{1,17},{2,18},{3,19},{4,20},{5,21},{6,22},{7,23},{8,24},{9,... | collective-permute-start | bytes 1572872 | tf_op jit(solution)/shard_map/ppermute | solution.py:307
  70.8 17.3 %collective-permute-start.9 = (f32[8,8,8,128]{3,2,1,0:T(8,128)S(1)}, f32[8,8,8,128]{3,2,1,0:T(8,128)S(1)}, u32[]{:S(2)}, u32[]{:S(2)}) collective-permute-start(f32[8,8,8,128]{3,2,1,0:T(8,128)S(1)} %turn_part.3.rest_1_), channel_id=1, source_target_pairs={{0,32},{32,0},{64,96},{96,64},{128,160},{160,128},{192,224},{224,1... | collective-permute-start | bytes 786440 | tf_op jit(solution)/shard_map/ppermute | solution.py:311
  75.5 11.9 %collective-permute-start.8 = (f32[8,8,8,128]{3,2,1,0:T(8,128)S(1)}, f32[8,8,8,128]{3,2,1,0:T(8,128)S(1)}, u32[]{:S(2)}, u32[]{:S(2)}) collective-permute-start(f32[8,8,8,128]{3,2,1,0:T(8,128)S(1)} %collective-permute-done.3.rest_0_.first), channel_id=1, source_target_pairs={{0,16},{1,17},{2,18},{3,19},{4,20},{5,21},{6,22},{7,23},{8,24},{9,... | collective-permute-start | bytes 786440 | tf_op jit(solution)/shard_map/ppermute | solution.py:307

commit v7 on v5

--- a/solution.py
+++ b/solution.py
@@ -8,7 +8,7 @@
 QL = 14
 QU = 5
 QUBITS = QL + QU
-STEP = 4
+STEP = 8
 SMEM = pl.BlockSpec(memory_space=pltpu.SMEM)
 VMEM = pl.BlockSpec(memory_space=pltpu.VMEM)
 ANY = pl.BlockSpec(memory_space=pl.ANY)

time: 95.9 us -> 96.2 us (level)
  no operation moved by 1% of the time
where the time goes in v7:
time: 96.2 us; the launch traced here: 95.6 us
  starting transfers between devices  60.2 us (63%)
  waiting for transfers between devices  20.7 us (22%)
  Pallas kernels  14.5 us (15%)
    ppermute x6, starting transfers between devices, swap_lo(): lax.ppermute(value, 'lo', [(i, i ^ count // 2) for i in range(count)])  24.6 us
    ppermute x4, starting transfers between devices, swap_hi(): lax.ppermute(value, 'hi', [(i, i ^ 1) for i in range(lax.axis_size('hi'))])  18.3 us
    all_to_all x2, starting transfers between devices, remap(): lax.all_to_all(value, 'hi', split_axis=0, concat_axis=0, tiled=True, axis...  17.3 us
    ppermute x6, waiting for transfers between devices, swap_lo(): lax.ppermute(value, 'lo', [(i, i ^ count // 2) for i in range(count)])  9.47 us
    ppermute x4, waiting for transfers between devices, swap_hi(): lax.ppermute(value, 'hi', [(i, i ^ 1) for i in range(lax.axis_size('hi'))])  7.34 us
    pallas_call x1, Pallas kernels, local_gates(): pl.pallas_call(local_kernel, out_shape=[pltpu.VMEM(ONE, jnp.float32), plt...  4.99 us
    all_to_all x2, waiting for transfers between devices, remap(): lax.all_to_all(value, 'hi', split_axis=0, concat_axis=0, tiled=True, axis...  3.93 us
    pallas_call x2, Pallas kernels, row_gate(): pl.pallas_call(body, out_shape=jax.ShapeDtypeStruct((128, 4, 8, 128), jnp...  3.82 us
  transfers between devices with their start and end apart: 12, of which 5 were waited for; matrix products, arithmetic and copies ran while one was open for 0% of the time, Pallas kernels for 8%

profile of v7, /device:TPU:56, one launch (start us, length us, event | category | flops | bytes accessed | tf_op | source)
XLA Modules:
  0.0 95.6 jit_solution(3483622182723761950)
XLA Ops:
  0.0 0.0 copy-start
  0.0 5.0 %local_gates.1 = (f32[8,16,8,128]{3,2,1,0:T(8,128)S(1)}, f32[8,8,8,128]{3,2,1,0:T(8,128)S(1)}, f32[8,8,8,128]{3,2,1,0:T(8,128)S(1)}, f32[8,2,16,8,128]{4,3,2,1,0:T(8,128)}) custom-call(s32[2,24]{1,0:T(2,128)} %bitcast.6, s32[1]{0:T(128)} %bitcast.hi_ref, f32[8,2,2,128,128]{4,3,2,1,0:T(8,128)} %bitcast.5, f32[3,128,128]{2,1,0:T(8,128)} %g_ref.3), custom_call_target="tpu_custom_call" | custom-call | tf_op jit(solution)/shard_map/local_gates/pallas_call | solution.py:126
  5.0 10.3 %all-to-all-start = ((f32[8,2,16,8,128]{4,3,2,1,0:T(8,128)}), f32[8,2,16,8,128]{4,3,2,1,0:T(8,128)}, u32[]{:S(2)}, u32[]{:S(2)}) async-start(f32[8,2,16,8,128]{4,3,2,1,0:T(8,128)} %get-tuple-element.12), calls=%async_computation | async-start | bytes 2097152 | tf_op jit(solution)/shard_map/all_to_all | solution.py:317
  15.3 4.7 %collective-permute-start = (f32[8,8,8,128]{3,2,1,0:T(8,128)S(1)}, f32[8,8,8,128]{3,2,1,0:T(8,128)S(1)}, u32[]{:S(2)}, u32[]{:S(2)}) collective-permute-start(f32[8,8,8,128]{3,2,1,0:T(8,128)S(1)} %get-tuple-element.13), channel_id=1, source_target_pairs={{0,32},{32,0},{64,96},{96,64},{128,160},{160,128},{192,224},{224,1... | collective-permute-start | bytes 786440 | tf_op jit(solution)/shard_map/ppermute | solution.py:311
  20.0 4.9 %collective-permute-start.5 = (f32[8,8,8,128]{3,2,1,0:T(8,128)S(1)}, f32[8,8,8,128]{3,2,1,0:T(8,128)S(1)}, u32[]{:S(2)}, u32[]{:S(2)}) collective-permute-start(f32[8,8,8,128]{3,2,1,0:T(8,128)S(1)} %get-tuple-element.17.own_ref), channel_id=1, source_target_pairs={{0,16},{1,17},{2,18},{3,19},{4,20},{5,21},{6,22},{7,23},{8,24},{9,... | collective-permute-start | bytes 786440 | tf_op jit(solution)/shard_map/ppermute | solution.py:307
  25.0 2.4 %collective-permute-start.4 = (f32[8,16,8,128]{3,2,1,0:T(8,128)S(1)}, f32[8,16,8,128]{3,2,1,0:T(8,128)S(1)}, u32[]{:S(2)}, u32[]{:S(2)}) collective-permute-start(f32[8,16,8,128]{3,2,1,0:T(8,128)S(1)} %get-tuple-element.16.keep), channel_id=1, source_target_pairs={{0,16},{1,17},{2,18},{3,19},{4,20},{5,21},{6,22},{7,23},{8,24},{9,... | collective-permute-start | bytes 1572872 | tf_op jit(solution)/shard_map/ppermute | solution.py:307
  27.4 7.1 %collective-permute-done.first = f32[8,8,8,128]{3,2,1,0:T(8,128)S(1)} collective-permute-done((f32[8,8,8,128]{3,2,1,0:T(8,128)S(1)}, f32[8,8,8,128]{3,2,1,0:T(8,128)S(1)}, u32[]{:S(2)}, u32[]{:S(2)}) %collective-permute-start) | collective-permute-done | bytes 262176 | tf_op jit(solution)/shard_map/ppermute | solution.py:311
  34.5 4.9 %collective-permute-start.1 = (f32[8,8,8,128]{3,2,1,0:T(8,128)S(1)}, f32[8,8,8,128]{3,2,1,0:T(8,128)S(1)}, u32[]{:S(2)}, u32[]{:S(2)}) collective-permute-start(f32[8,8,8,128]{3,2,1,0:T(8,128)S(1)} %collective-permute-done.first), channel_id=1, source_target_pairs={{0,16},{1,17},{2,18},{3,19},{4,20},{5,21},{6,22},{7,23},{8,24},{9,... | collective-permute-start | bytes 786440 | tf_op jit(solution)/shard_map/ppermute | solution.py:307
  39.5 0.0 copy-done
  39.5 0.0 collective-permute-done.5.partner_ref
  39.6 1.3 %turn_part.3 = f32[8,8,8,128]{3,2,1,0:T(8,128)} custom-call(f32[2]{0:T(128)S(1)} %get-tuple-element.20.cos_ref, f32[2]{0:T(128)S(1)} %get-tuple-element.19.sin_ref, s32[1]{0:T(128)} %bitcast.3.lo_ref, f32[8,8,8,128]{3,2,1,0:T(8,128)S(1)} %get-tuple-element.17.own_ref, f32[8,8,8,128]{3,2,1,0:T(8,128)S(1)} %collective-permute-done.5.partner_ref), custom_call_target="tpu_custom_call" | custom-call | tf_op jit(solution)/shard_map/turn_part/pallas_call | solution.py:166
  40.8 3.9 %collective-permute-start.6 = (f32[8,8,8,128]{3,2,1,0:T(8,128)}, f32[8,8,8,128]{3,2,1,0:T(8,128)S(1)}, u32[]{:S(2)}, u32[]{:S(2)}) collective-permute-start(f32[8,8,8,128]{3,2,1,0:T(8,128)} %turn_part.3), channel_id=1, source_target_pairs={{0,32},{32,0},{64,96},{96,64},{128,160},{160,128},{192,224},{224,1... | collective-permute-start | bytes 786440 | tf_op jit(solution)/shard_map/ppermute | solution.py:311
  44.7 3.0 %collective-permute-done.1.rest_0_.first_partner = f32[8,8,8,128]{3,2,1,0:T(8,128)S(1)} collective-permute-done((f32[8,8,8,128]{3,2,1,0:T(8,128)S(1)}, f32[8,8,8,128]{3,2,1,0:T(8,128)S(1)}, u32[]{:S(2)}, u32[]{:S(2)}) %collective-permute-start.1) | collective-permute-done | bytes 262176 | tf_op jit(solution)/shard_map/ppermute | solution.py:307
  47.8 0.0 all-to-all-done.in_ref
  47.8 1.2 %cut.1 = (f32[8,16,8,128]{3,2,1,0:T(8,128)S(1)}, f32[8,8,8,128]{3,2,1,0:T(8,128)S(1)}, f32[8,8,8,128]{3,2,1,0:T(8,128)S(1)}) custom-call(f32[8,2,16,8,128]{4,3,2,1,0:T(8,128)} %all-to-all-done.in_ref, f32[8,8,8,128]{3,2,1,0:T(8,128)S(1)} %collective-permute-done.1.rest_0_.first_partner), custom_call_target="tpu_custom_call" | custom-call | tf_op jit(solution)/shard_map/cut/pallas_call | solution.py:209
  49.0 4.9 %collective-permute-start.3 = (f32[8,8,8,128]{3,2,1,0:T(8,128)S(1)}, f32[8,8,8,128]{3,2,1,0:T(8,128)S(1)}, u32[]{:S(2)}, u32[]{:S(2)}) collective-permute-start(f32[8,8,8,128]{3,2,1,0:T(8,128)S(1)} %get-tuple-element.15.own_ref), channel_id=1, source_target_pairs={{0,16},{1,17},{2,18},{3,19},{4,20},{5,21},{6,22},{7,23},{8,24},{9,... | collective-permute-start | bytes 786440 | tf_op jit(solution)/shard_map/ppermute | solution.py:307
  54.0 5.0 %collective-permute-start.2 = (f32[8,8,8,128]{3,2,1,0:T(8,128)S(1)}, f32[8,8,8,128]{3,2,1,0:T(8,128)S(1)}, u32[]{:S(2)}, u32[]{:S(2)}) collective-permute-start(f32[8,8,8,128]{3,2,1,0:T(8,128)S(1)} %get-tuple-element.14.rest_0_), channel_id=1, source_target_pairs={{0,32},{32,0},{64,96},{96,64},{128,160},{160,128},{192,224},{224,1... | collective-permute-start | bytes 786440 | tf_op jit(solution)/shard_map/ppermute | solution.py:311
  59.0 0.0 collective-permute-done.4.keep_partner
  59.0 0.0 collective-permute-done.6.second
  59.0 1.6 %merge.1 = f32[8,2,16,8,128]{4,3,2,1,0:T(8,128)} custom-call(f32[2]{0:T(128)S(1)} %get-tuple-element.20.cos_ref, f32[2]{0:T(128)S(1)} %get-tuple-element.19.sin_ref, s32[1]{0:T(128)} %bitcast.3.lo_ref, f32[8,16,8,128]{3,2,1,0:T(8,128)S(1)} %get-tuple-element.16.keep, f32[8,16,8,128]{3,2,1,0:T(8,128)S(1)} %collective-permute-done.4.keep_partner, ...), custom_call_target="tpu_custom_call" | custom-call | tf_op jit(solution)/shard_map/merge/pallas_call | solution.py:185
  60.7 6.9 %all-to-all-start.1 = ((f32[8,2,16,8,128]{4,3,2,1,0:T(8,128)}), f32[8,2,16,8,128]{4,3,2,1,0:T(8,128)S(1)}, u32[]{:S(2)}, u32[]{:S(2)}) async-start(f32[8,2,16,8,128]{4,3,2,1,0:T(8,128)} %merge.1), calls=%async_computation.1 | async-start | bytes 2097152 | tf_op jit(solution)/shard_map/all_to_all | solution.py:317
  67.6 2.4 %collective-permute-start.7 = (f32[8,16,8,128]{3,2,1,0:T(8,128)S(1)}, f32[8,16,8,128]{3,2,1,0:T(8,128)S(1)}, u32[]{:S(2)}, u32[]{:S(2)}) collective-permute-start(f32[8,16,8,128]{3,2,1,0:T(8,128)S(1)} %get-tuple-element.18.keep), channel_id=1, source_target_pairs={{0,16},{1,17},{2,18},{3,19},{4,20},{5,21},{6,22},{7,23},{8,24},{9,... | collective-permute-start | bytes 1572872 | tf_op jit(solution)/shard_map/ppermute | solution.py:307
  70.0 0.0 collective-permute-done.3.partner_ref
  70.0 0.6 turn_part.2.rest_1_
  70.6 4.7 %collective-permute-start.9 = (f32[8,8,8,128]{3,2,1,0:T(8,128)S(1)}, f32[8,8,8,128]{3,2,1,0:T(8,128)S(1)}, u32[]{:S(2)}, u32[]{:S(2)}) collective-permute-start(f32[8,8,8,128]{3,2,1,0:T(8,128)S(1)} %turn_part.2.rest_1_), channel_id=1, source_target_pairs={{0,32},{32,0},{64,96},{96,64},{128,160},{160,128},{192,224},{224,1... | collective-permute-start | bytes 786440 | tf_op jit(solution)/shard_map/ppermute | solution.py:311
  75.3 0.0 collective-permute-done.2.rest_0_.first
  75.3 4.9 %collective-permute-start.8 = (f32[8,8,8,128]{3,2,1,0:T(8,128)S(1)}, f32[8,8,8,128]{3,2,1,0:T(8,128)S(1)}, u32[]{:S(2)}, u32[]{:S(2)}) collective-permute-start(f32[8,8,8,128]{3,2,1,0:T(8,128)S(1)} %collective-permute-done.2.rest_0_.first), channel_id=1, source_target_pairs={{0,16},{1,17},{2,18},{3,19},{4,20},{5,21},{6,22},{7,23},{8,24},{9,... | collective-permute-start | bytes 786440 | tf_op jit(solution)/shard_map/ppermute | solution.py:307
  80.3 1.0 %row_matrix.1.left = bf16[128,384]{1,0:T(8,128)(2,1)S(1)} custom-call(f32[2]{0:T(128)S(1)} %get-tuple-element.20.cos_ref, f32[2]{0:T(128)S(1)} %get-tuple-element.19.sin_ref, s32[1]{0:T(128)} %bitcast.hi_ref, f32[3,128,128]{2,1,0:T(8,128)} %g_ref.3, f32[8,8,8,128]{3,2,1,0:T(8,128)S(1)} %collective-permute-done.2.rest_0_.first, ...), custom_call_target="tpu_custom_call" | custom-call | flops 99999997952 | bytes 100000 | tf_op jit(solution)/shard_map/row_matrix/pallas_call | solution.py:236
  81.2 6.4 %collective-permute-done.8.first_partner = f32[8,8,8,128]{3,2,1,0:T(8,128)S(1)} collective-permute-done((f32[8,8,8,128]{3,2,1,0:T(8,128)S(1)}, f32[8,8,8,128]{3,2,1,0:T(8,128)S(1)}, u32[]{:S(2)}, u32[]{:S(2)}) %collective-permute-start.8) | collective-permute-done | bytes 262176 | tf_op jit(solution)/shard_map/ppermute | solution.py:307
  87.7 0.2 collective-permute-done.9.second
  87.9 0.0 collective-permute-done.7.keep_partner
  87.9 2.3 %row_gate.2.rest_0_ = f32[128,4,8,128]{3,2,1,0:T(8,128)} custom-call(f32[2]{0:T(128)S(1)} %get-tuple-element.20.cos_ref, f32[2]{0:T(128)S(1)} %get-tuple-element.19.sin_ref, s32[1]{0:T(128)} %bitcast.3.lo_ref, bf16[128,384]{1,0:T(8,128)(2,1)S(1)} %row_matrix.1.left, f32[8,16,8,128]{3,2,1,0:T(8,128)S(1)} %get-tuple-element.18.keep, ...), custom_call_target="tpu_custom_call" | custom-call | tf_op jit(solution)/shard_map/row_gate/pallas_call | solution.py:292
  90.1 3.9 %all-to-all-done.1.own = f32[8,2,16,8,128]{4,3,2,1,0:T(8,128)S(1)} async-done(((f32[8,2,16,8,128]{4,3,2,1,0:T(8,128)}), f32[8,2,16,8,128]{4,3,2,1,0:T(8,128)S(1)}, u32[]{:S(2)}, u32[]{:S(2)}) %all-to-all-start.1) | async-done | bytes 1048608 | tf_op jit(solution)/shard_map/all_to_all | solution.py:317
  94.0 1.6 %row_gate.3 = f32[128,4,8,128]{3,2,1,0:T(8,128)} custom-call(bf16[128,384]{1,0:T(8,128)(2,1)S(1)} %row_matrix.1.left, f32[8,2,16,8,128]{4,3,2,1,0:T(8,128)S(1)} %all-to-all-done.1.own, f32[128,4,8,128]{3,2,1,0:T(8,128)} %row_gate.2.rest_0_), custom_call_target="tpu_custom_call", output_to_operand_aliasing={{}: (2, {})} | custom-call | tf_op jit(solution)/shard_map/row_gate/pallas_call | solution.py:292
  (1 shorter events, 0.0 us)
Async XLA Ops:
  0.0 39.5 %copy-start = (f32[2]{0:T(128)S(1)}, f32[2]{0:T(128)}, u32[]{:S(2)}) copy-start(f32[2]{0:T(128)} %param.6) | copy-start | bytes 28
  5.0 42.8 %all-to-all-start = ((f32[8,2,16,8,128]{4,3,2,1,0:T(8,128)}), f32[8,2,16,8,128]{4,3,2,1,0:T(8,128)}, u32[]{:S(2)}, u32[]{:S(2)}) async-start(f32[8,2,16,8,128]{4,3,2,1,0:T(8,128)} %get-tuple-element.12), calls=%async_computation | async-start | bytes 2097152 | tf_op jit(solution)/shard_map/all_to_all | solution.py:317
  15.3 19.2 %collective-permute-start = (f32[8,8,8,128]{3,2,1,0:T(8,128)S(1)}, f32[8,8,8,128]{3,2,1,0:T(8,128)S(1)}, u32[]{:S(2)}, u32[]{:S(2)}) collective-permute-start(f32[8,8,8,128]{3,2,1,0:T(8,128)S(1)} %get-tuple-element.13), channel_id=1, source_target_pairs={{0,32},{32,0},{64,96},{96,64},{128,160},{160,128},{192,224},{224,1... | collective-permute-start | bytes 786440 | tf_op jit(solution)/shard_map/ppermute | solution.py:311
  20.0 19.5 %collective-permute-start.5 = (f32[8,8,8,128]{3,2,1,0:T(8,128)S(1)}, f32[8,8,8,128]{3,2,1,0:T(8,128)S(1)}, u32[]{:S(2)}, u32[]{:S(2)}) collective-permute-start(f32[8,8,8,128]{3,2,1,0:T(8,128)S(1)} %get-tuple-element.17.own_ref), channel_id=1, source_target_pairs={{0,16},{1,17},{2,18},{3,19},{4,20},{5,21},{6,22},{7,23},{8,24},{9,... | collective-permute-start | bytes 786440 | tf_op jit(solution)/shard_map/ppermute | solution.py:307
  25.0 34.0 %collective-permute-start.4 = (f32[8,16,8,128]{3,2,1,0:T(8,128)S(1)}, f32[8,16,8,128]{3,2,1,0:T(8,128)S(1)}, u32[]{:S(2)}, u32[]{:S(2)}) collective-permute-start(f32[8,16,8,128]{3,2,1,0:T(8,128)S(1)} %get-tuple-element.16.keep), channel_id=1, source_target_pairs={{0,16},{1,17},{2,18},{3,19},{4,20},{5,21},{6,22},{7,23},{8,24},{9,... | collective-permute-start | bytes 1572872 | tf_op jit(solution)/shard_map/ppermute | solution.py:307
  34.5 13.2 %collective-permute-start.1 = (f32[8,8,8,128]{3,2,1,0:T(8,128)S(1)}, f32[8,8,8,128]{3,2,1,0:T(8,128)S(1)}, u32[]{:S(2)}, u32[]{:S(2)}) collective-permute-start(f32[8,8,8,128]{3,2,1,0:T(8,128)S(1)} %collective-permute-done.first), channel_id=1, source_target_pairs={{0,16},{1,17},{2,18},{3,19},{4,20},{5,21},{6,22},{7,23},{8,24},{9,... | collective-permute-start | bytes 786440 | tf_op jit(solution)/shard_map/ppermute | solution.py:307
  40.8 18.2 %collective-permute-start.6 = (f32[8,8,8,128]{3,2,1,0:T(8,128)}, f32[8,8,8,128]{3,2,1,0:T(8,128)S(1)}, u32[]{:S(2)}, u32[]{:S(2)}) collective-permute-start(f32[8,8,8,128]{3,2,1,0:T(8,128)} %turn_part.3), channel_id=1, source_target_pairs={{0,32},{32,0},{64,96},{96,64},{128,160},{160,128},{192,224},{224,1... | collective-permute-start | bytes 786440 | tf_op jit(solution)/shard_map/ppermute | solution.py:311
  49.0 21.0 %collective-permute-start.3 = (f32[8,8,8,128]{3,2,1,0:T(8,128)S(1)}, f32[8,8,8,128]{3,2,1,0:T(8,128)S(1)}, u32[]{:S(2)}, u32[]{:S(2)}) collective-permute-start(f32[8,8,8,128]{3,2,1,0:T(8,128)S(1)} %get-tuple-element.15.own_ref), channel_id=1, source_target_pairs={{0,16},{1,17},{2,18},{3,19},{4,20},{5,21},{6,22},{7,23},{8,24},{9,... | collective-permute-start | bytes 786440 | tf_op jit(solution)/shard_map/ppermute | solution.py:307
  54.0 21.3 %collective-permute-start.2 = (f32[8,8,8,128]{3,2,1,0:T(8,128)S(1)}, f32[8,8,8,128]{3,2,1,0:T(8,128)S(1)}, u32[]{:S(2)}, u32[]{:S(2)}) collective-permute-start(f32[8,8,8,128]{3,2,1,0:T(8,128)S(1)} %get-tuple-element.14.rest_0_), channel_id=1, source_target_pairs={{0,32},{32,0},{64,96},{96,64},{128,160},{160,128},{192,224},{224,1... | collective-permute-start | bytes 786440 | tf_op jit(solution)/shard_map/ppermute | solution.py:311
  60.7 33.4 %all-to-all-start.1 = ((f32[8,2,16,8,128]{4,3,2,1,0:T(8,128)}), f32[8,2,16,8,128]{4,3,2,1,0:T(8,128)S(1)}, u32[]{:S(2)}, u32[]{:S(2)}) async-start(f32[8,2,16,8,128]{4,3,2,1,0:T(8,128)} %merge.1), calls=%async_computation.1 | async-start | bytes 2097152 | tf_op jit(solution)/shard_map/all_to_all | solution.py:317
  67.6 20.3 %collective-permute-start.7 = (f32[8,16,8,128]{3,2,1,0:T(8,128)S(1)}, f32[8,16,8,128]{3,2,1,0:T(8,128)S(1)}, u32[]{:S(2)}, u32[]{:S(2)}) collective-permute-start(f32[8,16,8,128]{3,2,1,0:T(8,128)S(1)} %get-tuple-element.18.keep), channel_id=1, source_target_pairs={{0,16},{1,17},{2,18},{3,19},{4,20},{5,21},{6,22},{7,23},{8,24},{9,... | collective-permute-start | bytes 1572872 | tf_op jit(solution)/shard_map/ppermute | solution.py:307
  70.6 17.3 %collective-permute-start.9 = (f32[8,8,8,128]{3,2,1,0:T(8,128)S(1)}, f32[8,8,8,128]{3,2,1,0:T(8,128)S(1)}, u32[]{:S(2)}, u32[]{:S(2)}) collective-permute-start(f32[8,8,8,128]{3,2,1,0:T(8,128)S(1)} %turn_part.2.rest_1_), channel_id=1, source_target_pairs={{0,32},{32,0},{64,96},{96,64},{128,160},{160,128},{192,224},{224,1... | collective-permute-start | bytes 786440 | tf_op jit(solution)/shard_map/ppermute | solution.py:311
  75.3 12.3 %collective-permute-start.8 = (f32[8,8,8,128]{3,2,1,0:T(8,128)S(1)}, f32[8,8,8,128]{3,2,1,0:T(8,128)S(1)}, u32[]{:S(2)}, u32[]{:S(2)}) collective-permute-start(f32[8,8,8,128]{3,2,1,0:T(8,128)S(1)} %collective-permute-done.2.rest_0_.first), channel_id=1, source_target_pairs={{0,16},{1,17},{2,18},{3,19},{4,20},{5,21},{6,22},{7,23},{8,24},{9,... | collective-permute-start | bytes 786440 | tf_op jit(solution)/shard_map/ppermute | solution.py:307
